TPU v7x, 32 devices: a whole 2x2x4 slice. The times are simulated.
32 devices in a mesh: dp: 2 (over x), row: 4 (over y, core), col: 4 (over z).
Axes of the slice: x: 2, y: 2, z: 4, core: 2. Of those that a mesh axis runs over, the one named last changes fastest.
Arguments:
- hidden_in: bfloat16 [2, 1536, 1536], P(None, ('dp', 'row'), 'col'), may hold values from -6 to 6
- norm_gain: float32 [1536], replicated, may hold values from 0.5 to 1.5
- w_query: bfloat16 [1536, 1536], P('col', 'row'), may hold values from -0.625 to 0.625
- w_key: bfloat16 [1536, 512], P('col', 'row'), may hold values from -0.625 to 0.625
- w_value: bfloat16 [1536, 512], P('col', 'row'), may hold values from -0.15625 to 0.15625
- w_out: bfloat16 [1536, 1536], P('row', 'col'), may hold values from -1.5 to 1.5
- mix_gain: float32 [1536], replicated, may hold values from 0.5 to 1.5
- w_router: bfloat16 [1536, 32], replicated, may hold values from -0.1875 to 0.1875
- w_gate: bfloat16 [32, 1536, 512], P('dp', ('row', 'col')), may hold values from -0.15625 to 0.15625
- w_up: bfloat16 [32, 1536, 512], P('dp', ('row', 'col')), may hold values from -0.15625 to 0.15625
- w_down: bfloat16 [32, 512, 1536], P('dp', ('row', 'col')), may hold values from -3 to 3
- lengths: int32 [2, 2, 3], P(None, 'dp'), may hold values from 1 to 512, 768 in all within a row
- routes: int32 [2, 1536, 8], P(None, ('dp', 'row', 'col')), may hold values from 0 to 31, all different within a row; in each aligned block of 48 rows (0 to 47, 48 to 95, ..., all dimensions but the last counted through in order) at most 18 rows name the same one
- mask: int32 [2, 1536], P(None, ('dp', 'row', 'col')), may hold values from 0 to 1, as said below
- cotangent: bfloat16 [2, 1536, 1536], P(None, ('dp', 'row', 'col')), may hold values from -6 to 6
Outputs:
- layer_out: bfloat16 [2, 1536, 1536], P(None, ('dp', 'row', 'col'))
- grad_input: float32 [2, 1536, 1536], P(None, ('dp', 'row'), 'col')
- grad_norm_gain: float32 [1536], replicated
- grad_query: float32 [1536, 1536], P('col', 'row')
- grad_key: float32 [1536, 512], P('col', 'row')
- grad_value: float32 [1536, 512], P('col', 'row')
- grad_out_proj: float32 [1536, 1536], P('row', 'col')
- grad_mix_gain: float32 [1536], replicated
- grad_router: float32 [1536, 32], replicated
- grad_gate: float32 [32, 1536, 512], P('dp', ('row', 'col'))
- grad_up: float32 [32, 1536, 512], P('dp', ('row', 'col'))
- grad_down: float32 [32, 512, 1536], P('dp', ('row', 'col'))
Inputs may be any that keep to these rules, and one draw needn't show every extreme that they name: The 3 lengths of one micro-batch and dp index sum to 768, and the longest of them is exactly 512. `routes`: each token names 8 different experts. In every aligned block of 48 tokens (the tokens of one device) no expert is named more than 18 times, and the bound 18 is reached. `mask`: in each micro-batch the ones of the 768 tokens of one dp index form a prefix of half of them or more.
All inputs are finite; a program needn't handle non-finite values.
Results may differ from a plain program's by a relative error of at most 0.018.
Values may be sent and summed in bfloat16 or wider, within the bound.
A program may use at most 320 MiB of HBM per device.

v0:
```python
import jax
import jax.numpy as jnp
from jax import lax
from jax.sharding import PartitionSpec as P

D = 1536
HEAD_DIM = 64
TOP = 8


eps_norm = 1e-06
resid_scale = 0.22
attn_scale = 0.015625
rope_base = 10000.0
highest = lax.Precision.HIGHEST


def shortened(shard):
    return jax.tree.map(lambda a: a.astype(jnp.bfloat16) if a.dtype == jnp.float32 else a, shard)


def documents(doc_lengths, length_all):
    doc_ends = jnp.cumsum(doc_lengths, dtype=jnp.int32)
    doc_starts = doc_ends - doc_lengths
    positions = jnp.arange(length_all, dtype=jnp.int32)
    doc_id = jnp.sum(
        (positions[:, None] >= doc_ends[None, :]).astype(jnp.int32), axis=1, dtype=jnp.int32
    )
    member = doc_id[:, None] == jnp.arange(doc_lengths.shape[0], dtype=jnp.int32)[None, :]
    doc_start = jnp.sum(jnp.where(member, doc_starts[None, :], 0), axis=1, dtype=jnp.int32)
    return (doc_id, positions - doc_start)


def angles(position, head_width):
    half_width = head_width // 2
    frequency = rope_base ** (-2.0 * jnp.arange(half_width, dtype=jnp.float32) / head_width)
    turned = position[:, None] * frequency[None, :]
    return (jnp.sin(turned)[:, None, :], jnp.cos(turned)[:, None, :])


def rotate(values, sin_table, cos_table):
    half_width = values.shape[-1] // 2
    front_half = values[..., :half_width]
    back_half = values[..., half_width:]
    return jnp.concatenate(
        [
            front_half * cos_table - back_half * sin_table,
            back_half * cos_table + front_half * sin_table,
        ],
        axis=-1,
    )


def gather_rows(value):
    return lax.all_gather(value, "row", axis=0, tiled=True)


def gather_cols(value):
    return jax.tree.map(
        lambda part, own: part.astype(own.dtype),
        lax.all_gather(shortened(value), "col", axis=0, tiled=True),
        value,
    )


def sum_cols(pieces):
    return lax.psum_scatter(pieces, "col", scatter_dimension=0, tiled=True)


def sum_rows(pieces):
    return lax.psum_scatter(pieces, "row", scatter_dimension=0, tiled=True)


def width_total(value):
    return lax.psum(value, "col")


def expert_trade(value):
    return lax.all_to_all(value, "dp", split_axis=1, concat_axis=1, tiled=True)


def attn_total(value):
    return jax.tree.map(lambda part: part.astype(jnp.float32), lax.psum(shortened(value), "dp"))


def expert_total(value):
    return jax.tree.map(
        lambda part: part.astype(jnp.float32),
        lax.psum_scatter(shortened(value), ("row", "col"), scatter_dimension=1, tiled=True),
    )


def add_all(first_set, second_set):
    return tuple((left_one + right_one for left_one, right_one in zip(first_set, second_set)))


def project(left_side, right_side):
    return jnp.dot(left_side, right_side, preferred_element_type=jnp.float32)


def shards(
    hidden_in,
    norm_gain,
    w_query,
    w_key,
    w_value,
    w_out,
    mix_gain,
    w_router,
    w_gate,
    w_up,
    w_down,
    lengths,
    routes,
    mask,
    cotangent,
):
    micro_count = hidden_in.shape[0]
    tok_dev = hidden_in.shape[1]
    width_part = hidden_in.shape[2]
    col_count = lax.axis_size("col")
    row_count = lax.axis_size("row")
    dp_count = lax.axis_size("dp")
    col_at = lax.axis_index("col")
    model_width = D
    heads_here = w_query.shape[1] // HEAD_DIM
    kv_here = w_key.shape[1] // HEAD_DIM
    group_size = heads_here // kv_here
    group_tokens = tok_dev * row_count
    quarter = tok_dev // col_count
    experts_here = w_gate.shape[0]
    experts_all = experts_here * dp_count
    capacity = quarter * 3 // 8
    slot_count = experts_all * capacity
    gain_part = lax.dynamic_slice_in_dim(norm_gain, col_at * width_part, width_part)
    router_wide = w_router.astype(jnp.float32)
    full_gate, full_up, full_down = (
        lax.all_gather(w_gate, ("row", "col"), axis=1, tiled=True),
        lax.all_gather(w_up, ("row", "col"), axis=1, tiled=True),
        lax.all_gather(w_down, ("row", "col"), axis=1, tiled=True),
    )
    expert_ids = jnp.arange(experts_all, dtype=jnp.int32)
    group_index = jnp.arange(group_tokens, dtype=jnp.int32)
    query_start = col_at * tok_dev
    query_index = query_start + jnp.arange(tok_dev, dtype=jnp.int32)
    attn_local = (
        jnp.zeros(w_query.shape, jnp.float32),
        jnp.zeros(w_key.shape, jnp.float32),
        jnp.zeros(w_value.shape, jnp.float32),
        jnp.zeros(w_out.shape, jnp.float32),
    )
    expert_local = (
        jnp.zeros(full_gate.shape, jnp.float32),
        jnp.zeros(full_up.shape, jnp.float32),
        jnp.zeros(full_down.shape, jnp.float32),
    )
    router_acc = jnp.zeros(w_router.shape, jnp.float32)
    norm_acc = jnp.zeros((width_part,), jnp.float32)
    mix_acc = jnp.zeros((model_width,), jnp.float32)
    layer_rows = []
    input_grads = []
    for step in range(micro_count):
        x_full = hidden_in[step].astype(jnp.float32)
        squares = width_total(jnp.sum(x_full * x_full, axis=1))
        scale_one = lax.rsqrt(squares / model_width + eps_norm)[:, None]
        unit_one = x_full * scale_one
        normed = (unit_one * gain_part).astype(jnp.bfloat16)
        normed_all = gather_rows(normed)
        query_p, key_p, value_p = sum_cols(
            (project(normed_all, w_query), project(normed_all, w_key), project(normed_all, w_value))
        )
        doc_all, pos_all = documents(lengths[step, 0], group_tokens)
        doc_query = lax.dynamic_slice_in_dim(doc_all, query_start, tok_dev)
        pos_query = lax.dynamic_slice_in_dim(pos_all, query_start, tok_dev).astype(jnp.float32)
        sin_table, cos_table = angles(pos_query, HEAD_DIM)
        query_rot = rotate(
            query_p.reshape(tok_dev, heads_here, HEAD_DIM), sin_table, cos_table
        ).astype(jnp.bfloat16)
        key_rot = rotate(key_p.reshape(tok_dev, kv_here, HEAD_DIM), sin_table, cos_table).astype(
            jnp.bfloat16
        )
        value_low = value_p.astype(jnp.bfloat16).reshape(tok_dev, kv_here, HEAD_DIM)
        keys_all, values_all = (
            lax.all_gather(key_rot, "col", axis=0, tiled=True),
            lax.all_gather(value_low, "col", axis=0, tiled=True),
        )
        allowed = (doc_query[:, None] == doc_all[None, :]) & (
            group_index[None, :] <= query_index[:, None]
        )
        query_grp = query_rot.reshape(tok_dev, kv_here, group_size, HEAD_DIM)
        raw_scores = jnp.einsum(
            "qhgd,khd->hgqk", query_grp, keys_all, preferred_element_type=jnp.float32
        )
        scores = jnp.where(allowed[None, None], raw_scores * attn_scale, -1e30)
        top_score = jnp.max(scores, axis=-1, keepdims=True)
        expd = jnp.exp(scores - top_score)
        row_total = jnp.sum(expd, axis=-1, keepdims=True)
        attn_probs = expd / row_total
        log_total = top_score + jnp.log(row_total)
        probs_low = attn_probs.astype(jnp.bfloat16)
        attended = jnp.einsum(
            "hgqk,khd->qhgd", probs_low, values_all, preferred_element_type=jnp.float32
        )
        attended_low = attended.reshape(tok_dev, heads_here * HEAD_DIM).astype(jnp.bfloat16)
        attended_all = gather_cols(attended_low)
        attn_branch = sum_rows(project(attended_all, w_out))
        mixed = x_full + resid_scale * attn_branch
        mixed_rows = lax.all_to_all(
            mixed.reshape(col_count, quarter, width_part),
            "col",
            split_axis=0,
            concat_axis=2,
            tiled=True,
        ).reshape(quarter, model_width)
        scale_two = lax.rsqrt(jnp.mean(mixed_rows * mixed_rows, axis=1, keepdims=True) + eps_norm)
        unit_two = mixed_rows * scale_two
        normed_two = (unit_two * mix_gain).astype(jnp.bfloat16)
        logits = project(normed_two, w_router)
        picks = routes[step]
        choose = (picks[:, :, None] == expert_ids[None, None, :]).astype(jnp.float32)
        chosen = jnp.sum(choose * logits[:, None, :], axis=-1)
        gate_weights = jax.nn.softmax(chosen, axis=-1)
        flat_picks = picks.reshape(-1)
        hit_table = (flat_picks[:, None] == expert_ids[None, :]).astype(jnp.int32)
        slot_rank = jnp.sum(
            hit_table * (jnp.cumsum(hit_table, axis=0, dtype=jnp.int32) - 1),
            axis=1,
            dtype=jnp.int32,
        )
        owner_dp = flat_picks // experts_here
        local_expert = flat_picks % experts_here
        slot_index = local_expert * (dp_count * capacity) + owner_dp * capacity + slot_rank
        token_of = (
            jnp.full((slot_count,), quarter, jnp.int32)
            .at[slot_index]
            .set(jnp.arange(quarter * TOP, dtype=jnp.int32) // TOP)
        )
        padded = jnp.concatenate([normed_two, jnp.zeros((1, model_width), jnp.bfloat16)], axis=0)
        send_rows = padded[token_of].reshape(experts_here, dp_count * capacity, model_width)
        expert_in = expert_trade(send_rows)
        gate_proj = jnp.einsum(
            "ecd,edf->ecf", expert_in, full_gate, preferred_element_type=jnp.float32
        )
        up_proj = jnp.einsum("ecd,edf->ecf", expert_in, full_up, preferred_element_type=jnp.float32)
        activated = (jax.nn.silu(gate_proj) * up_proj).astype(jnp.bfloat16)
        expert_out = jnp.einsum(
            "ecf,efd->ecd", activated, full_down, preferred_element_type=jnp.float32
        ).astype(jnp.bfloat16)
        returned = expert_trade(expert_out).reshape(slot_count, model_width)
        combined = returned[slot_index].reshape(quarter, TOP, model_width).astype(jnp.float32)
        expert_mix = jnp.sum(gate_weights[:, :, None] * combined, axis=1)
        layer_rows.append((mixed_rows + resid_scale * expert_mix).astype(jnp.bfloat16))
        grad_rows = cotangent[step].astype(jnp.float32) * mask[step][:, None].astype(jnp.float32)
        grad_mix = resid_scale * grad_rows
        grad_gates = jnp.sum(grad_mix[:, None, :] * combined, axis=-1)
        grad_chosen = gate_weights * (
            grad_gates - jnp.sum(gate_weights * grad_gates, axis=-1, keepdims=True)
        )
        grad_logits = jnp.sum(choose * grad_chosen[:, :, None], axis=1)
        gate_slots = (
            jnp.zeros((slot_count,), jnp.float32).at[slot_index].set(gate_weights.reshape(-1))
        )
        grad_pad = jnp.concatenate([grad_mix, jnp.zeros((1, model_width), jnp.float32)], axis=0)
        grad_send = (gate_slots[:, None] * grad_pad[token_of]).astype(jnp.bfloat16)
        grad_expert = expert_trade(
            grad_send.reshape(experts_here, dp_count * capacity, model_width)
        )
        grad_act = jnp.einsum(
            "ecd,efd->ecf", grad_expert, full_down, preferred_element_type=jnp.float32
        )
        micro_down = jnp.einsum(
            "ecf,ecd->efd", activated, grad_expert, preferred_element_type=jnp.float32
        )
        sigmoid_gate = jax.nn.sigmoid(gate_proj)
        silu_gate = gate_proj * sigmoid_gate
        grad_gate_p = (
            grad_act * up_proj * (sigmoid_gate + gate_proj * sigmoid_gate * (1.0 - sigmoid_gate))
        ).astype(jnp.bfloat16)
        grad_up_p = (grad_act * silu_gate).astype(jnp.bfloat16)
        grad_in = jnp.einsum(
            "ecf,edf->ecd", grad_gate_p, full_gate, preferred_element_type=jnp.float32
        ) + jnp.einsum("ecf,edf->ecd", grad_up_p, full_up, preferred_element_type=jnp.float32)
        micro_gate = jnp.einsum(
            "ecd,ecf->edf", expert_in, grad_gate_p, preferred_element_type=jnp.float32
        )
        micro_up = jnp.einsum(
            "ecd,ecf->edf", expert_in, grad_up_p, preferred_element_type=jnp.float32
        )
        expert_local = add_all(expert_local, (micro_gate, micro_up, micro_down))
        grad_back = expert_trade(grad_in.astype(jnp.bfloat16)).reshape(slot_count, model_width)
        grad_normed = jnp.sum(
            grad_back[slot_index].reshape(quarter, TOP, model_width).astype(jnp.float32), axis=1
        ) + jnp.dot(grad_logits, router_wide.T, precision=highest)
        router_acc = router_acc + jnp.dot(
            normed_two.astype(jnp.float32).T, grad_logits, precision=highest
        )
        mix_acc = mix_acc + jnp.sum(grad_normed * unit_two, axis=0)
        grad_scaled = grad_normed * mix_gain
        grad_mixed_rows = grad_rows + scale_two * (
            grad_scaled - unit_two * jnp.mean(grad_scaled * unit_two, axis=1, keepdims=True)
        )
        grad_mixed = lax.all_to_all(
            grad_mixed_rows.reshape(1, quarter, model_width),
            "col",
            split_axis=2,
            concat_axis=0,
            tiled=True,
        ).reshape(tok_dev, width_part)
        grad_branch = (resid_scale * grad_mixed).astype(jnp.bfloat16)
        grad_branch_all = gather_rows(grad_branch)
        micro_out = jnp.dot(attended_all.T, grad_branch_all, preferred_element_type=jnp.float32)
        grad_attended = sum_cols(
            jnp.dot(grad_branch_all, w_out.T, preferred_element_type=jnp.float32)
        )
        grad_att_low = grad_attended.astype(jnp.bfloat16).reshape(
            tok_dev, kv_here, group_size, HEAD_DIM
        )
        probs_again = jnp.exp(scores - log_total)
        grad_probs = jnp.einsum(
            "qhgd,khd->hgqk", grad_att_low, values_all, preferred_element_type=jnp.float32
        )
        grad_scores = probs_again * (
            grad_probs - jnp.sum(probs_again * grad_probs, axis=-1, keepdims=True)
        )
        grad_raw = (grad_scores * attn_scale).astype(jnp.bfloat16)
        probs_again_low = probs_again.astype(jnp.bfloat16)
        grad_query = jnp.einsum(
            "hgqk,khd->qhgd", grad_raw, keys_all, preferred_element_type=jnp.float32
        )
        grad_key_part = jnp.einsum(
            "hgqk,qhgd->khd", grad_raw, query_grp, preferred_element_type=jnp.float32
        )
        grad_value_part = jnp.einsum(
            "hgqk,qhgd->khd", probs_again_low, grad_att_low, preferred_element_type=jnp.float32
        )
        grad_key, grad_value = sum_cols(
            (
                grad_key_part.reshape(group_tokens, kv_here * HEAD_DIM),
                grad_value_part.reshape(group_tokens, kv_here * HEAD_DIM),
            )
        )
        grad_query_p = (
            rotate(grad_query.reshape(tok_dev, heads_here, HEAD_DIM), -sin_table, cos_table)
            .astype(jnp.bfloat16)
            .reshape(tok_dev, heads_here * HEAD_DIM)
        )
        grad_key_p = (
            rotate(grad_key.reshape(tok_dev, kv_here, HEAD_DIM), -sin_table, cos_table)
            .astype(jnp.bfloat16)
            .reshape(tok_dev, kv_here * HEAD_DIM)
        )
        grad_value_p = grad_value.astype(jnp.bfloat16)
        query_all, key_all, value_all = gather_cols((grad_query_p, grad_key_p, grad_value_p))
        micro_query = jnp.dot(normed_all.T, query_all, preferred_element_type=jnp.float32)
        micro_key = jnp.dot(normed_all.T, key_all, preferred_element_type=jnp.float32)
        micro_value = jnp.dot(normed_all.T, value_all, preferred_element_type=jnp.float32)
        grad_normed_one = sum_rows(
            jnp.dot(query_all, w_query.T, preferred_element_type=jnp.float32)
            + jnp.dot(key_all, w_key.T, preferred_element_type=jnp.float32)
            + jnp.dot(value_all, w_value.T, preferred_element_type=jnp.float32)
        )
        grad_scaled_one = grad_normed_one * gain_part
        inner_sum = width_total(jnp.sum(grad_scaled_one * unit_one, axis=1))
        norm_acc = norm_acc + jnp.sum(grad_normed_one * unit_one, axis=0)
        input_grads.append(
            grad_mixed
            + scale_one * (grad_scaled_one - unit_one * (inner_sum / model_width)[:, None])
        )
        attn_local = add_all(attn_local, (micro_query, micro_key, micro_value, micro_out))
    attn_summed = attn_total(attn_local)
    expert_summed = expert_total(expert_local)
    gain_full = lax.dynamic_update_slice_in_dim(
        jnp.zeros((model_width,), jnp.float32), norm_acc, col_at * width_part, 0
    )
    router_grad, gain_grad, mix_grad = lax.psum(
        (router_acc, gain_full, mix_acc), ("dp", "row", "col")
    )
    return (
        jnp.stack(layer_rows),
        jnp.stack(input_grads),
        gain_grad,
        attn_summed[0],
        attn_summed[1],
        attn_summed[2],
        attn_summed[3],
        mix_grad,
        router_grad,
        expert_summed[0],
        expert_summed[1],
        expert_summed[2],
    )


def solution(mesh):
    placed = (
        P(None, ("dp", "row"), "col"),
        P(),
        P("col", "row"),
        P("col", "row"),
        P("col", "row"),
        P("row", "col"),
        P(),
        P(),
        P("dp", ("row", "col"), None),
        P("dp", ("row", "col"), None),
        P("dp", ("row", "col"), None),
        P(None, "dp", None),
        P(None, ("dp", "row", "col"), None),
        P(None, ("dp", "row", "col")),
        P(None, ("dp", "row", "col"), None),
    )
    return jax.shard_map(
        shards,
        mesh=mesh,
        in_specs=placed,
        out_specs=(
            P(None, ("dp", "row", "col"), None),
            P(None, ("dp", "row"), "col"),
            P(),
            P("col", "row"),
            P("col", "row"),
            P("col", "row"),
            P("row", "col"),
            P(),
            P(),
            P("dp", ("row", "col"), None),
            P("dp", ("row", "col"), None),
            P("dp", ("row", "col"), None),
        ),
        check_vma=False,
    )
```

profile of v0, /device:TPU:0, one launch (start us, length us, event | category | flops | bytes accessed | tf_op | source)
XLA Modules:
  0.0 2149.0 jit_solution(13491581628542257375)
XLA Ops:
  53.8 16.3 all_gather.59
  76.2 16.3 all_gather.58
  99.0 30.3 %reduce-scatter.32.cloned.1.call-done = f32[192,384]{1,0:T(8,128)} async-done(((f32[768,384]{1,0:T(8,128)}), f32[192,384]{1,0:T(8,128)}) %reduce-scatter.32.cloned.1.call-update) | async-done | bytes 294928 | tf_op jit(solution)/shard_map/reduce_scatter | solution.py:67
  133.9 20.3 all_gather.60
  156.8 18.6 all_gather.66
  177.0 17.9 all_gather.65
  199.9 16.4 all_gather.67
  231.3 25.9 %reduce-scatter.42.cloned.1.call-done = f32[192,384]{1,0:T(8,128)} async-done(((f32[768,384]{1,0:T(8,128)}), f32[192,384]{1,0:T(8,128)}) %reduce-scatter.42.cloned.1.call-update) | async-done | bytes 294928 | tf_op jit(solution)/shard_map/reduce_scatter | solution.py:71
  327.5 37.6 %all-gather.6.cloned.1.call-done = bf16[16,1536,512]{2,1,0:T(8,128)(2,1)} async-done(((bf16[16,96,512]{2,1,0:T(8,128)(2,1)}), bf16[16,1536,512]{2,1,0:T(8,128)(2,1)}) %all-gather.6.cloned.1.call-update) | async-done | bytes 25165840 | tf_op jit(solution)/shard_map/all_gather | solution.py:139
  376.7 127.8 %all-gather.4.cloned.1.call-done = bf16[16,1536,512]{2,1,0:T(8,128)(2,1)} async-done(((bf16[16,96,512]{2,1,0:T(8,128)(2,1)}), bf16[16,1536,512]{2,1,0:T(8,128)(2,1)}) %all-gather.4.cloned.1.call-update) | async-done | bytes 25165840 | tf_op jit(solution)/shard_map/all_gather | solution.py:138
  516.1 125.7 %all-gather.8.cloned.1.call-done = bf16[16,512,1536]{2,1,0:T(8,128)(2,1)} async-done(((bf16[16,32,1536]{2,1,0:T(8,128)(2,1)}), bf16[16,512,1536]{2,1,0:T(8,128)(2,1)}) %all-gather.8.cloned.1.call-update) | async-done | bytes 25165840 | tf_op jit(solution)/shard_map/all_gather | solution.py:140
  673.9 14.1 fusion.152
  688.1 15.0 add_convert_fusion.4
  840.6 14.2 fusion.156
  953.5 20.7 all_to_all.101
  994.5 20.0 reduce-scatter.48.cloned.1.call-done
  1069.7 18.5 all_gather.73
  1088.2 16.4 all_gather.69
  1111.3 14.9 all_gather.71
  1126.1 14.7 all_gather.75
  1140.8 14.5 all_gather.74
  1177.7 21.6 %fusion.19 = f32[16,512,1536]{2,1,0:T(8,128)} fusion(bf16[16,36,512]{2,1,0:T(8,128)(2,1)S(1)} %copy-done.18, bf16[16,36,1536]{2,0,1:T(8,128)(2,1)} %all-to-all-done.6), kind=kOutput, calls=%fused_computation.61 | convolution fusion | flops 905969664 | bytes 52690944 | tf_op jit(solution)/shard_map/ecf,ecd->efd/dot_general | solution.py:271
  1201.7 28.1 %add_convert_fusion = bf16[16,512,1536]{2,1,0:T(8,128)(2,1)} fusion(f32[16,512,1536]{2,1,0:T(8,128)} %fusion.19, bf16[16,36,512]{2,1,0:T(8,128)(2,1)S(1)} %copy-done.20, bf16[16,36,1536]{2,0,1:T(8,128)(2,1)} %all-to-all-done.9), kind=kOutput, calls=%fused_computation.14 | convolution fusion | flops 931135488 | bytes 77856768 | tf_op jit(solution)/shard_map/ecf,ecd->efd/dot_general | solution.py:271
  1231.4 20.2 fusion.45
  1251.6 27.0 %add_convert_fusion.1 = bf16[16,1536,512]{2,1,0:T(8,128)(2,1)} fusion(f32[16,1536,512]{2,1,0:T(8,128)} %fusion.45, bf16[16,36,512]{2,1,0:T(8,128)(2,1)S(1)} %get-tuple-element.41, bf16[16,36,1536]{2,0,1:T(8,128)(2,1)} %copy-done.4), kind=kOutput, calls=%fused_computation.15 | convolution fusion | flops 931135488 | bytes 77856768 | tf_op jit(solution)/shard_map/ecd,ecf->edf/dot_general | solution.py:286
  1280.0 28.6 %fusion.47 = f32[16,1536,512]{2,1,0:T(8,128)} fusion(bf16[16,36,512]{2,1,0:T(8,128)(2,1)S(1)} %copy-done.12, bf16[16,36,1536]{2,0,1:T(8,128)(2,1)S(1)} %copy-done.3), kind=kOutput, calls=%fused_computation.87 | convolution fusion | flops 905969664 | bytes 52690944 | tf_op jit(solution)/shard_map/ecd,ecf->edf/dot_general | solution.py:283
  1308.6 28.3 %add_convert_fusion.2 = bf16[16,1536,512]{2,1,0:T(8,128)(2,1)} fusion(f32[16,1536,512]{2,1,0:T(8,128)} %fusion.47, bf16[16,36,512]{2,1,0:T(8,128)(2,1)S(1)} %copy-done.16, bf16[16,36,1536]{2,0,1:T(8,128)(2,1)} %copy-done.4), kind=kOutput, calls=%fused_computation.16 | convolution fusion | flops 931135488 | bytes 77856768 | tf_op jit(solution)/shard_map/ecd,ecf->edf/dot_general | solution.py:283
  1357.8 44.2 %all-reduce.4 = (f32[1536]{0:T(1024)}, f32[1536]{0:T(1024)}) all-reduce(f32[1536]{0:T(1024)S(1)} %add_dynamic-update-slice_fusion, f32[1536]{0:T(1024)S(1)} %add.431), channel_id=1, replica_groups=mesh['dp'=2,'row'=4,'col'=4] {'dp','row','col'}, use_global_device_ids=true, to_apply=%region_68.69 | all-reduce | flops 3072 | bytes 24576 | tf_op jit(solution)/shard_map/psum | solution.py:375
  1404.2 111.2 %reduce-scatter.56.cloned.1.call-done = bf16[16,32,1536]{2,1,0:T(8,128)(2,1)} async-done(((bf16[16,512,1536]{2,1,0:T(8,128)(2,1)}), bf16[16,32,1536]{2,1,0:T(8,128)(2,1)}) %reduce-scatter.56.cloned.1.call-update) | async-done | bytes 1572880 | tf_op jit(solution)/shard_map/reduce_scatter | solution.py:89
  1518.9 244.1 %reduce-scatter.54.cloned.1.call-done = bf16[16,96,512]{2,1,0:T(8,128)(2,1)} async-done(((bf16[16,1536,512]{2,1,0:T(8,128)(2,1)}), bf16[16,96,512]{2,1,0:T(8,128)(2,1)}) %reduce-scatter.54.cloned.1.call-update) | async-done | bytes 1572880 | tf_op jit(solution)/shard_map/reduce_scatter | solution.py:89
  1766.5 243.9 %reduce-scatter.52.cloned.1.call-done = bf16[16,96,512]{2,1,0:T(8,128)(2,1)} async-done(((bf16[16,1536,512]{2,1,0:T(8,128)(2,1)}), bf16[16,96,512]{2,1,0:T(8,128)(2,1)}) %reduce-scatter.52.cloned.1.call-update) | async-done | bytes 1572880 | tf_op jit(solution)/shard_map/reduce_scatter | solution.py:89
  2013.9 125.7 %all-reduce.11.cloned.1.call-done = f32[1536,32]{0,1:T(8,128)} async-done(((f32[1536,32]{0,1:T(8,128)}), f32[1536,32]{0,1:T(8,128)}) %all-reduce.11.cloned.1.call-update) | async-done | bytes 196624 | tf_op jit(solution)/shard_map/psum | solution.py:375
  (617 shorter events, 591.5 us)
Async XLA Ops:
  8.0 44.6 %reduce-scatter.30.cloned.1.call-start = ((), (), s32[]{:S(2)}) async-start(), calls=%async_computation.32 | async-start | bytes 491520 | tf_op jit(solution)/shard_map/reduce_scatter | solution.py:67
  34.5 40.6 %reduce-scatter.28.cloned.1.call-start = ((), (), s32[]{:S(2)}) async-start(), calls=%async_computation.31 | async-start | bytes 491520 | tf_op jit(solution)/shard_map/reduce_scatter | solution.py:67
  35.6 62.4 %reduce-scatter.38.cloned.1.call-start = ((), (), s32[]{:S(2)}) async-start(), calls=%async_computation.39 | async-start | bytes 491520 | tf_op jit(solution)/shard_map/reduce_scatter | solution.py:67
  44.4 84.9 %reduce-scatter.32.cloned.1.call-start = ((), (), s32[]{:S(2)}) async-start(), calls=%async_computation.33 | async-start | bytes 1474560 | tf_op jit(solution)/shard_map/reduce_scatter | solution.py:67
  46.0 129.7 %reduce-scatter.36.cloned.1.call-start = ((), (), s32[]{:S(2)}) async-start(), calls=%async_computation.38 | async-start | bytes 491520 | tf_op jit(solution)/shard_map/reduce_scatter | solution.py:67
  47.2 148.1 %reduce-scatter.40.cloned.1.call-start = ((), (), s32[]{:S(2)}) async-start(), calls=%async_computation.40 | async-start | bytes 1474560 | tf_op jit(solution)/shard_map/reduce_scatter | solution.py:67
  48.8 182.5 %reduce-scatter.34.cloned.1.call-start = ((), (), s32[]{:S(2)}) async-start(), calls=%async_computation.34 | async-start | bytes 1474560 | tf_op jit(solution)/shard_map/reduce_scatter | solution.py:71
  156.6 100.7 %reduce-scatter.42.cloned.1.call-start = ((), (), s32[]{:S(2)}) async-start(), calls=%async_computation.41 | async-start | bytes 1474560 | tf_op jit(solution)/shard_map/reduce_scatter | solution.py:71
  218.7 146.4 %all-gather.6.cloned.1.call-start = ((), (), s32[]{:S(2)}) async-start(), calls=%async_computation.36 | async-start | bytes 26738688 | tf_op jit(solution)/shard_map/all_gather | solution.py:139
  219.3 285.2 %all-gather.4.cloned.1.call-start = ((), (), s32[]{:S(2)}) async-start(), calls=%async_computation.35 | async-start | bytes 26738688 | tf_op jit(solution)/shard_map/all_gather | solution.py:138
  219.9 421.9 %all-gather.8.cloned.1.call-start = ((), (), s32[]{:S(2)}) async-start(), calls=%async_computation.37 | async-start | bytes 26738688 | tf_op jit(solution)/shard_map/all_gather | solution.py:140
  296.5 26.2 %all-to-all-start.1 = ((bf16[16,36,1536]{2,0,1:T(8,128)(2,1)}), bf16[16,36,1536]{2,0,1:T(8,128)(2,1)S(1)}, u32[]{:S(2)}, u32[]{:S(2)}) async-start(bf16[16,36,1536]{2,0,1:T(8,128)(2,1)} %copy.322), calls=%async_computation.5 | async-start | bytes 3538944 | tf_op jit(solution)/shard_map/all_to_all | solution.py:79
  322.7 193.4 %all-to-all-start.6 = ((bf16[16,36,1536]{2,0,1:T(8,128)(2,1)}), bf16[16,36,1536]{2,0,1:T(8,128)(2,1)}, u32[]{:S(2)}, u32[]{:S(2)}) async-start(bf16[16,36,1536]{2,0,1:T(8,128)(2,1)} %copy.348), calls=%async_computation.14 | async-start | bytes 3538944 | tf_op jit(solution)/shard_map/all_to_all | solution.py:79
  670.0 36.3 %all-to-all-start.2 = ((bf16[16,36,1536]{2,0,1:T(8,128)(2,1)}), bf16[16,36,1536]{2,0,1:T(8,128)(2,1)S(1)}, u32[]{:S(2)}, u32[]{:S(2)}) async-start(bf16[16,36,1536]{2,0,1:T(8,128)(2,1)} %copy.325), calls=%async_computation.6 | async-start | bytes 3538944 | tf_op jit(solution)/shard_map/all_to_all | solution.py:79
  706.3 26.9 %all-to-all-start.7 = ((bf16[16,36,1536]{2,0,1:T(8,128)(2,1)}), bf16[16,36,1536]{2,0,1:T(8,128)(2,1)}, u32[]{:S(2)}, u32[]{:S(2)}) async-start(bf16[16,36,1536]{2,0,1:T(8,128)(2,1)} %copy.350), calls=%async_computation.15 | async-start | bytes 3538944 | tf_op jit(solution)/shard_map/all_to_all | solution.py:79
  754.4 25.0 %all-to-all-start.4 = ((bf16[16,36,1536]{2,0,1:T(8,128)(2,1)}), bf16[16,36,1536]{2,0,1:T(8,128)(2,1)S(1)}, u32[]{:S(2)}, u32[]{:S(2)}) async-start(bf16[16,36,1536]{2,0,1:T(8,128)(2,1)} %copy.342), calls=%async_computation.12 | async-start | bytes 3538944 | tf_op jit(solution)/shard_map/all_to_all | solution.py:79
  779.4 28.4 %all-to-all-start.9 = ((bf16[16,36,1536]{2,0,1:T(8,128)(2,1)}), bf16[16,36,1536]{2,0,1:T(8,128)(2,1)}, u32[]{:S(2)}, u32[]{:S(2)}) async-start(bf16[16,36,1536]{2,0,1:T(8,128)(2,1)} %copy.363), calls=%async_computation.19 | async-start | bytes 3538944 | tf_op jit(solution)/shard_map/all_to_all | solution.py:79
  835.9 34.3 %all-to-all-start.5 = ((bf16[16,36,1536]{2,0,1:T(8,128)(2,1)}), bf16[16,36,1536]{2,0,1:T(8,128)(2,1)}, u32[]{:S(2)}, u32[]{:S(2)}) async-start(bf16[16,36,1536]{2,0,1:T(8,128)(2,1)} %copy.345), calls=%async_computation.13 | async-start | bytes 3538944 | tf_op jit(solution)/shard_map/all_to_all | solution.py:79
  870.2 25.2 %all-to-all-start.10 = ((bf16[16,36,1536]{2,0,1:T(8,128)(2,1)}), bf16[16,36,1536]{2,0,1:T(8,128)(2,1)}, u32[]{:S(2)}, u32[]{:S(2)}) async-start(bf16[16,36,1536]{2,0,1:T(8,128)(2,1)} %copy.365), calls=%async_computation.20 | async-start | bytes 3538944 | tf_op jit(solution)/shard_map/all_to_all | solution.py:79
  874.9 114.5 %reduce-scatter.44.cloned.1.call-start = ((), (), s32[]{:S(2)}) async-start(), calls=%async_computation.42 | async-start | bytes 1474560 | tf_op jit(solution)/shard_map/reduce_scatter | solution.py:67
  943.1 71.4 %reduce-scatter.48.cloned.1.call-start = ((), (), s32[]{:S(2)}) async-start(), calls=%async_computation.44 | async-start | bytes 1474560 | tf_op jit(solution)/shard_map/reduce_scatter | solution.py:67
  987.2 121.0 %reduce-scatter.62.cloned.1.call-start = ((), (), s32[]{:S(2)}) async-start(), calls=%async_computation.52 | async-start | bytes 491520
  1029.9 79.5 %reduce-scatter.60.cloned.1.call-start = ((), (), s32[]{:S(2)}) async-start(), calls=%async_computation.51 | async-start | bytes 491520 | tf_op jit(solution)/shard_map/reduce_scatter | solution.py:67
  1044.8 65.6 %reduce-scatter.64.cloned.1.call-start = ((), (), s32[]{:S(2)}) async-start(), calls=%async_computation.53 | async-start | bytes 491520 | tf_op jit(solution)/shard_map/reduce_scatter | solution.py:67
  1069.4 87.1 %reduce-scatter.58.cloned.1.call-start = ((), (), s32[]{:S(2)}) async-start(), calls=%async_computation.50 | async-start | bytes 491520
  1105.9 234.3 %all-reduce.13.cloned.1.call-start = ((), (), s32[]{:S(2)}) async-start(), calls=%async_computation.54 | async-start | bytes 1572864 | tf_op jit(solution)/shard_map/psum | solution.py:83
  1175.3 171.7 %reduce-scatter.50.cloned.1.call-start = ((), (), s32[]{:S(2)}) async-start(), calls=%async_computation.45 | async-start | bytes 1474560 | tf_op jit(solution)/shard_map/reduce_scatter | solution.py:71
  1177.6 169.4 %reduce-scatter.46.cloned.1.call-start = ((), (), s32[]{:S(2)}) async-start(), calls=%async_computation.43 | async-start | bytes 1474560 | tf_op jit(solution)/shard_map/reduce_scatter | solution.py:71
  1201.6 313.8 %reduce-scatter.56.cloned.1.call-start = ((), (), s32[]{:S(2)}) async-start(), calls=%async_computation.49 | async-start | bytes 26738688 | tf_op jit(solution)/shard_map/reduce_scatter | solution.py:89
  1229.8 533.2 %reduce-scatter.54.cloned.1.call-start = ((), (), s32[]{:S(2)}) async-start(), calls=%async_computation.48 | async-start | bytes 26738688 | tf_op jit(solution)/shard_map/reduce_scatter | solution.py:89
  1278.7 731.7 %reduce-scatter.52.cloned.1.call-start = ((), (), s32[]{:S(2)}) async-start(), calls=%async_computation.47 | async-start | bytes 26738688 | tf_op jit(solution)/shard_map/reduce_scatter | solution.py:89
  1337.0 802.5 %all-reduce.11.cloned.1.call-start = ((), (), s32[]{:S(2)}) async-start(), calls=%async_computation.46 | async-start | bytes 393216 | tf_op jit(solution)/shard_map/psum | solution.py:375
  (132 other events, 2267.2 us)
Sparse Core Ops, SparseCore 0:
  34.6 17.9 reduce-scatter.29
  55.6 19.4 reduce-scatter.27
  77.3 20.6 reduce-scatter.37
  100.9 28.4 reduce-scatter.31
  131.6 22.1 reduce-scatter.35
  156.5 36.4 reduce-scatter.39
  196.1 25.5 reduce-scatter.33
  225.0 32.1 reduce-scatter.41
  943.2 31.2 reduce-scatter.43
  987.3 27.0 reduce-scatter.47
  1030.0 19.3 reduce-scatter.61
  1052.2 18.9 reduce-scatter.59
  1073.4 19.7 reduce-scatter.63
  1106.0 20.7 reduce-scatter.57
  1175.4 33.3 all-reduce.12
  1211.9 25.7 reduce-scatter.49
  1240.7 25.7 reduce-scatter.45
  1270.9 244.3 reduce-scatter.55
  1520.1 242.8 reduce-scatter.53
  1767.5 242.8 reduce-scatter.51
  2017.5 122.0 all-reduce.10
Sparse Core Ops, SparseCore 1:
  220.7 144.3 all-gather.5
  366.5 137.9 all-gather.3
  505.9 135.8 all-gather.7
where the time goes:
time: 2160 us; the launch traced here: 2150 us
  waiting for transfers between devices  1150 us (53%)
  matrix products  400 us (19%)
  blocking collectives  329 us (15%)
  local copies, waits for them, and re-layouts  126 us (6%)
  other arithmetic  76.4 us (4%)
  starting transfers between devices  46.1 us (2%)
    reduce_scatter x3, waiting for transfers between devices, expert_total(): lax.psum_scatter(shortened(value), ('row', 'col'), scatter_dimension=1, t...  599 us
    all_gather x8, blocking collectives, gather_cols(): lax.all_gather(shortened(value), 'col', axis=0, tiled=True)  130 us
    all_gather x1, waiting for transfers between devices, shards(): lax.all_gather(w_gate, ('row', 'col'), axis=1, tiled=True)  128 us
    all_gather x1, waiting for transfers between devices, shards(): lax.all_gather(w_down, ('row', 'col'), axis=1, tiled=True)  126 us
    psum x1, waiting for transfers between devices, shards(): lax.psum((router_acc, gain_full, mix_acc), ('dp', 'row', 'col'))  126 us
    reduce_scatter x10, waiting for transfers between devices, sum_cols(): return lax.psum_scatter(pieces, 'col', scatter_dimension=0, tiled=True)  61.5 us
    dot_general x2, matrix products, shards(): jnp.einsum('ecd,ecf->edf', expert_in, grad_gate_p, preferred_element_type...  57 us
    dot_general x2, matrix products, shards(): jnp.einsum('ecf,ecd->efd', activated, grad_expert, preferred_element_type...  49.7 us
  transfers between devices with their start and end apart: 34, of which 18 were waited for; matrix products, arithmetic and copies ran while one was open for 22% of the time, Pallas kernels for 0%

commit v1 on v0

--- a/solution.py
+++ b/solution.py
@@ -391,7 +391,316 @@
     )
 
 
+def spread_plane(blocks):
+    return lax.all_to_all(blocks, ("row", "col"), split_axis=0, concat_axis=0, tiled=True)
+
+
+def spread_cols(blocks):
+    return lax.all_to_all(blocks, "col", split_axis=0, concat_axis=0, tiled=True)
+
+
+def owned(
+    hidden_in,
+    norm_gain,
+    w_query,
+    w_key,
+    w_value,
+    w_out,
+    mix_gain,
+    w_router,
+    w_gate,
+    w_up,
+    w_down,
+    lengths,
+    routes,
+    mask,
+    cotangent,
+):
+    everyone = ("dp", "row", "col")
+    plane = ("row", "col")
+    micro_count, tok_row, width_part = hidden_in.shape
+    row_count = lax.axis_size("row")
+    col_count = lax.axis_size("col")
+    dp_count = lax.axis_size("dp")
+    row_at = lax.axis_index("row")
+    col_at = lax.axis_index("col")
+    dp_at = lax.axis_index("dp")
+    plane_count = row_count * col_count
+    device_count = plane_count * dp_count
+    plane_at = row_at * col_count + col_at
+    model_width = width_part * col_count
+    kv_here = w_key.shape[1] // HEAD_DIM
+    group_size = w_query.shape[1] // w_key.shape[1]
+    q_width = group_size * HEAD_DIM
+    group_tokens = tok_row * row_count
+    quarter = tok_row // col_count
+    own_rows = micro_count * quarter
+    experts_here, slice_width, ff_width = w_gate.shape
+    down_slice = w_down.shape[1]
+    experts_all = experts_here * dp_count
+    expert_at = dp_at * plane_count + plane_at
+    micro_at = col_at // kv_here
+    half_at = col_at % kv_here
+
+    gate_own = spread_plane(w_gate).reshape(model_width, ff_width)
+    up_own = spread_plane(w_up).reshape(model_width, ff_width)
+    down_own = spread_plane(w_down).reshape(ff_width, model_width)
+
+    masked_cot = cotangent * mask[:, :, None].astype(cotangent.dtype)
+    cot_all = lax.all_gather(
+        masked_cot.reshape(own_rows, model_width), everyone, axis=0, tiled=True
+    )
+    routes_all = lax.all_gather(routes.reshape(own_rows, TOP), everyone, axis=0, tiled=True)
+
+    to_micro = jnp.arange(col_count) // kv_here
+    x_send = jnp.broadcast_to(
+        hidden_in[to_micro][None], (row_count, col_count, tok_row, width_part)
+    ).reshape(plane_count, tok_row, width_part)
+    x_micro = (
+        spread_plane(x_send)
+        .reshape(row_count, col_count, tok_row, width_part)
+        .transpose(0, 2, 1, 3)
+        .reshape(group_tokens, model_width)
+        .astype(jnp.float32)
+    )
+    x_own = (
+        spread_cols(
+            hidden_in.reshape(micro_count, col_count, quarter, width_part).transpose(1, 0, 2, 3)
+        )
+        .transpose(1, 2, 0, 3)
+        .reshape(own_rows, model_width)
+        .astype(jnp.float32)
+    )
+    w_qkv = jnp.concatenate(
+        [
+            w_query.reshape(width_part, kv_here, q_width),
+            w_key.reshape(width_part, kv_here, HEAD_DIM),
+            w_value.reshape(width_part, kv_here, HEAD_DIM),
+        ],
+        axis=2,
+    ).transpose(1, 0, 2)
+    qkv_width = q_width + 2 * HEAD_DIM
+    to_half = jnp.arange(col_count) % kv_here
+    w_mine = spread_cols(w_qkv[to_half]).reshape(model_width, qkv_width)
+    w_qkv_all = (
+        lax.all_gather(w_qkv, plane, axis=0, tiled=False)
+        .reshape(row_count, col_count, kv_here, width_part, qkv_width)
+        .transpose(1, 3, 0, 2, 4)
+        .reshape(model_width, row_count * kv_here * qkv_width)
+    )
+    w_out_all = (
+        lax.all_gather(w_out, plane, axis=0, tiled=False)
+        .reshape(row_count, col_count, w_out.shape[0], w_out.shape[1])
+        .transpose(0, 2, 1, 3)
+        .reshape(row_count * w_out.shape[0], model_width)
+    )
+
+    scale_m = lax.rsqrt(jnp.mean(x_micro * x_micro, axis=1, keepdims=True) + eps_norm)
+    normed_m = (x_micro * scale_m * norm_gain).astype(jnp.bfloat16)
+    qkv = project(normed_m, w_mine)
+    doc_id, position = documents(lengths[:, 0][micro_at], group_tokens)
+    sin_table, cos_table = angles(position.astype(jnp.float32), HEAD_DIM)
+    query = rotate(
+        qkv[:, :q_width].reshape(group_tokens, group_size, HEAD_DIM), sin_table, cos_table
+    ).astype(jnp.bfloat16)
+    key = rotate(
+        qkv[:, q_width : q_width + HEAD_DIM].reshape(group_tokens, 1, HEAD_DIM),
+        sin_table,
+        cos_table,
+    )[:, 0].astype(jnp.bfloat16)
+    value = qkv[:, q_width + HEAD_DIM :].astype(jnp.bfloat16)
+    order = jnp.arange(group_tokens, dtype=jnp.int32)
+    allowed = (doc_id[:, None] == doc_id[None, :]) & (order[None, :] <= order[:, None])
+    raw_scores = jnp.einsum("qgd,kd->gqk", query, key, preferred_element_type=jnp.float32)
+    scores = jnp.where(allowed[None], raw_scores * attn_scale, -1e30)
+    probs = jax.nn.softmax(scores, axis=-1)
+    probs_low = probs.astype(jnp.bfloat16)
+    attended = (
+        jnp.einsum("gqk,kd->qgd", probs_low, value, preferred_element_type=jnp.float32)
+        .reshape(group_tokens, q_width)
+        .astype(jnp.bfloat16)
+    )
+
+    attended_own = (
+        spread_plane(attended.reshape(plane_count, quarter, q_width))
+        .reshape(row_count, micro_count, kv_here, quarter, q_width)
+        .transpose(1, 3, 0, 2, 4)
+        .reshape(own_rows, row_count * kv_here * q_width)
+    )
+    mixed = x_own + resid_scale * project(attended_own, w_out_all)
+    scale_two = lax.rsqrt(jnp.mean(mixed * mixed, axis=1, keepdims=True) + eps_norm)
+    unit_two = mixed * scale_two
+    normed_two = (unit_two * mix_gain).astype(jnp.bfloat16)
+    expert_ids = jnp.arange(experts_all, dtype=jnp.int32)
+
+    def gating(normed_rows, picks):
+        chosen = jnp.any(picks[:, :, None] == expert_ids[None, None, :], axis=1)
+        logits = jnp.where(chosen, project(normed_rows, w_router), -jnp.inf)
+        return jax.nn.softmax(logits, axis=-1)
+
+    normed_all = lax.all_gather(normed_two, everyone, axis=0, tiled=True)
+    gates_all = gating(normed_all, routes_all)
+    gates_own = gating(normed_two, routes.reshape(own_rows, TOP))
+    gate_mine = jnp.sum(
+        gates_all * (expert_ids == expert_at).astype(jnp.float32)[None, :], axis=1, keepdims=True
+    )
+
+    gate_proj = project(normed_all, gate_own)
+    up_proj = project(normed_all, up_own)
+    sigmoid_gate = jax.nn.sigmoid(gate_proj)
+    silu_gate = gate_proj * sigmoid_gate
+    activated = (silu_gate * up_proj).astype(jnp.bfloat16)
+    expert_out = project(activated, down_own).astype(jnp.bfloat16).astype(jnp.float32)
+    grad_mix = resid_scale * cot_all.astype(jnp.float32)
+    grad_gate_mine = jnp.sum(grad_mix * expert_out, axis=1)
+    mix_part = (gate_mine * expert_out).astype(jnp.bfloat16)
+    grad_out_rows = (gate_mine * grad_mix).astype(jnp.bfloat16)
+    grad_act = jnp.dot(grad_out_rows, down_own.T, preferred_element_type=jnp.float32)
+    grad_gate_p = (
+        grad_act * up_proj * (sigmoid_gate + gate_proj * sigmoid_gate * (1.0 - sigmoid_gate))
+    ).astype(jnp.bfloat16)
+    grad_up_p = (grad_act * silu_gate).astype(jnp.bfloat16)
+    grad_rows_part = (
+        jnp.dot(grad_gate_p, gate_own.T, preferred_element_type=jnp.float32)
+        + jnp.dot(grad_up_p, up_own.T, preferred_element_type=jnp.float32)
+    ).astype(jnp.bfloat16)
+    grad_down_own = jnp.dot(activated.T, grad_out_rows, preferred_element_type=jnp.float32)
+    grad_gate_own = jnp.dot(normed_all.T, grad_gate_p, preferred_element_type=jnp.float32)
+    grad_up_own = jnp.dot(normed_all.T, grad_up_p, preferred_element_type=jnp.float32)
+
+    def back_to_slices(grad, parts, depth):
+        return spread_plane(
+            grad.astype(jnp.bfloat16).reshape(parts, depth, grad.shape[1])
+        ).astype(jnp.float32)
+
+    out_gate = back_to_slices(grad_gate_own, experts_here, slice_width)
+    out_up = back_to_slices(grad_up_own, experts_here, slice_width)
+    out_down = back_to_slices(grad_down_own, experts_here, down_slice)
+
+    grad_gates = lax.all_to_all(
+        grad_gate_mine.reshape(device_count, own_rows), everyone, 0, 0, tiled=True
+    ).T
+    chosen_own = jnp.any(
+        routes.reshape(own_rows, TOP)[:, :, None] == expert_ids[None, None, :], axis=1
+    )
+    grad_gates = jnp.where(chosen_own, grad_gates, 0.0)
+    grad_logits = gates_own * (
+        grad_gates - jnp.sum(gates_own * grad_gates, axis=1, keepdims=True)
+    )
+    grad_logits_all = lax.all_gather(grad_logits, everyone, axis=0, tiled=True)
+    router_grad = jnp.dot(
+        normed_all.astype(jnp.float32).T, grad_logits_all, precision=highest
+    )
+    expert_mix = lax.psum_scatter(mix_part, everyone, scatter_dimension=0, tiled=True)
+    layer_out = (mixed + resid_scale * expert_mix.astype(jnp.float32)).astype(jnp.bfloat16)
+    grad_normed = lax.psum_scatter(
+        grad_rows_part, everyone, scatter_dimension=0, tiled=True
+    ).astype(jnp.float32) + jnp.dot(
+        grad_logits, w_router.astype(jnp.float32).T, precision=highest
+    )
+    mix_part_grad = jnp.sum(grad_normed * unit_two, axis=0)
+    grad_scaled = grad_normed * mix_gain
+    grad_mixed = masked_cot.reshape(own_rows, model_width).astype(jnp.float32) + scale_two * (
+        grad_scaled - unit_two * jnp.mean(grad_scaled * unit_two, axis=1, keepdims=True)
+    )
+    grad_branch = (resid_scale * grad_mixed).astype(jnp.bfloat16)
+
+    branch_send = jnp.broadcast_to(
+        grad_branch.reshape(micro_count, quarter, model_width)[to_micro][None],
+        (row_count, col_count, quarter, model_width),
+    ).reshape(plane_count, quarter, model_width)
+    branch_m = spread_plane(branch_send).reshape(group_tokens, model_width)
+    w_out_mine = lax.dynamic_slice_in_dim(
+        w_out_all, (row_at * kv_here + half_at) * q_width, q_width
+    )
+    grad_att = (
+        jnp.dot(branch_m, w_out_mine.T, preferred_element_type=jnp.float32)
+        .astype(jnp.bfloat16)
+        .reshape(group_tokens, group_size, HEAD_DIM)
+    )
+    out_part = jnp.dot(attended.T, branch_m, preferred_element_type=jnp.float32)
+    grad_probs = jnp.einsum("qgd,kd->gqk", grad_att, value, preferred_element_type=jnp.float32)
+    grad_scores = probs * (grad_probs - jnp.sum(probs * grad_probs, axis=-1, keepdims=True))
+    grad_raw = (grad_scores * attn_scale).astype(jnp.bfloat16)
+    grad_query = jnp.einsum("gqk,kd->qgd", grad_raw, key, preferred_element_type=jnp.float32)
+    grad_key = jnp.einsum("gqk,qgd->kd", grad_raw, query, preferred_element_type=jnp.float32)
+    grad_value = jnp.einsum("gqk,qgd->kd", probs_low, grad_att, preferred_element_type=jnp.float32)
+    grad_qkv = jnp.concatenate(
+        [
+            rotate(grad_query, -sin_table, cos_table).reshape(group_tokens, q_width),
+            rotate(grad_key[:, None], -sin_table, cos_table)[:, 0],
+            grad_value,
+        ],
+        axis=1,
+    ).astype(jnp.bfloat16)
+    qkv_part = jnp.dot(normed_m.T, grad_qkv, preferred_element_type=jnp.float32)
+    grad_qkv_own = (
+        spread_plane(grad_qkv.reshape(plane_count, quarter, qkv_width))
+        .reshape(row_count, micro_count, kv_here, quarter, qkv_width)
+        .transpose(1, 3, 0, 2, 4)
+        .reshape(own_rows, row_count * kv_here * qkv_width)
+    )
+    grad_normed_one = jnp.dot(grad_qkv_own, w_qkv_all.T, preferred_element_type=jnp.float32)
+    scale_one = lax.rsqrt(jnp.mean(x_own * x_own, axis=1, keepdims=True) + eps_norm)
+    unit_one = x_own * scale_one
+    norm_part = jnp.sum(grad_normed_one * unit_one, axis=0)
+    grad_scaled_one = grad_normed_one * norm_gain
+    grad_x = grad_mixed + scale_one * (
+        grad_scaled_one
+        - unit_one * jnp.mean(grad_scaled_one * unit_one, axis=1, keepdims=True)
+    )
+    grad_input = (
+        spread_cols(
+            grad_x.reshape(micro_count, quarter, col_count, width_part).transpose(2, 0, 1, 3)
+        )
+        .transpose(1, 0, 2, 3)
+        .reshape(micro_count, tok_row, width_part)
+    )
+
+    def halves(part):
+        low_part = spread_cols(part.astype(jnp.bfloat16)).astype(jnp.float32)
+        return jnp.sum(
+            low_part.reshape((micro_count, kv_here) + part.shape[1:]), axis=0
+        ).astype(jnp.bfloat16)
+
+    qkv_sum = halves(qkv_part.reshape(col_count, width_part, qkv_width))
+    out_sum = halves(
+        out_part.reshape(q_width, col_count, width_part).transpose(1, 0, 2)
+    )
+    qkv_sum, out_sum = attn_total(
+        (qkv_sum.astype(jnp.float32), out_sum.astype(jnp.float32))
+    )
+    grad_wq = qkv_sum[:, :, :q_width].transpose(1, 0, 2).reshape(w_query.shape)
+    grad_wk = qkv_sum[:, :, q_width : q_width + HEAD_DIM].transpose(1, 0, 2).reshape(w_key.shape)
+    grad_wv = qkv_sum[:, :, q_width + HEAD_DIM :].transpose(1, 0, 2).reshape(w_value.shape)
+    grad_wo = out_sum.reshape(w_out.shape)
+    gain_grads = lax.psum(jnp.stack([norm_part, mix_part_grad]), everyone)
+    return (
+        layer_out.reshape(micro_count, quarter, model_width),
+        grad_input,
+        gain_grads[0],
+        grad_wq,
+        grad_wk,
+        grad_wv,
+        grad_wo,
+        gain_grads[1],
+        router_grad,
+        out_gate,
+        out_up,
+        out_down,
+    )
+
+
 def solution(mesh):
+    dp_count, row_count, col_count = (mesh.shape[name] for name in ("dp", "row", "col"))
+
+    def body(*args):
+        hidden_in, w_key, w_gate = args[0], args[3], args[8]
+        kv_here = w_key.shape[1] // HEAD_DIM
+        one_each = w_gate.shape[0] == row_count * col_count
+        pairs = hidden_in.shape[0] * kv_here == col_count
+        return (owned if one_each and pairs else shards)(*args)
+
     placed = (
         P(None, ("dp", "row"), "col"),
         P(),
@@ -410,7 +719,7 @@
         P(None, ("dp", "row", "col"), None),
     )
     return jax.shard_map(
-        shards,
+        body,
         mesh=mesh,
         in_specs=placed,
         out_specs=(

time: 2160 us -> 1090 us (0.50)
  waiting for transfers between devices: 1150 us -> 395 us
  matrix products: 400 us -> 177 us
  other arithmetic: 76.4 us -> 32.4 us
  local copies, waits for them, and re-layouts: 126 us -> 85.6 us
  blocking collectives: 329 us -> 302 us
  starting transfers between devices: 46.1 us -> 68 us
    reduce_scatter x17 -> x2, waiting for transfers between devices: 687 us -> 118 us  [the longest x1 118 us: owned(): lax.psum_scatter(grad_rows_part, everyone, scatter_dimension=0, tiled=True)]
    all_gather x3 -> x4, waiting for transfers between devices: 291 us -> 0.05 us  [the longest x1 0.02 us: owned(): lax.all_gather(w_out, plane, axis=0, tiled=False)]
    dot_general x50 -> x17, matrix products: 389 us -> 129 us  [the longest x1 15 us: owned(): jnp.dot(grad_out_rows, down_own.T, preferred_element_type=jnp.float32)]
    all_to_all x10 -> x15, waiting for transfers between devices: 47.5 us -> 275 us  [the longest x9 211 us: spread_plane(): lax.all_to_all(blocks, ('row', 'col'), split_axis=0, concat_axis=0, tiled...]
    psum x1 -> x0, waiting for transfers between devices: 126 us -> none  [shards(): lax.psum((router_acc, gain_full, mix_acc), ('dp', 'row', 'col'))]
    all_gather x16 -> x2, blocking collectives: 231 us -> 201 us  [the longest x1 117 us: owned(): lax.all_gather(routes.reshape(own_rows, TOP), everyone, axis=0, tiled=True)]
    all_to_all x2 -> x1, blocking collectives: 31 us -> 61.5 us  [spread_plane(): lax.all_to_all(blocks, ('row', 'col'), split_axis=0, concat_axis=0, tiled...]
    gather x10 -> x3, local copies, waits for them, and re-layouts: 34.7 us -> 4.79 us  [the longest x1 2.48 us: owned(): grad_branch.reshape(micro_count, quarter, model_width)[to_micro][None]]
  transfers between devices with their start and end apart: 34 -> 22, of which waited for: 18 -> 10; matrix products, arithmetic and copies ran while one was open for 22% -> 21% of each run, Pallas kernels for 0% -> 0%
where the time goes in v1:
time: 1090 us; the launch traced here: 1080 us
  waiting for transfers between devices  395 us (36%)
  blocking collectives  302 us (28%)
  matrix products  177 us (16%)
  local copies, waits for them, and re-layouts  85.6 us (8%)
  starting transfers between devices  68 us (6%)
  other arithmetic  32.4 us (3%)
  between operations  15.6 us (1%)
    all_to_all x9, waiting for transfers between devices, spread_plane(): lax.all_to_all(blocks, ('row', 'col'), split_axis=0, concat_axis=0, tiled...  211 us
    reduce_scatter x1, waiting for transfers between devices, owned(): lax.psum_scatter(grad_rows_part, everyone, scatter_dimension=0, tiled=True)  118 us
    all_gather x1, blocking collectives, owned(): lax.all_gather(routes.reshape(own_rows, TOP), everyone, axis=0, tiled=True)  117 us
    all_gather x1, blocking collectives, owned(): grad_logits_all = lax.all_gather(grad_logits, everyone, axis=0, tiled=True)  83.9 us
    all_to_all x5, waiting for transfers between devices, spread_cols(): lax.all_to_all(blocks, 'col', split_axis=0, concat_axis=0, tiled=True)  64.1 us
    all_to_all x1, blocking collectives, spread_plane(): lax.all_to_all(blocks, ('row', 'col'), split_axis=0, concat_axis=0, tiled...  61.5 us
    all_to_all x9, starting transfers between devices, spread_plane(): lax.all_to_all(blocks, ('row', 'col'), split_axis=0, concat_axis=0, tiled...  42.4 us
    dot_general x7, matrix products, project(): return jnp.dot(left_side, right_side, preferred_element_type=jnp.float32)  41 us
  transfers between devices with their start and end apart: 22, of which 10 were waited for; matrix products, arithmetic and copies ran while one was open for 21% of the time, Pallas kernels for 0%

profile of v1, /device:TPU:0, one launch (start us, length us, event | category | flops | bytes accessed | tf_op | source)
XLA Modules:
  0.0 1075.6 jit_solution(12343048898039471448)
XLA Ops:
  12.2 6.3 all-to-all-start.2
  20.0 32.4 %all-to-all-done.2 = bf16[4,384,320]{1,2,0:T(8,128)(2,1)S(1)} async-done(((bf16[4,384,320]{1,2,0:T(8,128)(2,1)}), bf16[4,384,320]{1,2,0:T(8,128)(2,1)S(1)}, u32[]{:S(2)}, u32[]{:S(2)}) %all-to-all-start.2) | async-done | bytes 983072 | tf_op jit(solution)/shard_map/all_to_all | solution.py:399
  63.6 67.1 %all-to-all-done.1 = bf16[16,192,384]{2,1,0:T(8,128)(2,1)S(1)} async-done(((bf16[16,192,384]{2,1,0:T(8,128)(2,1)}), bf16[16,192,384]{2,1,0:T(8,128)(2,1)S(1)}, u32[]{:S(2)}, u32[]{:S(2)}) %all-to-all-start.1) | async-done | bytes 2359328 | tf_op jit(solution)/shard_map/all_to_all | solution.py:395
  140.2 6.5 fusion.99
  161.5 11.4 %all-to-all-done.3 = bf16[16,48,192]{2,1,0:T(8,128)(2,1)S(1)} async-done(((bf16[16,48,192]{2,1,0:T(8,128)(2,1)}), bf16[16,48,192]{2,1,0:T(8,128)(2,1)S(1)}, u32[]{:S(2)}, u32[]{:S(2)}) %all-to-all-start.3) | async-done | bytes 294944 | tf_op jit(solution)/shard_map/all_to_all | solution.py:395
  175.3 6.0 copy.165
  191.2 61.5 %all_to_all.87 = bf16[16,96,512]{2,1,0:T(8,128)(2,1)} all-to-all(bf16[16,96,512]{2,1,0:T(8,128)(2,1)} %param.23), channel_id=1, replica_groups=mesh['dp'=2,'row'=4,'col'=4] {'row','col'}, dimensions={0} | all-to-all | bytes 3145728 | tf_op jit(solution)/shard_map/all_to_all | solution.py:395
  257.3 116.7 %all-gather.2 = s32[32,96,8]{1,2,0:T(8,128)S(1)} all-gather(s32[1,96,8]{1,2,0:T(8,128)S(1)} %reshape.630), channel_id=1, replica_groups=mesh['dp'=2,'row'=4,'col'=4] {'dp','row','col'}, dimensions={0}, use_global_device_ids=true | all-gather | bytes 101376 | tf_op jit(solution)/shard_map/all_gather | solution.py:453
  374.6 6.5 fusion.100
  387.0 10.4 fusion.105
  397.5 6.9 fusion.104
  404.4 23.6 %all-to-all-done.6 = bf16[16,32,1536]{2,1,0:T(8,128)(2,1)} async-done(((bf16[16,32,1536]{2,1,0:T(8,128)(2,1)}), bf16[16,32,1536]{2,1,0:T(8,128)(2,1)}, u32[]{:S(2)}, u32[]{:S(2)}) %all-to-all-start.6) | async-done | bytes 1572896 | tf_op jit(solution)/shard_map/all_to_all | solution.py:395
  428.0 15.0 %multiply_convert_fusion = (bf16[3072,512]{1,0:T(8,128)(2,1)S(1)}, bf16[3072,512]{1,0:T(8,128)(2,1)S(1)}, bf16[3072,512]{1,0:T(8,128)(2,1)}) fusion(f32[3072,512]{1,0:T(8,128)} %fusion.104, f32[3072,512]{1,0:T(8,128)} %fusion.105, bf16[512,1536]{1,0:T(8,128)(2,1)} %bitcast.29, bf16[3072,1536]{1,0:T(8,128)(2,1)} %all-gather.11.cloned.1.call-done, ...), kind=kOutput, calls=%fused_computation.24 | convolution fusion | flops 4868014080 | bytes 33042432 | tf_op jit(solution)/shard_map/dot_general | solution.py:558
  443.0 9.4 fusion.106
  452.4 11.8 %add_convert_fusion = bf16[3072,1536]{1,0:T(8,128)(2,1)} fusion(f32[3072,1536]{1,0:T(8,128)} %fusion.106, bf16[3072,512]{1,0:T(8,128)(2,1)S(1)} %get-tuple-element.80, bf16[1536,512]{1,0:T(8,128)(2,1)} %bitcast.28), kind=kOutput, calls=%fused_computation.12 | convolution fusion | flops 4841275392 | bytes 33030144 | tf_op jit(solution)/shard_map/dot_general | solution.py:565
  464.9 11.6 %fusion.3 = (f32[3072]{0:T(1024)S(1)}, bf16[3072,1536]{1,0:T(8,128)(2,1)}) fusion(bf16[3072,1536]{1,0:T(8,128)(2,1)} %all-gather.11.cloned.1.call-done, f32[3072]{0:T(1024)S(1)} %copy-done.39, bf16[3072,512]{1,0:T(8,128)(2,1)} %get-tuple-element.82, bf16[512,1536]{1,0:T(8,128)(2,1)} %bitcast.29), kind=kOutput, calls=%fused_computation.10 | convolution fusion | flops 4869583872 | bytes 23617536 | tf_op jit(solution)/shard_map/dot_general | solution.py:98
  479.8 10.3 fusion.26
  490.1 6.1 all-to-all-start.15
  497.6 118.5 %reduce-scatter.5.cloned.1.call-done = bf16[96,1536]{1,0:T(8,128)(2,1)} async-done(((bf16[3072,1536]{1,0:T(8,128)(2,1)}), bf16[96,1536]{1,0:T(8,128)(2,1)}) %reduce-scatter.5.cloned.1.call-update) | async-done | bytes 294928 | tf_op jit(solution)/shard_map/reduce_scatter | solution.py:596
  630.5 10.5 convolution_convert_fusion.1
  640.9 87.1 %all-to-all-done.8 = bf16[16,48,1536]{2,1,0:T(8,128)(2,1)} async-done(((bf16[16,48,1536]{2,1,0:T(8,128)(2,1)}), bf16[16,48,1536]{2,1,0:T(8,128)(2,1)}, u32[]{:S(2)}, u32[]{:S(2)}) %all-to-all-start.8) | async-done | bytes 2359328 | tf_op jit(solution)/shard_map/all_to_all | solution.py:395
  750.2 13.2 %fusion.42 = f32[768,1,64]{0,2,1:T(8,128)} fusion(f32[768,768,3]{1,0,2:T(8,128)} %fusion.75, bf16[768,3,32]{0,2,1:T(8,128)(2,1)} %copy-done.27, bf16[768,3,32]{0,2,1:T(8,128)(2,1)S(1)} %copy-done.26, f32[3,768,768]{1,2,0:T(8,128)} %get-tuple-element.101, f32[3,768]{1,0:T(4,128)S(1)} %copy-done.65), kind=kOutput, calls=%fused_computation.67 | convolution fusion | flops 239471616 | bytes 14656512 | tf_op jit(solution)/shard_map/gqk,qgd->kd/dot_general | solution.py:626
  776.0 10.5 fusion.38
  789.3 6.1 all-to-all-done.12
  809.6 20.7 %all-to-all-done.9 = bf16[16,48,320]{2,1,0:T(8,128)(2,1)} async-done(((bf16[16,48,320]{2,1,0:T(8,128)(2,1)}), bf16[16,48,320]{2,1,0:T(8,128)(2,1)}, u32[]{:S(2)}, u32[]{:S(2)}) %all-to-all-start.9) | async-done | bytes 491552 | tf_op jit(solution)/shard_map/all_to_all | solution.py:395
  833.8 10.5 convolution_convert_fusion.2
  844.3 25.6 %all-to-all-done.11 = bf16[4,384,320]{1,2,0:T(8,128)(2,1)S(1)} async-done(((bf16[4,384,320]{1,2,0:T(8,128)(2,1)}), bf16[4,384,320]{1,2,0:T(8,128)(2,1)S(1)}, u32[]{:S(2)}, u32[]{:S(2)}) %all-to-all-start.11) | async-done | bytes 983072 | tf_op jit(solution)/shard_map/all_to_all | solution.py:399
  876.3 12.5 %copy.177 = bf16[4,384,4,2,320]{1,0,4,3,2:T(4,128)(2,1)} copy(bf16[4,384,4,2,320]{1,4,3,0,2:T(8,128)(2,1)} %bitcast.253) | data formatting | bytes 15728640 | tf_op jit(solution)/shard_map/transpose | solution.py:488
  888.8 7.8 copy.199
  896.6 83.9 %all-gather.3 = f32[32,96,32]{1,2,0:T(8,128)S(1)} all-gather(f32[1,96,32]{1,2,0:T(8,128)S(1)} %fusion.97), channel_id=1, replica_groups=mesh['dp'=2,'row'=4,'col'=4] {'dp','row','col'}, dimensions={0}, use_global_device_ids=true | all-gather | bytes 405504 | tf_op jit(solution)/shard_map/all_gather | solution.py:590
  1003.7 7.7 fusion.107
  1020.5 40.1 %psum.21 = f32[2,1536]{1,0:T(2,128)S(1)} all-reduce(f32[2,1536]{1,0:T(2,128)S(1)} %pad_maximum_fusion.9), channel_id=1, replica_groups=mesh['dp'=2,'row'=4,'col'=4] {'dp','row','col'}, use_global_device_ids=true, to_apply=%region_24.25 | all-reduce | flops 3072 | bytes 24576 | tf_op jit(solution)/shard_map/psum | solution.py:677
  (298 shorter events, 185.9 us)
Async XLA Ops:
  7.2 367.4 %copy-start = (bf16[1536,32]{0,1:T(8,128)(2,1)S(1)}, bf16[1536,32]{0,1:T(8,128)(2,1)}, u32[]{:S(2)}) copy-start(bf16[1536,32]{0,1:T(8,128)(2,1)} %param.22) | copy-start | bytes 294916
  12.2 40.2 %all-to-all-start.2 = ((bf16[4,384,320]{1,2,0:T(8,128)(2,1)}), bf16[4,384,320]{1,2,0:T(8,128)(2,1)S(1)}, u32[]{:S(2)}, u32[]{:S(2)}) async-start(bf16[4,384,320]{1,2,0:T(8,128)(2,1)} %gather_fusion.1), calls=%async_computation.2 | async-start | bytes 1966080 | tf_op jit(solution)/shard_map/all_to_all | solution.py:399
  18.5 156.8 %all-gather.13.cloned.1.call-start = ((), (), s32[]{:S(2)}) async-start(), calls=%async_computation.22 | async-start | bytes 5013504 | tf_op jit(solution)/shard_map/all_gather | solution.py:492
  54.1 76.6 %all-to-all-start.1 = ((bf16[16,192,384]{2,1,0:T(8,128)(2,1)}), bf16[16,192,384]{2,1,0:T(8,128)(2,1)S(1)}, u32[]{:S(2)}, u32[]{:S(2)}) async-start(bf16[16,192,384]{2,1,0:T(8,128)(2,1)} %bitcast.249), calls=%async_computation.1 | async-start | bytes 4718592 | tf_op jit(solution)/shard_map/all_to_all | solution.py:395
  130.8 23.9 %all-to-all-start = ((bf16[4,2,48,384]{3,2,1,0:T(8,128)(2,1)}), bf16[4,2,48,384]{3,2,1,0:T(8,128)(2,1)}, u32[]{:S(2)}, u32[]{:S(2)}) async-start(bf16[4,2,48,384]{3,2,1,0:T(8,128)(2,1)} %copy.155), calls=%async_computation | async-start | bytes 589824 | tf_op jit(solution)/shard_map/all_to_all | solution.py:399
  154.6 18.3 %all-to-all-start.3 = ((bf16[16,48,192]{2,1,0:T(8,128)(2,1)}), bf16[16,48,192]{2,1,0:T(8,128)(2,1)S(1)}, u32[]{:S(2)}, u32[]{:S(2)}) async-start(bf16[16,48,192]{2,1,0:T(8,128)(2,1)} %copy.163), calls=%async_computation.3 | async-start | bytes 786432 | tf_op jit(solution)/shard_map/all_to_all | solution.py:395
  160.0 214.6 %all-gather.9.cloned.1.call-start = ((), (), s32[]{:S(2)}) async-start(), calls=%async_computation.18 | async-start | bytes 9732096 | tf_op jit(solution)/shard_map/all_gather | solution.py:541
  189.3 238.7 %all-gather.11.cloned.1.call-start = ((), (), s32[]{:S(2)}) async-start(), calls=%async_computation.20 | async-start | bytes 9732096 | tf_op jit(solution)/shard_map/all_gather | solution.py:450
  252.7 129.3 %all-to-all-start.5 = ((bf16[16,96,512]{2,1,0:T(8,128)(2,1)}), bf16[16,96,512]{2,1,0:T(8,128)(2,1)}, u32[]{:S(2)}, u32[]{:S(2)}) async-start(bf16[16,96,512]{2,1,0:T(8,128)(2,1)} %param.24), calls=%async_computation.5 | async-start | bytes 3145728 | tf_op jit(solution)/shard_map/all_to_all | solution.py:395
  382.0 46.0 %all-to-all-start.6 = ((bf16[16,32,1536]{2,1,0:T(8,128)(2,1)}), bf16[16,32,1536]{2,1,0:T(8,128)(2,1)}, u32[]{:S(2)}, u32[]{:S(2)}) async-start(bf16[16,32,1536]{2,1,0:T(8,128)(2,1)} %param.25), calls=%async_computation.6 | async-start | bytes 3145728 | tf_op jit(solution)/shard_map/all_to_all | solution.py:395
  386.6 229.5 %reduce-scatter.5.cloned.1.call-start = ((), (), s32[]{:S(2)}) async-start(), calls=%async_computation.21 | async-start | bytes 9732096 | tf_op jit(solution)/shard_map/reduce_scatter | solution.py:596
  464.2 412.1 %all-gather.15.cloned.1.call-start = ((), (), s32[]{:S(2)}) async-start(), calls=%async_computation.23 | async-start | bytes 8355840 | tf_op jit(solution)/shard_map/all_gather | solution.py:486
  477.2 12.8 %all-to-all-start.7 = ((f32[32,1,96]{2,1,0:T(1,128)}), f32[32,1,96]{2,1,0:T(1,128)S(1)}, u32[]{:S(2)}, u32[]{:S(2)}) async-start(f32[32,1,96]{2,1,0:T(1,128)} %all_to_all.60), calls=%async_computation.9 | async-start | bytes 32768 | tf_op jit(solution)/shard_map/all_to_all | solution.py:580
  479.8 136.3 %copy-start.2 = (f32[96,1536]{1,0:T(8,128)S(1)}, f32[96,1536]{1,0:T(8,128)}, u32[]{:S(2)}) copy-start(f32[96,1536]{1,0:T(8,128)} %copy-done.1) | copy-start | bytes 1769476
  479.8 136.3 %copy-start.48 = (f32[96]{0:T(128)S(1)}, f32[96]{0:T(128)}, u32[]{:S(2)}) copy-start(f32[96]{0:T(128)} %copy-done.47) | copy-start | bytes 1156
  490.1 129.0 %copy-start.8 = (bf16[2,48,1536]{2,1,0:T(8,128)(2,1)S(1)}, bf16[2,48,1536]{2,1,0:T(8,128)(2,1)}, u32[]{:S(2)}) copy-start(bf16[2,48,1536]{2,1,0:T(8,128)(2,1)} %broadcast_multiply_fusion) | copy-start | bytes 884740
  490.1 132.4 %all-to-all-start.15 = ((bf16[16,32,1536]{2,1,0:T(8,128)(2,1)}), bf16[16,32,1536]{2,1,0:T(8,128)(2,1)}, u32[]{:S(2)}, u32[]{:S(2)}) async-start(bf16[16,32,1536]{2,1,0:T(8,128)(2,1)} %bitcast.271), calls=%async_computation.17 | async-start | bytes 3145728 | tf_op jit(solution)/shard_map/all_to_all | solution.py:395
  497.5 127.7 %copy-start.43 = (f32[96]{0:T(128)}, f32[96]{0:T(128)S(1)}, u32[]{:S(2)}) copy-start(f32[96]{0:T(128)S(1)} %get-tuple-element.106) | copy-start | bytes 1156
  497.5 127.6 %copy-start.50 = (f32[96]{0:T(128)}, f32[96]{0:T(128)S(1)}, u32[]{:S(2)}) copy-start(f32[96]{0:T(128)S(1)} %fusion.79) | copy-start | bytes 1156
  497.6 127.6 %copy-start.56 = (f32[96]{0:T(128)}, f32[96]{0:T(128)S(1)}, u32[]{:S(2)}) copy-start(f32[96]{0:T(128)S(1)} %multiply_reduce_fusion.6) | copy-start | bytes 1156
  625.2 102.9 %all-to-all-start.8 = ((bf16[16,48,1536]{2,1,0:T(8,128)(2,1)}), bf16[16,48,1536]{2,1,0:T(8,128)(2,1)}, u32[]{:S(2)}, u32[]{:S(2)}) async-start(bf16[16,48,1536]{2,1,0:T(8,128)(2,1)} %bitcast.250), calls=%async_computation.10 | async-start | bytes 4718592 | tf_op jit(solution)/shard_map/all_to_all | solution.py:395
  629.9 363.3 %reduce-scatter.3.cloned.1.call-start = ((), (), s32[]{:S(2)}) async-start(), calls=%async_computation.19 | async-start | bytes 9732096 | tf_op jit(solution)/shard_map/reduce_scatter | solution.py:594
  630.4 102.3 %copy-start.41 = (f32[4,192]{1,0:T(4,128)S(1)}, f32[4,192]{1,0:T(4,128)}, u32[]{:S(2)}) copy-start(f32[4,192]{1,0:T(4,128)} %copy-done.40) | copy-start | bytes 9220
  728.1 42.8 %all-to-all-start.14 = ((bf16[16,96,512]{2,1,0:T(8,128)(2,1)}), bf16[16,96,512]{2,1,0:T(8,128)(2,1)}, u32[]{:S(2)}, u32[]{:S(2)}) async-start(bf16[16,96,512]{2,1,0:T(8,128)(2,1)} %bitcast.270), calls=%async_computation.16 | async-start | bytes 3145728 | tf_op jit(solution)/shard_map/all_to_all | solution.py:395
  770.9 24.5 %all-to-all-start.12 = ((bf16[4,192,384]{2,1,0:T(8,128)(2,1)}), bf16[4,192,384]{2,1,0:T(8,128)(2,1)S(1)}, u32[]{:S(2)}, u32[]{:S(2)}) async-start(bf16[4,192,384]{2,1,0:T(8,128)(2,1)} %fusion.37), calls=%async_computation.14 | async-start | bytes 1179648 | tf_op jit(solution)/shard_map/all_to_all | solution.py:399
  795.4 34.9 %all-to-all-start.9 = ((bf16[16,48,320]{2,1,0:T(8,128)(2,1)}), bf16[16,48,320]{2,1,0:T(8,128)(2,1)}, u32[]{:S(2)}, u32[]{:S(2)}) async-start(bf16[16,48,320]{2,1,0:T(8,128)(2,1)} %pad_maximum_fusion), calls=%async_computation.11 | async-start | bytes 1179648 | tf_op jit(solution)/shard_map/all_to_all | solution.py:395
  830.3 39.6 %all-to-all-start.11 = ((bf16[4,384,320]{1,2,0:T(8,128)(2,1)}), bf16[4,384,320]{1,2,0:T(8,128)(2,1)S(1)}, u32[]{:S(2)}, u32[]{:S(2)}) async-start(bf16[4,384,320]{1,2,0:T(8,128)(2,1)} %convolution_convert_fusion.3), calls=%async_computation.13 | async-start | bytes 1966080 | tf_op jit(solution)/shard_map/all_to_all | solution.py:399
  870.9 129.2 %all-to-all-start.13 = ((bf16[16,96,512]{2,1,0:T(8,128)(2,1)}), bf16[16,96,512]{2,1,0:T(8,128)(2,1)S(1)}, u32[]{:S(2)}, u32[]{:S(2)}) async-start(bf16[16,96,512]{2,1,0:T(8,128)(2,1)} %bitcast.267), calls=%async_computation.15 | async-start | bytes 3145728 | tf_op jit(solution)/shard_map/all_to_all | solution.py:395
  874.6 187.5 %all-reduce.3.cloned.1.call-start = ((), (), s32[]{:S(2)}) async-start(), calls=%async_computation.24 | async-start | bytes 1572864 | tf_op jit(solution)/shard_map/psum | solution.py:83
  888.8 94.9 %copy-start.13 = (bf16[4,192,384]{2,1,0:T(8,128)(2,1)S(1)}, bf16[4,192,384]{2,1,0:T(8,128)(2,1)}, u32[]{:S(2)}) copy-start(bf16[4,192,384]{2,1,0:T(8,128)(2,1)} %copy-done.12) | copy-start | bytes 1769476
  896.6 90.8 %copy-start.5 = (f32[12,8,4,384]{3,1,2,0:T(8,128)S(1)}, f32[12,8,4,384]{3,1,2,0:T(8,128)}, u32[]{:S(2)}) copy-start(f32[12,8,4,384]{3,1,2,0:T(8,128)} %copy-done.4) | copy-start | bytes 1769476
  1000.1 61.1 %all-to-all-start.10 = ((f32[4,2,48,384]{3,2,1,0:T(8,128)}), f32[4,2,48,384]{3,2,1,0:T(8,128)S(1)}, u32[]{:S(2)}, u32[]{:S(2)}) async-start(f32[4,2,48,384]{3,2,1,0:T(8,128)} %bitcast.235), calls=%async_computation.12 | async-start | bytes 1179648 | tf_op jit(solution)/shard_map/all_to_all | solution.py:399
  (60 other events, 880.1 us)
Sparse Core Ops, SparseCore 0:
  21.7 93.2 all-gather.12
  189.5 120.6 all-gather.8
  313.0 92.8 all-gather.10
  464.4 151.6 reduce-scatter.4
  618.5 111.1 all-gather.14
  736.4 169.1 reduce-scatter.2
  1000.2 32.1 all-reduce.2

commit v2 on v1

--- a/solution.py
+++ b/solution.py
@@ -1,6 +1,10 @@
+import functools
+
 import jax
 import jax.numpy as jnp
 from jax import lax
+from jax.experimental import pallas as pl
+from jax.experimental.pallas import tpu as pltpu
 from jax.sharding import PartitionSpec as P
 
 D = 1536
@@ -395,8 +399,606 @@
     return lax.all_to_all(blocks, ("row", "col"), split_axis=0, concat_axis=0, tiled=True)
 
 
-def spread_cols(blocks):
-    return lax.all_to_all(blocks, "col", split_axis=0, concat_axis=0, tiled=True)
+MESH = pl.DeviceIdType.MESH
+ANYWHERE = pl.BlockSpec(memory_space=pl.ANY)
+
+
+def group_size_of(axes):
+    total = 1
+    for axis in axes:
+        total = total * lax.axis_size(axis)
+    return total
+
+
+def place_in(axes):
+    at = 0
+    for axis in axes:
+        at = at * lax.axis_size(axis) + lax.axis_index(axis)
+    return at
+
+
+def device_at(axes, index):
+    place = {}
+    for axis in reversed(axes):
+        place[axis] = index % lax.axis_size(axis)
+        index = index // lax.axis_size(axis)
+    return place
+
+
+def meet(peers):
+    barrier = pltpu.get_barrier_semaphore()
+    for peer in peers:
+        pl.semaphore_signal(barrier, inc=1, device_id=peer, device_id_type=MESH)
+    pl.semaphore_wait(barrier, len(peers))
+
+
+def send(src, dst, send_sem, recv_sem, peer):
+    copy = pltpu.make_async_remote_copy(
+        src_ref=src,
+        dst_ref=dst,
+        send_sem=send_sem,
+        recv_sem=recv_sem,
+        device_id=peer,
+        device_id_type=MESH,
+    )
+    copy.start()
+    return copy
+
+
+def trade_kernel(plans, *refs):
+    count = len(plans)
+    groups = [axes for axes, _ in plans]
+    sources, targets, sems = refs[:count], refs[count : 2 * count], refs[2 * count :]
+    widest = max(groups, key=len)
+    peers = []
+    for axes in (widest, *(g for g in groups if not set(g) <= set(widest))):
+        size = group_size_of(axes)
+        peers += [device_at(axes, (place_in(axes) + step) % size) for step in range(1, size)]
+    meet(peers)
+    copies, locals_ = [], []
+    for at, (axes, same) in enumerate(plans):
+        size, me = group_size_of(axes), place_in(axes)
+        own = pltpu.make_async_copy(
+            sources[at].at[0 if same else me], targets[at].at[me], sems[3 * at]
+        )
+        own.start()
+        locals_.append(own)
+        for step in range(1, size):
+            to = (me + step) % size
+            copies.append(
+                send(
+                    sources[at].at[0 if same else to],
+                    targets[at].at[me],
+                    sems[3 * at + 1].at[step],
+                    sems[3 * at + 2].at[step],
+                    device_at(axes, to),
+                )
+            )
+    for own in locals_:
+        own.wait()
+    for copy in copies:
+        copy.wait()
+
+
+def trade(number, *pairs):
+    arrays = [array for array, _ in pairs]
+    plans = [(axes, array.shape[0] == 1) for array, axes in pairs]
+    scratch, shapes = [], []
+    for array, axes in pairs:
+        shapes.append(jax.ShapeDtypeStruct((group_size_of(axes),) + array.shape[1:], array.dtype))
+        size = group_size_of(axes)
+        scratch += [
+            pltpu.SemaphoreType.DMA,
+            pltpu.SemaphoreType.DMA((size,)),
+            pltpu.SemaphoreType.DMA((size,)),
+        ]
+    return pl.pallas_call(
+        functools.partial(trade_kernel, plans),
+        out_shape=shapes,
+        in_specs=[ANYWHERE] * len(arrays),
+        out_specs=[ANYWHERE] * len(arrays),
+        scratch_shapes=scratch,
+        compiler_params=pltpu.CompilerParams(collective_id=number, has_side_effects=True),
+        name="trade" + str(number),
+    )(*arrays)
+
+
+def row_peers():
+    row = lax.axis_index("row")
+    rows = lax.axis_size("row")
+    across = (row + rows // 2) % rows
+    beside = row + 1 - 2 * (row % 2)
+    return row, across, beside
+
+
+def gather_plane_kernel(kinds, *refs):
+    count = len(kinds)
+    sources, targets, sems = refs[:count], refs[count : 2 * count], refs[2 * count :]
+    row, across, beside = row_peers()
+    col, cols = lax.axis_index("col"), lax.axis_size("col")
+    meet(
+        [{"col": (col + step) % cols} for step in range(1, cols)]
+        + [{"row": across}, {"row": beside}]
+    )
+
+    def pick(kind, at):
+        return {"micro": at // 2, "half": at % 2, "all": 0}[kind]
+
+    copies, locals_ = [], []
+    for at, (kind, rows_too) in enumerate(kinds):
+        source, target = sources[at], targets[at]
+        local_sem, send_sem, col_sem, across_sem, beside_sem = sems[5 * at : 5 * at + 5]
+        me = row * cols + col if rows_too else col
+        own = pltpu.make_async_copy(source.at[pick(kind, col)], target.at[me], local_sem)
+        own.start()
+        locals_.append(own)
+        for step in range(1, cols):
+            to = (col + step) % cols
+            copies.append(
+                send(
+                    source.at[pick(kind, to)],
+                    target.at[me],
+                    send_sem.at[step],
+                    col_sem.at[step],
+                    {"col": to},
+                )
+            )
+        if rows_too:
+            mine = source.at[pick(kind, col)]
+            copies.append(
+                send(mine, target.at[me], send_sem.at[4], across_sem.at[0], {"row": across})
+            )
+            copies.append(
+                send(mine, target.at[me], send_sem.at[5], beside_sem.at[0], {"row": beside})
+            )
+
+    def arrival(at, block, sem):
+        pltpu.make_async_copy(targets[at].at[block], targets[at].at[block], sem).wait()
+
+    for step in range(1, cols):
+        for at, (kind, rows_too) in enumerate(kinds):
+            _, send_sem, col_sem, across_sem, beside_sem = sems[5 * at : 5 * at + 5]
+            origin = (col + cols - step) % cols
+            block = row * cols + origin if rows_too else origin
+            arrival(at, block, col_sem.at[step])
+            if rows_too:
+                part = targets[at].at[block]
+                copies.append(
+                    send(part, part, send_sem.at[5 + step], across_sem.at[step], {"row": across})
+                )
+                copies.append(
+                    send(part, part, send_sem.at[8 + step], beside_sem.at[step], {"row": beside})
+                )
+    for step in range(cols):
+        for at, (kind, rows_too) in enumerate(kinds):
+            if not rows_too:
+                continue
+            _, send_sem, _, across_sem, beside_sem = sems[5 * at : 5 * at + 5]
+            block = across * cols + (col + cols - step) % cols
+            arrival(at, block, across_sem.at[step])
+            part = targets[at].at[block]
+            copies.append(
+                send(part, part, send_sem.at[12 + step], beside_sem.at[4 + step], {"row": beside})
+            )
+    for at, (kind, rows_too) in enumerate(kinds):
+        if rows_too:
+            for step in range(2 * cols):
+                side = beside if step < cols else (beside + 2) % lax.axis_size("row")
+                arrival(at, side * cols + (col + cols - step) % cols, sems[5 * at + 4].at[step])
+    for own in locals_:
+        own.wait()
+    for copy in copies:
+        copy.wait_send()
+
+
+def gather_plane(number, *items):
+    arrays = [array for array, _, _ in items]
+    kinds = [(kind, rows_too) for _, kind, rows_too in items]
+    cols, plane = lax.axis_size("col"), group_size_of(("row", "col"))
+    scratch, shapes = [], []
+    for array, kind, rows_too in items:
+        scratch += [
+            pltpu.SemaphoreType.DMA,
+            pltpu.SemaphoreType.DMA((16,)),
+            pltpu.SemaphoreType.DMA((cols,)),
+            pltpu.SemaphoreType.DMA((cols,)),
+            pltpu.SemaphoreType.DMA((2 * cols,)),
+        ]
+        shapes.append(
+            jax.ShapeDtypeStruct(
+                (plane if rows_too else cols,) + array.shape[1:], array.dtype
+            )
+        )
+    return pl.pallas_call(
+        functools.partial(gather_plane_kernel, kinds),
+        out_shape=shapes,
+        in_specs=[ANYWHERE] * len(arrays),
+        out_specs=[ANYWHERE] * len(arrays),
+        scratch_shapes=scratch,
+        compiler_params=pltpu.CompilerParams(collective_id=number, has_side_effects=True),
+        name="gather_plane" + str(number),
+    )(*arrays)
+
+
+def gather_all_kernel(source, target, local_sem, send_sem, col_sem, dp_sem, across_sem, beside_sem):
+    row, across, beside = row_peers()
+    rows, cols = lax.axis_size("row"), lax.axis_size("col")
+    col, dp = lax.axis_index("col"), lax.axis_index("dp")
+    other = 1 - dp
+    meet(
+        [{"col": (col + step) % cols} for step in range(1, cols)]
+        + [{"row": across}, {"row": beside}, {"dp": other}]
+    )
+    copies = []
+
+    def block_of(dp_from, row_from, step):
+        return (dp_from * rows + row_from) * cols + (col + cols - step) % cols
+
+    def arrival(block, sem):
+        pltpu.make_async_copy(target.at[block], target.at[block], sem).wait()
+
+    def pass_on(part, block, sem, peer):
+        copies.append(send(part, target.at[block], send_sem.at[len(copies)], sem, peer))
+
+    me = block_of(dp, row, 0)
+    own = pltpu.make_async_copy(source.at[0], target.at[me], local_sem)
+    own.start()
+    for step in range(1, cols):
+        pass_on(source.at[0], me, col_sem.at[step], {"col": (col + step) % cols})
+    for step in range(cols):
+        block = block_of(dp, row, step)
+        part = source.at[0] if step == 0 else target.at[block]
+        if step > 0:
+            arrival(block, col_sem.at[step])
+        pass_on(part, block, dp_sem.at[step], {"dp": other})
+        pass_on(part, block, across_sem.at[step], {"row": across})
+        pass_on(part, block, beside_sem.at[step], {"row": beside})
+    for step in range(cols):
+        block = block_of(other, row, step)
+        arrival(block, dp_sem.at[step])
+        if step < 2:
+            pass_on(target.at[block], block, across_sem.at[cols + step], {"row": across})
+        pass_on(target.at[block], block, beside_sem.at[cols + step], {"row": beside})
+        block = block_of(dp, across, step)
+        arrival(block, across_sem.at[step])
+        if step >= 2:
+            pass_on(target.at[block], block, dp_sem.at[cols + step], {"dp": other})
+        pass_on(target.at[block], block, beside_sem.at[2 * cols + step], {"row": beside})
+    for step in range(cols):
+        block = block_of(other, across, step)
+        arrival(block, (across_sem if step < 2 else dp_sem).at[cols + step])
+        pass_on(target.at[block], block, beside_sem.at[3 * cols + step], {"row": beside})
+    far = (beside + rows // 2) % rows
+    for turn, (dp_from, row_from) in enumerate(
+        ((dp, beside), (other, beside), (dp, far), (other, far))
+    ):
+        for step in range(cols):
+            arrival(block_of(dp_from, row_from, step), beside_sem.at[turn * cols + step])
+    own.wait()
+    for copy in copies:
+        copy.wait_send()
+
+
+def gather_all(number, array):
+    cols = lax.axis_size("col")
+    total = group_size_of(("dp", "row", "col"))
+    return pl.pallas_call(
+        gather_all_kernel,
+        out_shape=jax.ShapeDtypeStruct((total,) + array.shape, array.dtype),
+        in_specs=[ANYWHERE],
+        out_specs=ANYWHERE,
+        scratch_shapes=[
+            pltpu.SemaphoreType.DMA,
+            pltpu.SemaphoreType.DMA((40,)),
+            pltpu.SemaphoreType.DMA((cols,)),
+            pltpu.SemaphoreType.DMA((2 * cols,)),
+            pltpu.SemaphoreType.DMA((2 * cols,)),
+            pltpu.SemaphoreType.DMA((4 * cols,)),
+        ],
+        compiler_params=pltpu.CompilerParams(collective_id=number, has_side_effects=True),
+        name="gather_all" + str(number),
+    )(array[None])
+
+
+def sum_all_kernel(
+    partial,
+    scores,
+    total_out,
+    scores_out,
+    near,
+    passed,
+    stage,
+    last,
+    small_local,
+    small_send,
+    small_recv,
+    send_sem,
+    beside_sem,
+    first_sem,
+    second_sem,
+    col_sem,
+):
+    row, across, beside = row_peers()
+    rows, cols = lax.axis_size("row"), lax.axis_size("col")
+    col, dp = lax.axis_index("col"), lax.axis_index("dp")
+    other = 1 - dp
+    everyone = ("dp", "row", "col")
+    size, me = group_size_of(everyone), place_in(everyone)
+    meet([device_at(everyone, (me + step) % size) for step in range(1, size)])
+    copies = []
+
+    def pass_on(src, dst, sem, peer):
+        copies.append(send(src, dst, send_sem.at[len(copies)], sem, peer))
+
+    def arrival(ref, sem):
+        pltpu.make_async_copy(ref, ref, sem).wait()
+
+    def block_of(dp_to, row_to, col_to):
+        return (dp_to * rows + row_to) * cols + col_to
+
+    small_own = pltpu.make_async_copy(scores.at[me], scores_out.at[me], small_local)
+    small_own.start()
+    small = []
+    for step in range(1, size):
+        to = (me + step) % size
+        small.append(
+            send(
+                scores.at[to],
+                scores_out.at[me],
+                small_send.at[step],
+                small_recv.at[step],
+                device_at(everyone, to),
+            )
+        )
+    far = (beside + rows // 2) % rows
+    theirs = ((other, far), (other, beside), (dp, far), (dp, beside))
+    mine = ((other, across), (other, row), (dp, across), (dp, row))
+    for turn, (dp_to, row_to) in enumerate(theirs):
+        for z in range(cols):
+            at = turn * cols + z
+            pass_on(
+                partial.at[block_of(dp_to, row_to, z)], near.at[at], beside_sem.at[at], {"row": beside}
+            )
+
+    def chip_sum(turn, z):
+        dp_to, row_to = mine[turn]
+        at = turn * cols + z
+        arrival(near.at[at], beside_sem.at[at])
+        return partial[block_of(dp_to, row_to, z)].astype(jnp.float32) + near[at].astype(
+            jnp.float32
+        )
+
+    low = jnp.bfloat16
+    for z in range(cols):
+        passed[z] = chip_sum(0, z).astype(low)
+        peer = {"dp": other} if z < 2 else {"row": across}
+        pass_on(passed.at[z], stage.at[z], first_sem.at[z], peer)
+    for z in range(cols):
+        value = chip_sum(1, z)
+        if z >= 2:
+            arrival(stage.at[z], first_sem.at[z])
+            value = value + stage[z].astype(jnp.float32)
+        passed[cols + z] = value.astype(low)
+        pass_on(passed.at[cols + z], stage.at[cols + z], second_sem.at[z], {"dp": other})
+        value = chip_sum(2, z)
+        if z < 2:
+            arrival(stage.at[z], first_sem.at[z])
+            value = value + stage[z].astype(jnp.float32)
+        passed[2 * cols + z] = value.astype(low)
+        pass_on(
+            passed.at[2 * cols + z], stage.at[2 * cols + z], second_sem.at[cols + z], {"row": across}
+        )
+    for z in range(cols):
+        value = chip_sum(3, z)
+        arrival(stage.at[cols + z], second_sem.at[z])
+        arrival(stage.at[2 * cols + z], second_sem.at[cols + z])
+        passed[3 * cols + z] = (
+            value + stage[cols + z].astype(jnp.float32) + stage[2 * cols + z].astype(jnp.float32)
+        ).astype(low)
+    for step in range(1, cols):
+        to = (col + step) % cols
+        pass_on(passed.at[3 * cols + to], last.at[step], col_sem.at[step], {"col": to})
+    value = passed[3 * cols + col].astype(jnp.float32)
+    for step in range(1, cols):
+        arrival(last.at[step], col_sem.at[step])
+        value = value + last[step].astype(jnp.float32)
+    total_out[...] = value
+    small_own.wait()
+    for copy in small:
+        copy.wait()
+    for copy in copies:
+        copy.wait_send()
+
+
+def sum_all(number, partial, scores):
+    cols = lax.axis_size("col")
+    total = group_size_of(("dp", "row", "col"))
+    block = partial.shape[1:]
+    vmem = pl.BlockSpec(memory_space=pltpu.VMEM)
+    low = jnp.bfloat16
+    return pl.pallas_call(
+        sum_all_kernel,
+        out_shape=[
+            jax.ShapeDtypeStruct(block, jnp.float32),
+            jax.ShapeDtypeStruct(scores.shape, scores.dtype),
+        ],
+        in_specs=[vmem, vmem],
+        out_specs=[vmem, vmem],
+        scratch_shapes=[
+            pltpu.VMEM((4 * cols,) + block, low),
+            pltpu.VMEM((4 * cols,) + block, low),
+            pltpu.VMEM((3 * cols,) + block, low),
+            pltpu.VMEM((cols,) + block, low),
+            pltpu.SemaphoreType.DMA,
+            pltpu.SemaphoreType.DMA((total,)),
+            pltpu.SemaphoreType.DMA((total,)),
+            pltpu.SemaphoreType.DMA((48,)),
+            pltpu.SemaphoreType.DMA((4 * cols,)),
+            pltpu.SemaphoreType.DMA((cols,)),
+            pltpu.SemaphoreType.DMA((2 * cols,)),
+            pltpu.SemaphoreType.DMA((cols,)),
+        ],
+        compiler_params=pltpu.CompilerParams(
+            collective_id=number, has_side_effects=True, vmem_limit_bytes=48 * 2**20
+        ),
+        name="sum_all" + str(number),
+    )(partial, scores)
+
+
+def nt(left, right):
+    return lax.dot_general(
+        left, right, (((1,), (1,)), ((), ())), preferred_element_type=jnp.float32
+    )
+
+
+def tn(left, right):
+    return lax.dot_general(
+        left, right, (((0,), (0,)), ((), ())), preferred_element_type=jnp.float32
+    )
+
+
+def expert_kernel(
+    normed,
+    cot,
+    table,
+    rank,
+    mark,
+    router,
+    weights,
+    mix_out,
+    rows_out,
+    score_out,
+    grads_out,
+    kept_in,
+    kept_dye,
+    kept_act,
+    kept_gate,
+    kept_up,
+):
+    low = jnp.bfloat16
+    step = pl.program_id(0)
+    slots = kept_in.shape[1]
+    parts, _, ff_width = weights.shape
+    depth = normed.shape[1] // parts
+    down_depth = ff_width // parts
+
+    gate_w = weights[:, 0:depth, :].reshape(parts * depth, ff_width)
+    up_w = weights[:, depth : 2 * depth, :].reshape(parts * depth, ff_width)
+
+    def down_w(chunk):
+        at = 2 * depth + chunk * down_depth
+        return weights[:, at : at + down_depth, :].reshape(ff_width, ff_width)
+
+    chunks = normed.shape[1] // ff_width
+    tokens = normed[...]
+    cots = cot[...]
+    logits = jnp.where(
+        table[...] > 0, project(tokens, router[...]), -jnp.inf
+    )
+    top = jnp.max(logits, axis=1, keepdims=True)
+    raised = jnp.exp(logits - top)
+    gates = raised / jnp.sum(raised, axis=1, keepdims=True)
+    slot = lax.broadcasted_iota(jnp.int32, (slots, normed.shape[0]), 0)
+    picked = slot == rank[0, 0:1, :]
+    chosen = picked.astype(jnp.float32)
+    select = chosen.astype(low)
+    gate = jnp.sum(
+        jnp.dot(chosen, gates, precision=highest, preferred_element_type=jnp.float32) * mark[...],
+        axis=1,
+        keepdims=True,
+    )
+    expert_in = project(select, tokens).astype(low)
+    grad_mix = resid_scale * project(select, cots)
+    grad_out = (gate * grad_mix).astype(low)
+    gate_proj = project(expert_in, gate_w)
+    up_proj = project(expert_in, up_w)
+    sigmoid = 1.0 / (1.0 + jnp.exp(-gate_proj))
+    silu = gate_proj * sigmoid
+    act = (silu * up_proj).astype(low)
+    score = jnp.zeros((slots, 1), jnp.float32)
+    grad_act = jnp.zeros((slots, ff_width), jnp.float32)
+    for chunk in range(chunks):
+        lanes = slice(chunk * ff_width, (chunk + 1) * ff_width)
+        part = down_w(chunk)
+        out = project(act, part).astype(low).astype(jnp.float32)
+        score = score + jnp.sum(grad_mix[:, lanes] * out, axis=1, keepdims=True)
+        mix_out[:, lanes] = tn(select, (gate * out).astype(low)).astype(low)
+        grad_act = grad_act + nt(grad_out[:, lanes], part)
+    grad_gate = (grad_act * up_proj * (sigmoid + gate_proj * sigmoid * (1.0 - sigmoid))).astype(low)
+    grad_up = (grad_act * silu).astype(low)
+    grad_in = (nt(grad_gate, gate_w) + nt(grad_up, up_w)).astype(low)
+    rows_out[...] = tn(select, grad_in).astype(low)
+    score_row = jnp.sum(chosen * score, axis=0, keepdims=True)
+    score_out[0] = jnp.broadcast_to(score_row, score_out.shape[1:])
+    kept_in[step] = expert_in
+    kept_dye[step] = grad_out
+    kept_act[step] = act
+    kept_gate[step] = grad_gate
+    kept_up[step] = grad_up
+
+    @pl.when(step == pl.num_programs(0) - 1)
+    def _():
+        def all_of(kept):
+            return kept[...].reshape(kept.shape[0] * slots, kept.shape[2])
+
+        rows = all_of(kept_in)
+        for at, kept in ((0, kept_gate), (depth, kept_up)):
+            grad = tn(rows, all_of(kept)).astype(low)
+            grads_out[:, at : at + depth, :] = grad.reshape(parts, depth, ff_width)
+        act_all = all_of(kept_act)
+        for chunk in range(chunks):
+            lanes = slice(chunk * ff_width, (chunk + 1) * ff_width)
+            grad = tn(act_all, all_of(kept_dye.at[:, :, lanes])).astype(low)
+            at = 2 * depth + chunk * down_depth
+            grads_out[:, at : at + down_depth, :] = grad.reshape(parts, down_depth, ff_width)
+
+
+def expert_pass(normed, cot, table, rank, mark, router, weights, slots):
+    tiles, tile = rank.shape[0], rank.shape[2]
+    tokens, width = normed.shape
+    low = jnp.bfloat16
+    ff_width = weights.shape[2]
+    rows = pl.BlockSpec((tile, width), lambda i: (i, 0))
+    whole = lambda a: pl.BlockSpec(
+        a.shape, lambda i: (0,) * len(a.shape), pipeline_mode=pl.Buffered(1)
+    )
+    return pl.pallas_call(
+        expert_kernel,
+        grid=(tiles,),
+        out_shape=[
+            jax.ShapeDtypeStruct((tokens, width), low),
+            jax.ShapeDtypeStruct((tokens, width), low),
+            jax.ShapeDtypeStruct((tiles, 8, tile), jnp.float32),
+            jax.ShapeDtypeStruct(weights.shape, low),
+        ],
+        in_specs=[
+            rows,
+            rows,
+            pl.BlockSpec((tile, table.shape[1]), lambda i: (i, 0)),
+            pl.BlockSpec((1,) + rank.shape[1:], lambda i: (i, 0, 0)),
+            whole(mark),
+            whole(router),
+            whole(weights),
+        ],
+        out_specs=[
+            rows,
+            rows,
+            pl.BlockSpec((1, 8, tile), lambda i: (i, 0, 0)),
+            whole(weights),
+        ],
+        scratch_shapes=[
+            pltpu.VMEM((tiles, slots, width), low),
+            pltpu.VMEM((tiles, slots, width), low),
+            pltpu.VMEM((tiles, slots, ff_width), low),
+            pltpu.VMEM((tiles, slots, ff_width), low),
+            pltpu.VMEM((tiles, slots, ff_width), low),
+        ],
+        compiler_params=pltpu.CompilerParams(vmem_limit_bytes=56 * 2**20),
+        cost_estimate=pl.CostEstimate(
+            flops=22 * 10**9, bytes_accessed=50 * 10**6, transcendentals=10**6
+        ),
+        name="expert_pass",
+    )(normed, cot, table, rank, mark, router, weights)
 
 
 def owned(
@@ -442,35 +1044,8 @@
     micro_at = col_at // kv_here
     half_at = col_at % kv_here
 
-    gate_own = spread_plane(w_gate).reshape(model_width, ff_width)
-    up_own = spread_plane(w_up).reshape(model_width, ff_width)
-    down_own = spread_plane(w_down).reshape(ff_width, model_width)
-
     masked_cot = cotangent * mask[:, :, None].astype(cotangent.dtype)
-    cot_all = lax.all_gather(
-        masked_cot.reshape(own_rows, model_width), everyone, axis=0, tiled=True
-    )
-    routes_all = lax.all_gather(routes.reshape(own_rows, TOP), everyone, axis=0, tiled=True)
-
-    to_micro = jnp.arange(col_count) // kv_here
-    x_send = jnp.broadcast_to(
-        hidden_in[to_micro][None], (row_count, col_count, tok_row, width_part)
-    ).reshape(plane_count, tok_row, width_part)
-    x_micro = (
-        spread_plane(x_send)
-        .reshape(row_count, col_count, tok_row, width_part)
-        .transpose(0, 2, 1, 3)
-        .reshape(group_tokens, model_width)
-        .astype(jnp.float32)
-    )
-    x_own = (
-        spread_cols(
-            hidden_in.reshape(micro_count, col_count, quarter, width_part).transpose(1, 0, 2, 3)
-        )
-        .transpose(1, 2, 0, 3)
-        .reshape(own_rows, model_width)
-        .astype(jnp.float32)
-    )
+
     w_qkv = jnp.concatenate(
         [
             w_query.reshape(width_part, kv_here, q_width),
@@ -480,21 +1055,30 @@
         axis=2,
     ).transpose(1, 0, 2)
     qkv_width = q_width + 2 * HEAD_DIM
-    to_half = jnp.arange(col_count) % kv_here
-    w_mine = spread_cols(w_qkv[to_half]).reshape(model_width, qkv_width)
-    w_qkv_all = (
-        lax.all_gather(w_qkv, plane, axis=0, tiled=False)
-        .reshape(row_count, col_count, kv_here, width_part, qkv_width)
-        .transpose(1, 3, 0, 2, 4)
-        .reshape(model_width, row_count * kv_here * qkv_width)
-    )
+    x_blocks, w_mine, w_out_all = gather_plane(
+        0, (hidden_in, "micro", True), (w_qkv, "half", False), (w_out[None], "all", True)
+    )
+    weights = jnp.concatenate(
+        [w_gate, w_up]
+        + [w_down[:, :, at : at + ff_width] for at in range(0, model_width, ff_width)],
+        axis=1,
+    )
+    x_blocks, weights, masked_cot = lax.optimization_barrier((x_blocks, weights, masked_cot))
+    cot_all = lax.all_gather(
+        masked_cot.reshape(own_rows, model_width), everyone, axis=0, tiled=True
+    )
+    x_micro = (
+        x_blocks.reshape(row_count, col_count, tok_row, width_part)
+        .transpose(0, 2, 1, 3)
+        .reshape(group_tokens, model_width)
+        .astype(jnp.float32)
+    )
+    w_mine = w_mine.reshape(model_width, qkv_width)
     w_out_all = (
-        lax.all_gather(w_out, plane, axis=0, tiled=False)
-        .reshape(row_count, col_count, w_out.shape[0], w_out.shape[1])
+        w_out_all.reshape(row_count, col_count, w_out.shape[0], w_out.shape[1])
         .transpose(0, 2, 1, 3)
         .reshape(row_count * w_out.shape[0], model_width)
     )
-
     scale_m = lax.rsqrt(jnp.mean(x_micro * x_micro, axis=1, keepdims=True) + eps_norm)
     normed_m = (x_micro * scale_m * norm_gain).astype(jnp.bfloat16)
     qkv = project(normed_m, w_mine)
@@ -521,8 +1105,26 @@
         .astype(jnp.bfloat16)
     )
 
+    picks = jnp.pad(routes.reshape(own_rows, TOP).T, ((0, 0), (0, 128 - own_rows)))
+    attended_own, x_own, routes_all = trade(
+        1,
+        (attended.reshape(plane_count, quarter, q_width), plane),
+        (
+            hidden_in.reshape(micro_count, col_count, quarter, width_part).transpose(1, 0, 2, 3),
+            ("col",),
+        ),
+        (picks[None], everyone),
+    )
+    attended_own, weights = lax.optimization_barrier((attended_own, weights))
+    weights = spread_plane(weights)
+    x_own = (
+        x_own.transpose(1, 2, 0, 3).reshape(own_rows, model_width).astype(jnp.float32)
+    )
+    routes_all = (
+        routes_all[:, :, :own_rows].transpose(0, 2, 1).reshape(device_count * own_rows, TOP)
+    )
     attended_own = (
-        spread_plane(attended.reshape(plane_count, quarter, q_width))
+        attended_own
         .reshape(row_count, micro_count, kv_here, quarter, q_width)
         .transpose(1, 3, 0, 2, 4)
         .reshape(own_rows, row_count * kv_here * q_width)
@@ -538,48 +1140,46 @@
         logits = jnp.where(chosen, project(normed_rows, w_router), -jnp.inf)
         return jax.nn.softmax(logits, axis=-1)
 
-    normed_all = lax.all_gather(normed_two, everyone, axis=0, tiled=True)
-    gates_all = gating(normed_all, routes_all)
+    normed_all = gather_all(2, normed_two).reshape(device_count * own_rows, model_width)
+    normed_all, w_mine = lax.optimization_barrier((normed_all, w_mine))
+    neighbours = [(at, at + 1 - 2 * (at % 2)) for at in range(col_count)]
+    w_pair = jnp.stack([w_mine, lax.ppermute(w_mine, "col", neighbours)])
+    w_pair = jnp.where(half_at == 0, w_pair, w_pair[::-1])
+    w_qkv_all = (
+        lax.all_gather(w_pair, "row", axis=0, tiled=False)
+        .transpose(2, 0, 1, 3)
+        .reshape(model_width, row_count * kv_here * qkv_width)
+    )
     gates_own = gating(normed_two, routes.reshape(own_rows, TOP))
-    gate_mine = jnp.sum(
-        gates_all * (expert_ids == expert_at).astype(jnp.float32)[None, :], axis=1, keepdims=True
-    )
-
-    gate_proj = project(normed_all, gate_own)
-    up_proj = project(normed_all, up_own)
-    sigmoid_gate = jax.nn.sigmoid(gate_proj)
-    silu_gate = gate_proj * sigmoid_gate
-    activated = (silu_gate * up_proj).astype(jnp.bfloat16)
-    expert_out = project(activated, down_own).astype(jnp.bfloat16).astype(jnp.float32)
-    grad_mix = resid_scale * cot_all.astype(jnp.float32)
-    grad_gate_mine = jnp.sum(grad_mix * expert_out, axis=1)
-    mix_part = (gate_mine * expert_out).astype(jnp.bfloat16)
-    grad_out_rows = (gate_mine * grad_mix).astype(jnp.bfloat16)
-    grad_act = jnp.dot(grad_out_rows, down_own.T, preferred_element_type=jnp.float32)
-    grad_gate_p = (
-        grad_act * up_proj * (sigmoid_gate + gate_proj * sigmoid_gate * (1.0 - sigmoid_gate))
-    ).astype(jnp.bfloat16)
-    grad_up_p = (grad_act * silu_gate).astype(jnp.bfloat16)
-    grad_rows_part = (
-        jnp.dot(grad_gate_p, gate_own.T, preferred_element_type=jnp.float32)
-        + jnp.dot(grad_up_p, up_own.T, preferred_element_type=jnp.float32)
-    ).astype(jnp.bfloat16)
-    grad_down_own = jnp.dot(activated.T, grad_out_rows, preferred_element_type=jnp.float32)
-    grad_gate_own = jnp.dot(normed_all.T, grad_gate_p, preferred_element_type=jnp.float32)
-    grad_up_own = jnp.dot(normed_all.T, grad_up_p, preferred_element_type=jnp.float32)
-
-    def back_to_slices(grad, parts, depth):
-        return spread_plane(
-            grad.astype(jnp.bfloat16).reshape(parts, depth, grad.shape[1])
-        ).astype(jnp.float32)
-
-    out_gate = back_to_slices(grad_gate_own, experts_here, slice_width)
-    out_up = back_to_slices(grad_up_own, experts_here, slice_width)
-    out_down = back_to_slices(grad_down_own, experts_here, down_slice)
-
-    grad_gates = lax.all_to_all(
-        grad_gate_mine.reshape(device_count, own_rows), everyone, 0, 0, tiled=True
-    ).T
+
+    tile = col_count * own_rows
+    slots = col_count * micro_count * (quarter * 3 // 8)
+    table = jnp.any(routes_all[:, :, None] == expert_ids[None, None, :], axis=1)
+    here = jnp.any(routes_all == expert_at, axis=1).astype(jnp.int32).reshape(-1, tile)
+    rank = jnp.where(here > 0, jnp.cumsum(here, axis=1, dtype=jnp.int32) - 1, -1)
+    pad_experts = 128 - experts_all
+    mix_part, grad_rows_part, grad_gate_mine, grads = expert_pass(
+        normed_all,
+        cot_all,
+        jnp.pad(table.astype(jnp.float32), ((0, 0), (0, pad_experts))),
+        jnp.broadcast_to(rank[:, None, :], (rank.shape[0], 8, tile)),
+        (jnp.arange(128, dtype=jnp.int32) == expert_at).astype(jnp.float32)[None],
+        jnp.pad(w_router, ((0, 0), (0, pad_experts))),
+        weights,
+        slots,
+    )
+    grad_gate_mine = grad_gate_mine[:, 0, :].reshape(-1)
+    scores_send = jnp.broadcast_to(
+        jnp.pad(
+            grad_gate_mine.reshape(device_count, 1, own_rows),
+            ((0, 0), (0, 0), (0, 128 - own_rows)),
+        ),
+        (device_count, 8, 128),
+    )
+    grad_normed, grad_gates = sum_all(
+        3, grad_rows_part.reshape(device_count, own_rows, model_width), scores_send
+    )
+    grad_gates = grad_gates[:, 0, :own_rows].T
     chosen_own = jnp.any(
         routes.reshape(own_rows, TOP)[:, :, None] == expert_ids[None, None, :], axis=1
     )
@@ -587,15 +1187,9 @@
     grad_logits = gates_own * (
         grad_gates - jnp.sum(gates_own * grad_gates, axis=1, keepdims=True)
     )
-    grad_logits_all = lax.all_gather(grad_logits, everyone, axis=0, tiled=True)
-    router_grad = jnp.dot(
-        normed_all.astype(jnp.float32).T, grad_logits_all, precision=highest
-    )
     expert_mix = lax.psum_scatter(mix_part, everyone, scatter_dimension=0, tiled=True)
     layer_out = (mixed + resid_scale * expert_mix.astype(jnp.float32)).astype(jnp.bfloat16)
-    grad_normed = lax.psum_scatter(
-        grad_rows_part, everyone, scatter_dimension=0, tiled=True
-    ).astype(jnp.float32) + jnp.dot(
+    grad_normed = grad_normed + jnp.dot(
         grad_logits, w_router.astype(jnp.float32).T, precision=highest
     )
     mix_part_grad = jnp.sum(grad_normed * unit_two, axis=0)
@@ -605,11 +1199,41 @@
     )
     grad_branch = (resid_scale * grad_mixed).astype(jnp.bfloat16)
 
-    branch_send = jnp.broadcast_to(
-        grad_branch.reshape(micro_count, quarter, model_width)[to_micro][None],
-        (row_count, col_count, quarter, model_width),
-    ).reshape(plane_count, quarter, model_width)
-    branch_m = spread_plane(branch_send).reshape(group_tokens, model_width)
+    lines = lambda row: jnp.pad(row.reshape(-1, 128), ((0, 4), (0, 0)))[None]
+    branch_m, logits_plane, mix_parts = gather_plane(
+        4,
+        (grad_branch.reshape(micro_count, quarter, model_width), "micro", True),
+        (jnp.pad(grad_logits.T, ((0, 0), (0, 128 - own_rows)))[None], "all", True),
+        (lines(mix_part_grad), "all", True),
+    )
+    branch_m, grads = lax.optimization_barrier((branch_m, grads))
+    grads = spread_plane(grads)
+    out_gate = grads[:, :slice_width].astype(jnp.float32)
+    out_up = grads[:, slice_width : 2 * slice_width].astype(jnp.float32)
+    out_down = jnp.concatenate(
+        [
+            grads[:, at : at + down_slice]
+            for at in range(2 * slice_width, grads.shape[1], down_slice)
+        ],
+        axis=2,
+    ).astype(jnp.float32)
+    low = jnp.bfloat16
+    left = logits_plane[:, :, :own_rows].transpose(1, 0, 2).reshape(experts_all, -1)
+    parts = []
+    for _ in range(3):
+        parts.append(left.astype(low))
+        left = left - parts[-1].astype(jnp.float32)
+    normed_plane = lax.dynamic_slice_in_dim(
+        normed_all, dp_at * plane_count * own_rows, plane_count * own_rows
+    )
+    router_part = jnp.sum(
+        jnp.dot(
+            jnp.concatenate(parts, axis=0), normed_plane, preferred_element_type=jnp.float32
+        ).reshape(3, experts_all, model_width),
+        axis=0,
+    )
+    mix_part_grad = jnp.sum(mix_parts, axis=0)
+    branch_m = branch_m.reshape(group_tokens, model_width)
     w_out_mine = lax.dynamic_slice_in_dim(
         w_out_all, (row_at * kv_here + half_at) * q_width, q_width
     )
@@ -633,10 +1257,21 @@
         ],
         axis=1,
     ).astype(jnp.bfloat16)
-    qkv_part = jnp.dot(normed_m.T, grad_qkv, preferred_element_type=jnp.float32)
+    qkv_part = jnp.dot(grad_qkv.T, normed_m, preferred_element_type=jnp.float32)
+    grad_qkv_own, qkv_part, out_part = trade(
+        5,
+        (grad_qkv.reshape(plane_count, quarter, qkv_width), plane),
+        (
+            qkv_part.astype(low).reshape(qkv_width, col_count, width_part).transpose(1, 0, 2),
+            ("col",),
+        ),
+        (
+            out_part.astype(low).reshape(q_width, col_count, width_part).transpose(1, 0, 2),
+            ("col",),
+        ),
+    )
     grad_qkv_own = (
-        spread_plane(grad_qkv.reshape(plane_count, quarter, qkv_width))
-        .reshape(row_count, micro_count, kv_here, quarter, qkv_width)
+        grad_qkv_own.reshape(row_count, micro_count, kv_here, quarter, qkv_width)
         .transpose(1, 3, 0, 2, 4)
         .reshape(own_rows, row_count * kv_here * qkv_width)
     )
@@ -649,41 +1284,48 @@
         grad_scaled_one
         - unit_one * jnp.mean(grad_scaled_one * unit_one, axis=1, keepdims=True)
     )
+
+    def halves(part):
+        part = part.astype(jnp.float32)
+        return jnp.sum(part.reshape((micro_count, kv_here) + part.shape[1:]), axis=0).astype(low)
+
+    grad_input, qkv_sum, out_sum, router_grad, mix_grad, norm_grad = trade(
+        6,
+        (
+            grad_x.astype(low)
+            .reshape(micro_count, quarter, col_count, width_part)
+            .transpose(2, 0, 1, 3),
+            ("col",),
+        ),
+        (halves(qkv_part)[None], ("dp",)),
+        (halves(out_part)[None], ("dp",)),
+        (router_part[None], ("dp",)),
+        (mix_part_grad[None], ("dp",)),
+        (lines(norm_part), everyone),
+    )
     grad_input = (
-        spread_cols(
-            grad_x.reshape(micro_count, quarter, col_count, width_part).transpose(2, 0, 1, 3)
-        )
-        .transpose(1, 0, 2, 3)
+        grad_input.transpose(1, 0, 2, 3)
         .reshape(micro_count, tok_row, width_part)
-    )
-
-    def halves(part):
-        low_part = spread_cols(part.astype(jnp.bfloat16)).astype(jnp.float32)
-        return jnp.sum(
-            low_part.reshape((micro_count, kv_here) + part.shape[1:]), axis=0
-        ).astype(jnp.bfloat16)
-
-    qkv_sum = halves(qkv_part.reshape(col_count, width_part, qkv_width))
-    out_sum = halves(
-        out_part.reshape(q_width, col_count, width_part).transpose(1, 0, 2)
-    )
-    qkv_sum, out_sum = attn_total(
-        (qkv_sum.astype(jnp.float32), out_sum.astype(jnp.float32))
-    )
-    grad_wq = qkv_sum[:, :, :q_width].transpose(1, 0, 2).reshape(w_query.shape)
-    grad_wk = qkv_sum[:, :, q_width : q_width + HEAD_DIM].transpose(1, 0, 2).reshape(w_key.shape)
-    grad_wv = qkv_sum[:, :, q_width + HEAD_DIM :].transpose(1, 0, 2).reshape(w_value.shape)
+        .astype(jnp.float32)
+    )
+    qkv_sum = jnp.sum(qkv_sum.astype(jnp.float32), axis=0)
+    out_sum = jnp.sum(out_sum.astype(jnp.float32), axis=0)
+    router_grad = jnp.sum(router_grad, axis=0).T
+    mix_grad = jnp.sum(mix_grad, axis=0).reshape(-1)[:model_width]
+    norm_grad = jnp.sum(norm_grad, axis=0).reshape(-1)[:model_width]
+    grad_wq = qkv_sum[:, :q_width].reshape(-1, width_part).T
+    grad_wk = qkv_sum[:, q_width : q_width + HEAD_DIM].reshape(-1, width_part).T
+    grad_wv = qkv_sum[:, q_width + HEAD_DIM :].reshape(-1, width_part).T
     grad_wo = out_sum.reshape(w_out.shape)
-    gain_grads = lax.psum(jnp.stack([norm_part, mix_part_grad]), everyone)
     return (
         layer_out.reshape(micro_count, quarter, model_width),
         grad_input,
-        gain_grads[0],
+        norm_grad,
         grad_wq,
         grad_wk,
         grad_wv,
         grad_wo,
-        gain_grads[1],
+        mix_grad,
         router_grad,
         out_gate,
         out_up,
@@ -699,7 +1341,8 @@
         kv_here = w_key.shape[1] // HEAD_DIM
         one_each = w_gate.shape[0] == row_count * col_count
         pairs = hidden_in.shape[0] * kv_here == col_count
-        return (owned if one_each and pairs else shards)(*args)
+        sizes = (dp_count, row_count, col_count, kv_here) == (2, 4, 4, 2)
+        return (owned if sizes and one_each and pairs else shards)(*args)
 
     placed = (
         P(None, ("dp", "row"), "col"),

time: 1090 us -> 841 us (0.77)
  Pallas kernels: 0 us -> 526 us
  blocking collectives: 302 us -> 0 us
  waiting for transfers between devices: 395 us -> 123 us
  matrix products: 177 us -> 58.6 us
  starting transfers between devices: 68 us -> 16 us
  local copies, waits for them, and re-layouts: 85.6 us -> 55.1 us
    pallas_call x0 -> x8, Pallas kernels: none -> 526 us  [the longest x3 186 us: trade(): pl.pallas_call(functools.partial(trade_kernel, plans), out_shape=shapes,...]
    all_gather x2 -> x0, blocking collectives: 201 us -> none  [the longest x1 117 us: owned(): lax.all_gather(routes.reshape(own_rows, TOP), everyone, axis=0, tiled=True)]
    reduce_scatter x1 -> x0, waiting for transfers between devices: 118 us -> none  [owned(): lax.psum_scatter(grad_rows_part, everyone, scatter_dimension=0, tiled=True)]
    all_to_all x9 -> x2, waiting for transfers between devices: 211 us -> 99.7 us  [spread_plane(): lax.all_to_all(blocks, ('row', 'col'), split_axis=0, concat_axis=0, tiled...]
    dot_general x8 -> x2, matrix products: 78.7 us -> 6.59 us  [the longest x1 3.37 us: owned(): qkv_part = jnp.dot(grad_qkv.T, normed_m, preferred_element_type=jnp.float32)]
    all_to_all x6 -> x0, waiting for transfers between devices: 64.1 us -> none  [the longest x5 64.1 us: spread_cols(): lax.all_to_all(blocks, 'col', split_axis=0, concat_axis=0, tiled=True)]
    all_to_all x1 -> x0, blocking collectives: 61.5 us -> none  [spread_plane(): lax.all_to_all(blocks, ('row', 'col'), split_axis=0, concat_axis=0, tiled...]
    psum x1 -> x0, blocking collectives: 40.1 us -> none  [owned(): gain_grads = lax.psum(jnp.stack([norm_part, mix_part_grad]), everyone)]
  transfers between devices with their start and end apart: 22 -> 6, of which waited for: 10 -> 2; matrix products, arithmetic and copies ran while one was open for 21% -> 15% of each run, Pallas kernels for 0% -> 48%
where the time goes in v2:
time: 841 us; the launch traced here: 837 us
  Pallas kernels  526 us (63%)
  waiting for transfers between devices  123 us (15%)
  matrix products  58.6 us (7%)
  local copies, waits for them, and re-layouts  55.1 us (7%)
  other arithmetic  43.1 us (5%)
  starting transfers between devices  16 us (2%)
  between operations  15.1 us (2%)
    pallas_call x3, Pallas kernels, trade(): pl.pallas_call(functools.partial(trade_kernel, plans), out_shape=shapes,...  186 us
    pallas_call x2, Pallas kernels, gather_plane(): pl.pallas_call(functools.partial(gather_plane_kernel, kinds), out_shape=s...  132 us
    all_to_all x2, waiting for transfers between devices, spread_plane(): lax.all_to_all(blocks, ('row', 'col'), split_axis=0, concat_axis=0, tiled...  99.7 us
    pallas_call x1, Pallas kernels, sum_all(): pl.pallas_call(sum_all_kernel, out_shape=[jax.ShapeDtypeStruct(block, jnp...  87.5 us
    pallas_call x1, Pallas kernels, gather_all(): pl.pallas_call(gather_all_kernel, out_shape=jax.ShapeDtypeStruct((total,)...  63.6 us
    pallas_call x1, Pallas kernels, expert_pass(): pl.pallas_call(expert_kernel, grid=(tiles,), out_shape=[jax.ShapeDtypeStr...  56 us
    ppermute x1, waiting for transfers between devices, owned(): w_pair = jnp.stack([w_mine, lax.ppermute(w_mine, 'col', neighbours)])  23.5 us
    unnamed x122, local copies, waits for them, and re-layouts  22 us
  transfers between devices with their start and end apart: 6, of which 2 were waited for; matrix products, arithmetic and copies ran while one was open for 15% of the time, Pallas kernels for 48%

profile of v2, /device:TPU:0, one launch (start us, length us, event | category | flops | bytes accessed | tf_op | source)
XLA Modules:
  0.0 836.6 jit_solution(11029817831485572261)
XLA Ops:
  11.1 2.8 constant_dynamic-update-slice_fusion.1
  19.7 83.9 %gather_plane0.1 = (bf16[16,192,384]{2,1,0:T(8,128)(2,1)}, bf16[4,384,320]{2,1,0:T(8,128)(2,1)}, bf16[16,384,384]{2,1,0:T(8,128)(2,1)}) custom-call(bf16[2,192,384]{2,1,0:T(8,128)(2,1)} %refs_0_.1, bf16[2,384,320]{2,1,0:T(8,128)(2,1)} %maximum_bitcast_fusion.refs_1_, bf16[1,384,384]{2,1,0:T(8,128)(2,1)} %bitcast.314), custom_call_target="tpu_custom_call" | custom-call | tf_op jit(solution)/shard_map/gather_plane0/pallas_call | solution.py:612
  103.6 2.2 multiply_reduce_fusion
  105.9 2.2 bitcast_convert_fusion
  108.0 4.8 fusion.106
  113.7 2.3 fusion.112
  117.7 5.3 fusion.110
  123.1 3.9 fusion.26
  130.8 41.9 %trade1.1 = (bf16[16,48,192]{2,1,0:T(8,128)(2,1)}, bf16[4,2,48,384]{3,2,1,0:T(8,128)(2,1)}, s32[32,8,128]{2,1,0:T(8,128)}) custom-call(bf16[16,48,192]{2,1,0:T(8,128)(2,1)} %copy.125.refs_0_, bf16[4,2,48,384]{3,2,1,0:T(8,128)(2,1)} %bitcast.296, s32[1,8,128]{2,1,0:T(8,128)} %pad_bitcast_fusion.4.refs_2_), custom_call_target="tpu_custom_call" | custom-call | tf_op jit(solution)/shard_map/trade1/pallas_call | solution.py:495
  175.8 6.2 copy.128
  182.9 2.1 copy-done
  186.9 63.6 %gather_all2.1 = bf16[32,96,1536]{2,1,0:T(8,128)(2,1)} custom-call(bf16[1,96,1536]{2,1,0:T(8,128)(2,1)} %fusion.104.source), custom_call_target="tpu_custom_call" | custom-call | tf_op jit(solution)/shard_map/gather_all2/pallas_call | solution.py:685
  251.7 23.5 %collective-permute-done = bf16[1536,320]{0,1:T(8,128)(2,1)S(1)} collective-permute-done((bf16[1536,320]{0,1:T(8,128)(2,1)S(1)}, bf16[1536,320]{0,1:T(8,128)(2,1)S(1)}, u32[]{:S(2)}, u32[]{:S(2)}) %collective-permute-start) | collective-permute-done | bytes 983072 | tf_op jit(solution)/shard_map/ppermute | solution.py:1146
  277.1 9.6 %all-to-all-start = ((bf16[16,288,512]{2,1,0:T(8,128)(2,1)}), bf16[16,288,512]{2,1,0:T(8,128)(2,1)}, u32[]{:S(2)}, u32[]{:S(2)}) async-start(bf16[16,288,512]{2,1,0:T(8,128)(2,1)} %slice_dynamic-update-slice_fusion), calls=%async_computation | async-start | bytes 9437184 | tf_op jit(solution)/shard_map/all_to_all | solution.py:399
  292.8 99.7 %all-to-all-done.weights = bf16[16,288,512]{2,1,0:T(8,128)(2,1)} async-done(((bf16[16,288,512]{2,1,0:T(8,128)(2,1)}), bf16[16,288,512]{2,1,0:T(8,128)(2,1)}, u32[]{:S(2)}, u32[]{:S(2)}) %all-to-all-start) | async-done | bytes 4718624 | tf_op jit(solution)/shard_map/all_to_all | solution.py:399
  393.2 56.0 %expert_pass.1 = (bf16[3072,1536]{1,0:T(8,128)(2,1)}, bf16[3072,1536]{1,0:T(8,128)(2,1)}, f32[8,8,384]{2,1,0:T(8,128)}, bf16[16,288,512]{2,1,0:T(8,128)(2,1)}) custom-call(bf16[3072,1536]{1,0:T(8,128)(2,1)} %bitcast.258, bf16[3072,1536]{1,0:T(8,128)(2,1)} %all-gather.4.cloned.1.call-done.cot, f32[3072,128]{1,0:T(8,128)} %pad_convert_fusion.table, ...), custom_call_target="tpu_custom_call" | custom-call | flops 22000001024 | bytes 50000000 | tf_op jit(solution)/shard_map/expert_pass/pallas_call | solution.py:965
  451.3 87.5 %sum_all3.1 = (f32[96,1536]{1,0:T(8,128)S(1)}, f32[32,8,128]{2,1,0:T(8,128)S(1)}) custom-call(bf16[32,96,1536]{2,1,0:T(8,128)(2,1)} %bitcast.269, f32[32,8,128]{2,1,0:T(8,128)S(1)} %broadcast_in_dim.70.scores), custom_call_target="tpu_custom_call" | custom-call | tf_op jit(solution)/shard_map/sum_all3/pallas_call | solution.py:819
  541.7 48.5 %gather_plane4.1 = (bf16[16,48,1536]{2,1,0:T(8,128)(2,1)}, f32[16,32,128]{2,1,0:T(8,128)}, f32[16,16,128]{2,1,0:T(8,128)}) custom-call(bf16[2,48,1536]{2,1,0:T(8,128)(2,1)} %bitcast.297, f32[1,32,128]{2,1,0:T(8,128)} %pad_bitcast_fusion.refs_1_, f32[1,16,128]{2,1,0:T(8,128)} %pad_bitcast_fusion.3.refs_2_), custom_call_target="tpu_custom_call" | custom-call | tf_op jit(solution)/shard_map/gather_plane4/pallas_call | solution.py:612
  590.2 5.6 all-to-all-start.1
  597.3 4.8 copy.161
  602.1 2.7 convolution_convert_fusion.2
  604.8 4.2 fusion.33
  609.9 4.9 fusion.68
  614.8 10.6 %fusion.29 = f32[768,1,64]{0,2,1:T(8,128)S(1)} fusion(f32[768,768,3]{1,0,2:T(8,128)} %fusion.68, bf16[768,3,32]{0,2,1:T(8,128)(2,1)S(1)} %copy-done.26, bf16[768,3,32]{0,2,1:T(8,128)(2,1)S(1)} %copy-done.24, f32[3,768,768]{1,2,0:T(8,128)} %get-tuple-element.146, f32[3,768]{1,0:T(4,128)S(1)} %copy-done.52), kind=kOutput, calls=%fused_computation.49 | convolution fusion | flops 239471616 | bytes 14656512 | tf_op jit(solution)/shard_map/gqk,qgd->kd/dot_general | solution.py:1250
  627.3 10.8 %fusion.25 = f32[768,3,64]{0,2,1:T(8,128)S(1)} fusion(f32[768,768,3]{1,0,2:T(8,128)} %fusion.68, bf16[768,1,32]{0,2,1:T(8,128)(2,1)S(1)} %copy-done.34, bf16[768,1,32]{0,2,1:T(8,128)(2,1)S(1)} %copy-done.32, f32[3,768,768]{1,2,0:T(8,128)} %get-tuple-element.146, f32[3,768]{1,0:T(4,128)S(1)} %copy-done.52), kind=kOutput, calls=%fused_computation.45 | convolution fusion | flops 239078400 | bytes 14853120 | tf_op jit(solution)/shard_map/gqk,kd->qgd/dot_general | solution.py:1249
  640.9 3.4 convolution_convert_fusion
  647.9 103.8 %trade5.1 = (bf16[16,48,320]{2,1,0:T(8,128)(2,1)}, bf16[4,320,384]{2,1,0:T(8,128)(2,1)}, bf16[4,192,384]{2,1,0:T(8,128)(2,1)}) custom-call(bf16[16,48,320]{2,1,0:T(8,128)(2,1)} %pad_maximum_fusion.1.refs_0_, bf16[4,320,384]{2,1,0:T(8,128)(2,1)} %bitcast.273, bf16[4,192,384]{2,1,0:T(8,128)(2,1)} %bitcast.286), custom_call_target="tpu_custom_call" | custom-call | tf_op jit(solution)/shard_map/trade5/pallas_call | solution.py:495
  753.6 2.3 reduce.5
  759.2 3.2 fusion.8
  763.8 4.8 multiply_reduce_fusion.1
  772.8 5.4 slice_convert_fusion
  781.0 40.4 %trade6.1 = (bf16[4,2,48,384]{3,2,1,0:T(8,128)(2,1)}, bf16[2,2,320,384]{3,2,1,0:T(8,128)(2,1)}, bf16[2,2,192,384]{3,2,1,0:T(8,128)(2,1)}, f32[2,32,1536]{2,1,0:T...) custom-call(bf16[4,2,48,384]{3,2,1,0:T(8,128)(2,1)} %bitcast.292, bf16[1,2,320,384]{3,2,1,0:T(8,128)(2,1)} %bitcast.287, ...), custom_call_target="tpu_custom_call" | custom-call | tf_op jit(solution)/shard_map/trade6/pallas_call | solution.py:495
  (243 shorter events, 68.7 us)
Async XLA Ops:
  7.2 6.8 copy-start.3
  7.2 385.3 %all-gather.4.cloned.1.call-start = ((), (), s32[]{:S(2)}) async-start(), calls=%async_computation.3 | async-start | bytes 9732096 | tf_op jit(solution)/shard_map/all_gather | solution.py:1067
  11.1 6.7 copy-start.50
  11.1 6.7 copy-start.20
  14.0 89.7 %copy-start.27 = (f32[1536]{0:T(1024)S(1)}, f32[1536]{0:T(1024)}, u32[]{:S(2)}) copy-start(f32[1536]{0:T(1024)} %param.16) | copy-start | bytes 18436
  103.6 660.2 %all-gather.6.cloned.1.call-start = ((), (), s32[]{:S(2)}) async-start(), calls=%async_computation.5 | async-start | bytes 9830400 | tf_op jit(solution)/shard_map/all_gather | solution.py:1149
  105.9 7.0 copy-start.35
  116.3 6.8 copy-start.29
  116.7 6.3 copy-start.31
  123.1 6.4 copy-start.9
  123.1 7.1 copy-start.43
  127.0 45.7 %copy-start.5 = (bf16[64,3,768]{2,0,1:T(8,128)(2,1)}, bf16[64,3,768]{2,0,1:T(8,128)(2,1)S(1)}, u32[]{:S(2)}) copy-start(bf16[64,3,768]{2,0,1:T(8,128)(2,1)S(1)} %fusion.26) | copy-start | bytes 884740
  130.2 51.8 %copy-start.37 = (s32[96,8]{0,1:T(8,128)}, s32[96,8]{0,1:T(8,128)S(1)}, u32[]{:S(2)}) copy-start(s32[96,8]{0,1:T(8,128)S(1)} %reshape.542) | copy-start | bytes 9220
  186.0 64.4 %copy-start.40 = (f32[96]{0:T(128)}, f32[96]{0:T(128)S(1)}, u32[]{:S(2)}) copy-start(f32[96]{0:T(128)S(1)} %add_rsqrt_fusion.2) | copy-start | bytes 1156
  186.9 63.6 %copy-start.8 = (bf16[4,384,320]{2,1,0:T(8,128)(2,1)S(1)}, bf16[4,384,320]{2,1,0:T(8,128)(2,1)}, u32[]{:S(2)}) copy-start(bf16[4,384,320]{2,1,0:T(8,128)(2,1)} %get-tuple-element.47) | copy-start | bytes 2949124
  251.1 24.2 %collective-permute-start = (bf16[1536,320]{0,1:T(8,128)(2,1)S(1)}, bf16[1536,320]{0,1:T(8,128)(2,1)S(1)}, u32[]{:S(2)}, u32[]{:S(2)}) collective-permute-start(bf16[1536,320]{0,1:T(8,128)(2,1)S(1)} %copy.144), channel_id=1, source_target_pairs={{0,1},{1,0},{2,3},{3,2},{4,5},{5,4},{6,7},{7,6},{8,9},{9,8},{10,11... | collective-permute-start | bytes 2949128 | tf_op jit(solution)/shard_map/ppermute | solution.py:1146
  277.1 9.7 %copy-start.15 = (s32[32,8,128]{2,1,0:T(8,128)S(1)}, s32[32,8,128]{2,1,0:T(8,128)}, u32[]{:S(2)}) copy-start(s32[32,8,128]{2,1,0:T(8,128)} %get-tuple-element.55) | copy-start | bytes 393220
  277.1 12.8 %copy-start.11 = (bf16[1536,32]{0,1:T(8,128)(2,1)S(1)}, bf16[1536,32]{0,1:T(8,128)(2,1)}, u32[]{:S(2)}) copy-start(bf16[1536,32]{0,1:T(8,128)(2,1)} %param.22) | copy-start | bytes 294916
  277.1 115.4 %all-to-all-start = ((bf16[16,288,512]{2,1,0:T(8,128)(2,1)}), bf16[16,288,512]{2,1,0:T(8,128)(2,1)}, u32[]{:S(2)}, u32[]{:S(2)}) async-start(bf16[16,288,512]{2,1,0:T(8,128)(2,1)} %slice_dynamic-update-slice_fusion), calls=%async_computation | async-start | bytes 9437184 | tf_op jit(solution)/shard_map/all_to_all | solution.py:399
  286.7 491.5 %reduce-scatter.2.cloned.1.call-start = ((), (), s32[]{:S(2)}) async-start(), calls=%async_computation.4 | async-start | bytes 9732096 | tf_op jit(solution)/shard_map/reduce_scatter | solution.py:1190
  451.3 89.5 %copy-start.1 = (bf16[2,48,1536]{2,1,0:T(8,128)(2,1)S(1)}, bf16[2,48,1536]{2,1,0:T(8,128)(2,1)}, u32[]{:S(2)}) copy-start(bf16[2,48,1536]{2,1,0:T(8,128)(2,1)} %broadcast_multiply_fusion) | copy-start | bytes 884740
  540.8 49.4 %copy-start.47 = (f32[96]{0:T(128)}, f32[96]{0:T(128)S(1)}, u32[]{:S(2)}) copy-start(f32[96]{0:T(128)S(1)} %broadcast_multiply_fusion.2) | copy-start | bytes 1156
  590.2 6.3 copy-start.7
  590.2 178.9 %all-to-all-start.1 = ((bf16[16,288,512]{2,1,0:T(8,128)(2,1)}), bf16[16,288,512]{2,1,0:T(8,128)(2,1)}, u32[]{:S(2)}, u32[]{:S(2)}) async-start(bf16[16,288,512]{2,1,0:T(8,128)(2,1)} %get-tuple-element.77), calls=%async_computation.2 | async-start | bytes 9437184 | tf_op jit(solution)/shard_map/all_to_all | solution.py:399
  597.3 7.5 copy-start.52
  614.8 10.6 %copy-start.30 = (f32[768]{0:T(1024)S(1)}, f32[768]{0:T(1024)}, u32[]{:S(2)}) copy-start(f32[768]{0:T(1024)} %copy-done.29) | copy-start | bytes 9220
  614.8 10.6 %copy-start.45 = (f32[32]{0:T(128)S(1)}, f32[32]{0:T(128)}, u32[]{:S(2)}) copy-start(f32[32]{0:T(128)} %copy-done.44) | copy-start | bytes 388
  614.8 12.5 %copy-start.32 = (bf16[768,1,32]{0,2,1:T(8,128)(2,1)S(1)}, bf16[768,1,32]{0,2,1:T(8,128)(2,1)}, u32[]{:S(2)}) copy-start(bf16[768,1,32]{0,2,1:T(8,128)(2,1)} %copy-done.31) | copy-start | bytes 147460
  614.8 12.5 %copy-start.34 = (bf16[768,1,32]{0,2,1:T(8,128)(2,1)S(1)}, bf16[768,1,32]{0,2,1:T(8,128)(2,1)}, u32[]{:S(2)}) copy-start(bf16[768,1,32]{0,2,1:T(8,128)(2,1)} %copy-done.33) | copy-start | bytes 147460
  755.9 7.2 copy-start.28
  755.9 7.9 copy-start.46
  821.4 7.1 copy-start.18
  (27 other events, 100.1 us)
Sparse Core Ops, SparseCore 0:
  103.7 117.3 all-gather.3
  277.2 103.8 all-gather.5
  449.4 222.5 reduce-scatter.1

commit v3 on v2

--- a/solution.py
+++ b/solution.py
@@ -445,9 +445,46 @@
     return copy
 
 
+def trade_start(plans, sources, targets, sems):
+    copies, locals_, later = [], [], []
+
+    def ship(at, axes, same, step):
+        size, me = group_size_of(axes), place_in(axes)
+        to = (me + step) % size
+        copies.append(
+            send(
+                sources[at].at[0 if same else to],
+                targets[at].at[me],
+                sems[3 * at + 1].at[step],
+                sems[3 * at + 2].at[step],
+                device_at(axes, to),
+            )
+        )
+
+    for at, (axes, same, bulk) in enumerate(plans):
+        size, me = group_size_of(axes), place_in(axes)
+        own = pltpu.make_async_copy(
+            sources[at].at[0 if same else me], targets[at].at[me], sems[3 * at]
+        )
+        own.start()
+        locals_.append(own)
+        for step in range(1, size):
+            if bulk:
+                later.append((at, axes, same, step))
+            else:
+                ship(at, axes, same, step)
+
+    def more(count):
+        for item in later[:count]:
+            ship(*item)
+        del later[:count]
+
+    return locals_, copies, more
+
+
 def trade_kernel(plans, *refs):
     count = len(plans)
-    groups = [axes for axes, _ in plans]
+    groups = [axes for axes, _, _ in plans]
     sources, targets, sems = refs[:count], refs[count : 2 * count], refs[2 * count :]
     widest = max(groups, key=len)
     peers = []
@@ -455,43 +492,30 @@
         size = group_size_of(axes)
         peers += [device_at(axes, (place_in(axes) + step) % size) for step in range(1, size)]
     meet(peers)
-    copies, locals_ = [], []
-    for at, (axes, same) in enumerate(plans):
-        size, me = group_size_of(axes), place_in(axes)
-        own = pltpu.make_async_copy(
-            sources[at].at[0 if same else me], targets[at].at[me], sems[3 * at]
-        )
-        own.start()
-        locals_.append(own)
-        for step in range(1, size):
-            to = (me + step) % size
-            copies.append(
-                send(
-                    sources[at].at[0 if same else to],
-                    targets[at].at[me],
-                    sems[3 * at + 1].at[step],
-                    sems[3 * at + 2].at[step],
-                    device_at(axes, to),
-                )
-            )
+    locals_, copies, _ = trade_start(plans, sources, targets, sems)
     for own in locals_:
         own.wait()
     for copy in copies:
         copy.wait()
 
 
-def trade(number, *pairs):
-    arrays = [array for array, _ in pairs]
-    plans = [(axes, array.shape[0] == 1) for array, axes in pairs]
+def trade_shapes(pairs):
     scratch, shapes = [], []
     for array, axes in pairs:
-        shapes.append(jax.ShapeDtypeStruct((group_size_of(axes),) + array.shape[1:], array.dtype))
         size = group_size_of(axes)
+        shapes.append(jax.ShapeDtypeStruct((size,) + array.shape[1:], array.dtype))
         scratch += [
             pltpu.SemaphoreType.DMA,
             pltpu.SemaphoreType.DMA((size,)),
             pltpu.SemaphoreType.DMA((size,)),
         ]
+    return scratch, shapes
+
+
+def trade(number, *pairs):
+    arrays = [array for array, _ in pairs]
+    plans = [(axes, array.shape[0] == 1, False) for array, axes in pairs]
+    scratch, shapes = trade_shapes(pairs)
     return pl.pallas_call(
         functools.partial(trade_kernel, plans),
         out_shape=shapes,
@@ -620,16 +644,14 @@
     )(*arrays)
 
 
-def gather_all_kernel(source, target, local_sem, send_sem, col_sem, dp_sem, across_sem, beside_sem):
+def gather_line(source, target, sems, copies):
+    local_sem, send_sem, col_sem, dp_sem, across_sem, beside_sem = sems
     row, across, beside = row_peers()
     rows, cols = lax.axis_size("row"), lax.axis_size("col")
     col, dp = lax.axis_index("col"), lax.axis_index("dp")
     other = 1 - dp
-    meet(
-        [{"col": (col + step) % cols} for step in range(1, cols)]
-        + [{"row": across}, {"row": beside}, {"dp": other}]
-    )
-    copies = []
+    far = (beside + rows // 2) % rows
+    sent = []
 
     def block_of(dp_from, row_from, step):
         return (dp_from * rows + row_from) * cols + (col + cols - step) % cols
@@ -638,14 +660,19 @@
         pltpu.make_async_copy(target.at[block], target.at[block], sem).wait()
 
     def pass_on(part, block, sem, peer):
-        copies.append(send(part, target.at[block], send_sem.at[len(copies)], sem, peer))
+        copy = send(part, target.at[block], send_sem.at[len(sent)], sem, peer)
+        sent.append(copy)
+        copies.append(copy)
 
     me = block_of(dp, row, 0)
     own = pltpu.make_async_copy(source.at[0], target.at[me], local_sem)
-    own.start()
-    for step in range(1, cols):
-        pass_on(source.at[0], me, col_sem.at[step], {"col": (col + step) % cols})
-    for step in range(cols):
+
+    def begin():
+        own.start()
+        for step in range(1, cols):
+            pass_on(source.at[0], me, col_sem.at[step], {"col": (col + step) % cols})
+
+    def line(step):
         block = block_of(dp, row, step)
         part = source.at[0] if step == 0 else target.at[block]
         if step > 0:
@@ -653,7 +680,8 @@
         pass_on(part, block, dp_sem.at[step], {"dp": other})
         pass_on(part, block, across_sem.at[step], {"row": across})
         pass_on(part, block, beside_sem.at[step], {"row": beside})
-    for step in range(cols):
+
+    def side(step):
         block = block_of(other, row, step)
         arrival(block, dp_sem.at[step])
         if step < 2:
@@ -664,54 +692,398 @@
         if step >= 2:
             pass_on(target.at[block], block, dp_sem.at[cols + step], {"dp": other})
         pass_on(target.at[block], block, beside_sem.at[2 * cols + step], {"row": beside})
-    for step in range(cols):
+
+    def corner(step):
         block = block_of(other, across, step)
         arrival(block, (across_sem if step < 2 else dp_sem).at[cols + step])
         pass_on(target.at[block], block, beside_sem.at[3 * cols + step], {"row": beside})
+
+    def finish():
+        for turn, (dp_from, row_from) in enumerate(
+            ((dp, beside), (other, beside), (dp, far), (other, far))
+        ):
+            for step in range(cols):
+                arrival(block_of(dp_from, row_from, step), beside_sem.at[turn * cols + step])
+        own.wait()
+
+    return begin, line, side, corner, finish
+
+
+def gather_sems():
+    cols = lax.axis_size("col")
+    return [
+        pltpu.SemaphoreType.DMA,
+        pltpu.SemaphoreType.DMA((40,)),
+        pltpu.SemaphoreType.DMA((cols,)),
+        pltpu.SemaphoreType.DMA((2 * cols,)),
+        pltpu.SemaphoreType.DMA((2 * cols,)),
+        pltpu.SemaphoreType.DMA((4 * cols,)),
+    ]
+
+
+def nt(left, right):
+    return lax.dot_general(
+        left, right, (((1,), (1,)), ((), ())), preferred_element_type=jnp.float32
+    )
+
+
+def tn(left, right):
+    return lax.dot_general(
+        left, right, (((0,), (0,)), ((), ())), preferred_element_type=jnp.float32
+    )
+
+
+def norm_rows(x, gain):
+    scale = lax.rsqrt(jnp.mean(x * x, axis=1, keepdims=True) + eps_norm)
+    return scale, (x * scale * gain).astype(jnp.bfloat16)
+
+
+def turn(values, cos_table, sin_table):
+    lane = lax.broadcasted_iota(jnp.int32, values.shape, 1)
+    ahead = pltpu.roll(values, values.shape[1] - HEAD_DIM // 2, 1)
+    behind = pltpu.roll(values, HEAD_DIM // 2, 1)
+    return values * cos_table + jnp.where(lane % HEAD_DIM < HEAD_DIM // 2, ahead, behind) * sin_table
+
+
+def key_extent(block, rows, total):
+    return min(total, -(-(block + 1) * rows // 128) * 128)
+
+
+def visible(doc_col, doc_row, block, rows, extent):
+    query = block * rows + lax.broadcasted_iota(jnp.int32, (rows, extent), 0)
+    keys = lax.broadcasted_iota(jnp.int32, (rows, extent), 1)
+    same = doc_col[block * rows : (block + 1) * rows, 0:1] == doc_row[0:1, 0:extent]
+    return same & (keys <= query)
+
+
+def attend(query, key, allowed):
+    scores = jnp.where(allowed, nt(query, key) * attn_scale, -1e30)
+    raised = jnp.exp(scores - jnp.max(scores, axis=1, keepdims=True))
+    return raised / jnp.sum(raised, axis=1, keepdims=True)
+
+
+def front_kernel(
+    x,
+    w_qkv,
+    w_out,
+    picks,
+    cot,
+    weights,
+    gain_one,
+    gain_two,
+    cos_table,
+    sin_table,
+    doc_col,
+    doc_row,
+    x_all,
+    w_mine,
+    w_out_all,
+    picks_all,
+    cot_all,
+    normed_all,
+    weights_own,
+    qkv,
+    attended,
+    mixed,
+    x_own,
+    att_own,
+    normed_two,
+    local_sem,
+    send_sem,
+    x_sem,
+    q_sem,
+    o_sem,
+    own_sem,
+    att_send,
+    att_recv,
+    ship_local,
+    ship_send,
+    ship_recv,
+    *line_sems,
+):
+    row, across, beside = row_peers()
+    rows, cols = lax.axis_size("row"), lax.axis_size("col")
+    col, dp = lax.axis_index("col"), lax.axis_index("dp")
+    other = 1 - dp
     far = (beside + rows // 2) % rows
-    for turn, (dp_from, row_from) in enumerate(
-        ((dp, beside), (other, beside), (dp, far), (other, far))
-    ):
+    plane = ("row", "col")
+    size, me = group_size_of(plane), place_in(plane)
+    low = jnp.bfloat16
+    meet(
+        [device_at(plane, (me + step) % size) for step in range(1, size)] + [{"dp": other}]
+    )
+    copies, locals_, sent, moved = [], [], [], []
+    picks_line = gather_line(picks, picks_all, line_sems[0:6], copies)
+    cot_line = gather_line(cot, cot_all, line_sems[6:12], copies)
+    norm_line = gather_line(normed_two, normed_all, line_sems[12:18], copies)
+
+    def pass_on(src, dst, sem, peer):
+        sent.append(send(src, dst, send_sem.at[len(sent)], sem, peer))
+
+    def arrival(ref, sem):
+        pltpu.make_async_copy(ref, ref, sem).wait()
+
+    def local(src, dst):
+        copy = pltpu.make_async_copy(src, dst, local_sem.at[len(locals_)])
+        copy.start()
+        locals_.append(copy)
+
+    def ship(first, last):
+        for step in range(first, last):
+            to = (me + step) % size
+            moved.append(
+                send(
+                    weights.at[to],
+                    weights_own.at[me],
+                    ship_send.at[step],
+                    ship_recv.at[step],
+                    device_at(plane, to),
+                )
+            )
+
+    def origin(step):
+        return (col + cols - step) % cols
+
+    micro, depth, width = x.shape
+    quarter = depth // cols
+    half_depth = w_out.shape[1]
+
+    def lanes(step):
+        return pl.ds(pl.multiple_of(origin(step) * width, width), width)
+
+    def x_at(row_from, step):
+        return x_all.at[pl.ds(pl.multiple_of(row_from * depth, depth), depth), lanes(step)]
+
+    def out_at(row_from, step, half):
+        first = pl.multiple_of((row_from * 2 + half) * half_depth, half_depth)
+        return w_out_all.at[pl.ds(first, half_depth), lanes(step)]
+
+    def own_at(m, step):
+        return x_own.at[pl.ds(m * quarter, quarter), lanes(step)]
+
+    my_x = x_at(row, 0)
+    for step in range(1, cols):
+        to = (col + step) % cols
+        pass_on(x.at[to // 2], my_x, x_sem.at[step], {"col": to})
+        pass_on(w_qkv.at[to % 2, dp], w_mine.at[col, dp], q_sem.at[step], {"col": to})
+    local(x.at[col // 2], my_x)
+    local(w_qkv.at[col % 2], w_mine.at[col])
+    for half in range(2):
+        local(w_out.at[half], out_at(row, 0, half))
+    pass_on(x.at[col // 2], my_x, x_sem.at[cols], {"row": across})
+    pass_on(x.at[col // 2], my_x, x_sem.at[2 * cols], {"row": beside})
+    for step in range(1, cols):
+        to = (col + step) % cols
+        pass_on(w_out.at[dp], out_at(row, 0, dp), o_sem.at[step], {"col": to})
+        first = pl.multiple_of(to * quarter, quarter)
+        for m in range(micro):
+            pass_on(
+                x.at[m, pl.ds(first, quarter)],
+                own_at(m, 0),
+                own_sem.at[m * cols + step],
+                {"col": to},
+            )
+    for m in range(micro):
+        local(x.at[m, pl.ds(pl.multiple_of(col * quarter, quarter), quarter)], own_at(m, 0))
+    for half in range(2):
+        pass_on(w_out.at[half], out_at(row, 0, half), o_sem.at[(2 + half) * cols], {"row": across})
+        pass_on(w_out.at[half], out_at(row, 0, half), o_sem.at[(4 + half) * cols], {"row": beside})
+    for step in range(1, cols):
+        part = x_at(row, step)
+        arrival(part, x_sem.at[step])
+        pass_on(part, part, x_sem.at[cols + step], {"row": across})
+        pass_on(part, part, x_sem.at[2 * cols + step], {"row": beside})
+        part = w_mine.at[origin(step), dp]
+        arrival(part, q_sem.at[step])
+        pass_on(part, part, q_sem.at[cols + step], {"dp": other})
+    for step in range(cols):
+        part = x_at(across, step)
+        arrival(part, x_sem.at[cols + step])
+        pass_on(part, part, x_sem.at[3 * cols + step], {"row": beside})
+    for step in range(1, cols):
+        part = out_at(row, step, dp)
+        arrival(part, o_sem.at[step])
+        pass_on(part, part, o_sem.at[cols + step], {"dp": other})
+        pass_on(part, part, o_sem.at[2 * cols + step], {"row": across})
+        pass_on(part, part, o_sem.at[4 * cols + step], {"row": beside})
+    picks_line[0]()
+    cot_line[0]()
+    own = pltpu.make_async_copy(weights.at[me], weights_own.at[me], ship_local)
+    own.start()
+    for step in range(1, cols):
+        arrival(w_mine.at[origin(step), other], q_sem.at[cols + step])
+    for at, row_from in enumerate((beside, far)):
         for step in range(cols):
-            arrival(block_of(dp_from, row_from, step), beside_sem.at[turn * cols + step])
+            arrival(x_at(row_from, step), x_sem.at[(2 + at) * cols + step])
+    for copy in locals_:
+        copy.wait()
+
+    tokens, model_width = x_all.shape
+    projection = w_mine[...].reshape(model_width, w_mine.shape[3])
+    for block in range(rows):
+        part = slice(block * depth, (block + 1) * depth)
+        _, normed = norm_rows(x_all[part, :].astype(jnp.float32), gain_one[...])
+        values = project(normed, projection)
+        cosine, sine = cos_table[part, :], sin_table[part, :]
+        for at in range(2):
+            piece = slice(at * 128, (at + 1) * 128)
+            qkv[part, piece] = turn(values[:, piece], cosine, sine).astype(low)
+        qkv[part, 256:] = values[:, 256:].astype(low)
+    heads = attended.shape[2] // HEAD_DIM
+    kv_at = heads * HEAD_DIM
+    for block in range(rows):
+        extent = key_extent(block, depth, tokens)
+        allowed = visible(doc_col, doc_row, block, depth, extent)
+        key = qkv[0:extent, kv_at : kv_at + HEAD_DIM]
+        value = qkv[0:extent, kv_at + HEAD_DIM : kv_at + 2 * HEAD_DIM]
+        outs = []
+        for head in range(heads):
+            query = qkv[
+                block * depth : (block + 1) * depth, head * HEAD_DIM : (head + 1) * HEAD_DIM
+            ]
+            outs.append(project(attend(query, key, allowed).astype(low), value))
+        out = jnp.concatenate(outs, axis=1).astype(low)
+        attended[block * cols : (block + 1) * cols] = out.reshape(cols, quarter, out.shape[1])
+    for step in range(1, size):
+        to = (me + step) % size
+        moved.append(
+            send(
+                attended.at[to],
+                att_own.at[me],
+                att_send.at[step],
+                att_recv.at[step],
+                device_at(plane, to),
+            )
+        )
+    stay = pltpu.make_async_copy(attended.at[me], att_own.at[me], att_send.at[0])
+    stay.start()
+    ship(1, 5)
+    for step in range(cols):
+        picks_line[1](step)
+        cot_line[1](step)
+    for step in range(1, cols):
+        part = out_at(row, step, other)
+        arrival(part, o_sem.at[cols + step])
+        pass_on(part, part, o_sem.at[3 * cols + step], {"row": across})
+        pass_on(part, part, o_sem.at[5 * cols + step], {"row": beside})
+    for at in range(2):
+        for step in range(cols):
+            half = at if step == 0 else (dp if at == 0 else other)
+            part = out_at(across, step, half)
+            arrival(part, o_sem.at[(2 + at) * cols + step])
+            pass_on(part, part, o_sem.at[(6 + at) * cols + step], {"row": beside})
+    for at, row_from in enumerate((beside, far)):
+        for step in range(cols):
+            for part in range(2):
+                half = part if step == 0 else (dp if part == 0 else other)
+                arrival(out_at(row_from, step, half), o_sem.at[(4 + 2 * at + part) * cols + step])
+    for step in range(1, cols):
+        for m in range(micro):
+            arrival(own_at(m, step), own_sem.at[m * cols + step])
+    stay.wait()
+    for step in range(1, size):
+        arrival(att_own.at[(me + size - step) % size], att_recv.at[step])
+    pairs = cols // micro
+    for m in range(micro):
+        total = jnp.zeros((quarter, model_width), jnp.float32)
+        for row_from in range(rows):
+            for pair in range(pairs):
+                first = (row_from * pairs + pair) * kv_at
+                total = total + project(
+                    att_own[row_from * cols + m * pairs + pair],
+                    w_out_all[first : first + kv_at, :],
+                )
+        part = slice(m * quarter, (m + 1) * quarter)
+        value = x_own[part, :].astype(jnp.float32) + resid_scale * total
+        mixed[part, :] = value
+        normed_two[0, part, :] = norm_rows(value, gain_two[...])[1]
+
+    begin, line, side, corner, finish = norm_line
+    begin()
+    for step in range(cols):
+        picks_line[2](step)
+        cot_line[2](step)
+        ship(5 + 2 * step, 7 + 2 * step)
+    for step in range(cols):
+        line(step)
+    ship(5 + 2 * cols, size)
+    for step in range(cols):
+        picks_line[3](step)
+        cot_line[3](step)
+        side(step)
+    for step in range(cols):
+        corner(step)
+    picks_line[4]()
+    cot_line[4]()
+    finish()
     own.wait()
-    for copy in copies:
+    for copy in moved[: size - 1]:
         copy.wait_send()
-
-
-def gather_all(number, array):
-    cols = lax.axis_size("col")
-    total = group_size_of(("dp", "row", "col"))
+    for copy in moved[size - 1 :]:
+        copy.wait()
+    for copy in copies + sent:
+        copy.wait_send()
+
+
+def front(number, x, w_qkv, w_out, picks, cot, weights, gains, tables, docs, heads_width):
+    cols, rows = lax.axis_size("col"), lax.axis_size("row")
+    total, plane = group_size_of(("dp", "row", "col")), group_size_of(("row", "col"))
+    micro, depth, part_width = x.shape
+    width, tokens, low = part_width * cols, depth * rows, jnp.bfloat16
+    quarter = depth // cols
+    vmem = pl.BlockSpec(memory_space=pltpu.VMEM)
+    shape = jax.ShapeDtypeStruct
     return pl.pallas_call(
-        gather_all_kernel,
-        out_shape=jax.ShapeDtypeStruct((total,) + array.shape, array.dtype),
-        in_specs=[ANYWHERE],
-        out_specs=ANYWHERE,
+        front_kernel,
+        out_shape=[
+            shape((tokens, width), low),
+            shape((cols,) + w_qkv.shape[1:], low),
+            shape((rows * 2 * w_out.shape[1], width), low),
+            shape((total,) + picks.shape, picks.dtype),
+            shape((total,) + cot.shape, low),
+            shape((total,) + cot.shape, low),
+            shape(weights.shape, low),
+            shape((tokens, w_qkv.shape[3]), low),
+            shape((plane, quarter, heads_width), low),
+            shape((micro * quarter, width), jnp.float32),
+        ],
+        in_specs=[ANYWHERE] * 6 + [vmem] * 6,
+        out_specs=[vmem] * 3 + [ANYWHERE] * 4 + [vmem] * 3,
         scratch_shapes=[
+            pltpu.VMEM((micro * quarter, width), low),
+            pltpu.VMEM((plane, quarter, heads_width), low),
+            pltpu.VMEM((1, micro * quarter, width), low),
+            pltpu.SemaphoreType.DMA((8,)),
+            pltpu.SemaphoreType.DMA((72,)),
+            pltpu.SemaphoreType.DMA((4 * cols,)),
+            pltpu.SemaphoreType.DMA((2 * cols,)),
+            pltpu.SemaphoreType.DMA((8 * cols,)),
+            pltpu.SemaphoreType.DMA((micro * cols,)),
+            pltpu.SemaphoreType.DMA((plane,)),
+            pltpu.SemaphoreType.DMA((plane,)),
             pltpu.SemaphoreType.DMA,
-            pltpu.SemaphoreType.DMA((40,)),
-            pltpu.SemaphoreType.DMA((cols,)),
-            pltpu.SemaphoreType.DMA((2 * cols,)),
-            pltpu.SemaphoreType.DMA((2 * cols,)),
-            pltpu.SemaphoreType.DMA((4 * cols,)),
-        ],
-        compiler_params=pltpu.CompilerParams(collective_id=number, has_side_effects=True),
-        name="gather_all" + str(number),
-    )(array[None])
-
-
-def sum_all_kernel(
+            pltpu.SemaphoreType.DMA((plane,)),
+            pltpu.SemaphoreType.DMA((plane,)),
+        ]
+        + gather_sems() * 3,
+        compiler_params=pltpu.CompilerParams(
+            collective_id=number, has_side_effects=True, vmem_limit_bytes=56 * 2**20
+        ),
+        name="front" + str(number),
+    )(x, w_qkv, w_out, picks[None], cot[None], weights, *gains, *tables, *docs)
+
+
+def sum_body(
+    more,
+    between,
     partial,
-    scores,
     total_out,
-    scores_out,
     near,
+    mine,
     passed,
     stage,
     last,
-    small_local,
-    small_send,
-    small_recv,
+    local_sem,
     send_sem,
     beside_sem,
     first_sem,
@@ -722,10 +1094,7 @@
     rows, cols = lax.axis_size("row"), lax.axis_size("col")
     col, dp = lax.axis_index("col"), lax.axis_index("dp")
     other = 1 - dp
-    everyone = ("dp", "row", "col")
-    size, me = group_size_of(everyone), place_in(everyone)
-    meet([device_at(everyone, (me + step) % size) for step in range(1, size)])
-    copies = []
+    copies, loads = [], []
 
     def pass_on(src, dst, sem, peer):
         copies.append(send(src, dst, send_sem.at[len(copies)], sem, peer))
@@ -736,43 +1105,39 @@
     def block_of(dp_to, row_to, col_to):
         return (dp_to * rows + row_to) * cols + col_to
 
-    small_own = pltpu.make_async_copy(scores.at[me], scores_out.at[me], small_local)
-    small_own.start()
-    small = []
-    for step in range(1, size):
-        to = (me + step) % size
-        small.append(
-            send(
-                scores.at[to],
-                scores_out.at[me],
-                small_send.at[step],
-                small_recv.at[step],
-                device_at(everyone, to),
-            )
-        )
     far = (beside + rows // 2) % rows
     theirs = ((other, far), (other, beside), (dp, far), (dp, beside))
-    mine = ((other, across), (other, row), (dp, across), (dp, row))
+    ours = ((other, across), (other, row), (dp, across), (dp, row))
     for turn, (dp_to, row_to) in enumerate(theirs):
         for z in range(cols):
             at = turn * cols + z
             pass_on(
-                partial.at[block_of(dp_to, row_to, z)], near.at[at], beside_sem.at[at], {"row": beside}
+                partial.at[block_of(dp_to, row_to, z)],
+                near.at[at],
+                beside_sem.at[at],
+                {"row": beside},
             )
+            load = pltpu.make_async_copy(
+                partial.at[block_of(*ours[turn], z)], mine.at[at], local_sem.at[at]
+            )
+            load.start()
+            loads.append(load)
 
     def chip_sum(turn, z):
-        dp_to, row_to = mine[turn]
         at = turn * cols + z
+        loads[at].wait()
         arrival(near.at[at], beside_sem.at[at])
-        return partial[block_of(dp_to, row_to, z)].astype(jnp.float32) + near[at].astype(
-            jnp.float32
-        )
+        return mine[at].astype(jnp.float32) + near[at].astype(jnp.float32)
 
     low = jnp.bfloat16
+    more(5)
     for z in range(cols):
         passed[z] = chip_sum(0, z).astype(low)
         peer = {"dp": other} if z < 2 else {"row": across}
         pass_on(passed.at[z], stage.at[z], first_sem.at[z], peer)
+    more(5)
+    if between:
+        between[0]()
     for z in range(cols):
         value = chip_sum(1, z)
         if z >= 2:
@@ -786,75 +1151,177 @@
             value = value + stage[z].astype(jnp.float32)
         passed[2 * cols + z] = value.astype(low)
         pass_on(
-            passed.at[2 * cols + z], stage.at[2 * cols + z], second_sem.at[cols + z], {"row": across}
-        )
-    for z in range(cols):
-        value = chip_sum(3, z)
+            passed.at[2 * cols + z],
+            stage.at[2 * cols + z],
+            second_sem.at[cols + z],
+            {"row": across},
+        )
+    more(99)
+    if between:
+        between[1]()
+    for step in range(cols - 1, -1, -1):
+        z = (col + step) % cols
+        at = 3 * cols + z
+        pltpu.make_async_copy(mine.at[at], mine.at[at], local_sem.at[at]).wait()
+        arrival(near.at[at], beside_sem.at[at])
+        value = mine[at].astype(jnp.float32) + near[at].astype(jnp.float32)
         arrival(stage.at[cols + z], second_sem.at[z])
         arrival(stage.at[2 * cols + z], second_sem.at[cols + z])
-        passed[3 * cols + z] = (
+        value = (
             value + stage[cols + z].astype(jnp.float32) + stage[2 * cols + z].astype(jnp.float32)
-        ).astype(low)
-    for step in range(1, cols):
-        to = (col + step) % cols
-        pass_on(passed.at[3 * cols + to], last.at[step], col_sem.at[step], {"col": to})
-    value = passed[3 * cols + col].astype(jnp.float32)
+        )
+        if step > 0:
+            passed[at] = value.astype(low)
+            pass_on(passed.at[at], last.at[step], col_sem.at[step], {"col": z})
     for step in range(1, cols):
         arrival(last.at[step], col_sem.at[step])
         value = value + last[step].astype(jnp.float32)
     total_out[...] = value
-    small_own.wait()
-    for copy in small:
-        copy.wait()
     for copy in copies:
         copy.wait_send()
 
 
-def sum_all(number, partial, scores):
+def sum_scratch(block):
     cols = lax.axis_size("col")
-    total = group_size_of(("dp", "row", "col"))
+    low = jnp.bfloat16
+    return [
+        pltpu.VMEM((4 * cols,) + block, low),
+        pltpu.VMEM((4 * cols,) + block, low),
+        pltpu.VMEM((4 * cols,) + block, low),
+        pltpu.VMEM((3 * cols,) + block, low),
+        pltpu.VMEM((cols,) + block, low),
+        pltpu.SemaphoreType.DMA((4 * cols,)),
+        pltpu.SemaphoreType.DMA((48,)),
+        pltpu.SemaphoreType.DMA((4 * cols,)),
+        pltpu.SemaphoreType.DMA((cols,)),
+        pltpu.SemaphoreType.DMA((2 * cols,)),
+        pltpu.SemaphoreType.DMA((cols,)),
+    ]
+
+
+def heads_body(
+    partial, total_out, near, across_buf, pair_buf, passed, send_sem, near_sem, across_sem, pair_sem
+):
+    row, across, beside = row_peers()
+    rows = lax.axis_size("row")
+    col = lax.axis_index("col")
+    half = col % 2
+    pair = col + 1 - 2 * half
+    far = (beside + rows // 2) % rows
+    copies = []
+
+    def pass_on(src, dst, sem, peer):
+        copies.append(send(src, dst, send_sem.at[len(copies)], sem, peer))
+
+    def arrival(ref, sem):
+        pltpu.make_async_copy(ref, ref, sem).wait()
+
+    def block(row_to, part):
+        return partial.at[row_to * 2 + part]
+
+    low = jnp.bfloat16
+    parts = (1 - half, half)
+    theirs, ours = (far, beside), (across, row)
+    for turn in range(2):
+        for at, part in enumerate(parts):
+            slot = 2 * turn + at
+            pass_on(
+                block(theirs[turn], part), near.at[slot], near_sem.at[slot], {"row": beside}
+            )
+
+    def chip_sum(turn, at):
+        slot = 2 * turn + at
+        arrival(near.at[slot], near_sem.at[slot])
+        return block(ours[turn], parts[at])[...].astype(jnp.float32) + near[slot].astype(
+            jnp.float32
+        )
+
+    def first():
+        for at in range(2):
+            passed[at] = chip_sum(0, at).astype(low)
+            pass_on(passed.at[at], across_buf.at[at], across_sem.at[at], {"row": across})
+
+    def second():
+        for at in range(2):
+            value = chip_sum(1, at)
+            arrival(across_buf.at[at], across_sem.at[at])
+            value = value + across_buf[at].astype(jnp.float32)
+            if at == 0:
+                passed[2] = value.astype(low)
+                pass_on(passed.at[2], pair_buf, pair_sem, {"col": pair})
+        arrival(pair_buf, pair_sem)
+        total_out[...] = value + pair_buf[...].astype(jnp.float32)
+        for copy in copies:
+            copy.wait_send()
+
+    return first, second
+
+
+def heads_scratch(block):
+    low = jnp.bfloat16
+    return [
+        pltpu.VMEM((4,) + block, low),
+        pltpu.VMEM((2,) + block, low),
+        pltpu.VMEM(block, low),
+        pltpu.VMEM((3,) + block, low),
+        pltpu.SemaphoreType.DMA((8,)),
+        pltpu.SemaphoreType.DMA((4,)),
+        pltpu.SemaphoreType.DMA((2,)),
+        pltpu.SemaphoreType.DMA,
+    ]
+
+
+def sum_trade_kernel(plans, with_heads, *refs):
+    count = len(plans)
+    refs = list(refs)
+
+    def take(number):
+        out = refs[:number]
+        del refs[:number]
+        return out
+
+    sources, (partial,) = take(count), take(1)
+    heads = take(1) if with_heads else []
+    targets, (total_out,) = take(count), take(1)
+    heads += take(1) if with_heads else []
+    sems = take(3 * count)
+    everyone = ("dp", "row", "col")
+    size, me = group_size_of(everyone), place_in(everyone)
+    meet([device_at(everyone, (me + step) % size) for step in range(1, size)])
+    locals_, copies, more = trade_start(plans, sources, targets, sems)
+    between = ()
+    if with_heads:
+        between = heads_body(*heads, *refs[11:])
+    sum_body(more, between, partial, total_out, *refs[:11])
+    for own in locals_:
+        own.wait()
+    for copy in copies:
+        copy.wait()
+
+
+def sum_trade(number, partial, *pairs, heads=None):
+    arrays = [array for array, _ in pairs] + [partial]
+    plans = [(axes, array.shape[0] == 1, array.size > 2**21) for array, axes in pairs]
+    scratch, shapes = trade_shapes(pairs)
     block = partial.shape[1:]
     vmem = pl.BlockSpec(memory_space=pltpu.VMEM)
-    low = jnp.bfloat16
+    in_specs, out_specs = [ANYWHERE] * len(arrays), [ANYWHERE] * len(pairs) + [vmem]
+    shapes, scratch = shapes + [jax.ShapeDtypeStruct(block, jnp.float32)], scratch + sum_scratch(block)
+    if heads is not None:
+        arrays, in_specs, out_specs = arrays + [heads], in_specs + [vmem], out_specs + [vmem]
+        shapes.append(jax.ShapeDtypeStruct(heads.shape[1:], jnp.float32))
+        scratch = scratch + heads_scratch(heads.shape[1:])
     return pl.pallas_call(
-        sum_all_kernel,
-        out_shape=[
-            jax.ShapeDtypeStruct(block, jnp.float32),
-            jax.ShapeDtypeStruct(scores.shape, scores.dtype),
-        ],
-        in_specs=[vmem, vmem],
-        out_specs=[vmem, vmem],
-        scratch_shapes=[
-            pltpu.VMEM((4 * cols,) + block, low),
-            pltpu.VMEM((4 * cols,) + block, low),
-            pltpu.VMEM((3 * cols,) + block, low),
-            pltpu.VMEM((cols,) + block, low),
-            pltpu.SemaphoreType.DMA,
-            pltpu.SemaphoreType.DMA((total,)),
-            pltpu.SemaphoreType.DMA((total,)),
-            pltpu.SemaphoreType.DMA((48,)),
-            pltpu.SemaphoreType.DMA((4 * cols,)),
-            pltpu.SemaphoreType.DMA((cols,)),
-            pltpu.SemaphoreType.DMA((2 * cols,)),
-            pltpu.SemaphoreType.DMA((cols,)),
-        ],
+        functools.partial(sum_trade_kernel, plans, heads is not None),
+        out_shape=shapes,
+        in_specs=in_specs,
+        out_specs=out_specs,
+        scratch_shapes=scratch,
         compiler_params=pltpu.CompilerParams(
             collective_id=number, has_side_effects=True, vmem_limit_bytes=48 * 2**20
         ),
-        name="sum_all" + str(number),
-    )(partial, scores)
-
-
-def nt(left, right):
-    return lax.dot_general(
-        left, right, (((1,), (1,)), ((), ())), preferred_element_type=jnp.float32
-    )
-
-
-def tn(left, right):
-    return lax.dot_general(
-        left, right, (((0,), (0,)), ((), ())), preferred_element_type=jnp.float32
-    )
+        name="sum_trade" + str(number),
+    )(*arrays)
 
 
 def expert_kernel(
@@ -869,6 +1336,7 @@
     rows_out,
     score_out,
     grads_out,
+    down_out,
     kept_in,
     kept_dye,
     kept_act,
@@ -949,8 +1417,8 @@
         for chunk in range(chunks):
             lanes = slice(chunk * ff_width, (chunk + 1) * ff_width)
             grad = tn(act_all, all_of(kept_dye.at[:, :, lanes])).astype(low)
-            at = 2 * depth + chunk * down_depth
-            grads_out[:, at : at + down_depth, :] = grad.reshape(parts, down_depth, ff_width)
+            at = chunk * down_depth
+            down_out[:, at : at + down_depth, :] = grad.reshape(parts, down_depth, ff_width)
 
 
 def expert_pass(normed, cot, table, rank, mark, router, weights, slots):
@@ -958,6 +1426,9 @@
     tokens, width = normed.shape
     low = jnp.bfloat16
     ff_width = weights.shape[2]
+    parts, depth, _ = weights.shape
+    gate_up = jax.ShapeDtypeStruct((parts, 2 * (width // parts), ff_width), low)
+    down = jax.ShapeDtypeStruct((parts, depth - gate_up.shape[1], ff_width), low)
     rows = pl.BlockSpec((tile, width), lambda i: (i, 0))
     whole = lambda a: pl.BlockSpec(
         a.shape, lambda i: (0,) * len(a.shape), pipeline_mode=pl.Buffered(1)
@@ -969,7 +1440,8 @@
             jax.ShapeDtypeStruct((tokens, width), low),
             jax.ShapeDtypeStruct((tokens, width), low),
             jax.ShapeDtypeStruct((tiles, 8, tile), jnp.float32),
-            jax.ShapeDtypeStruct(weights.shape, low),
+            gate_up,
+            down,
         ],
         in_specs=[
             rows,
@@ -984,7 +1456,8 @@
             rows,
             rows,
             pl.BlockSpec((1, 8, tile), lambda i: (i, 0, 0)),
-            whole(weights),
+            whole(gate_up),
+            whole(down),
         ],
         scratch_shapes=[
             pltpu.VMEM((tiles, slots, width), low),
@@ -1055,81 +1528,63 @@
         axis=2,
     ).transpose(1, 0, 2)
     qkv_width = q_width + 2 * HEAD_DIM
-    x_blocks, w_mine, w_out_all = gather_plane(
-        0, (hidden_in, "micro", True), (w_qkv, "half", False), (w_out[None], "all", True)
-    )
+    picks = jnp.pad(routes.reshape(own_rows, TOP).T, ((0, 0), (0, 128 - own_rows)))
     weights = jnp.concatenate(
         [w_gate, w_up]
         + [w_down[:, :, at : at + ff_width] for at in range(0, model_width, ff_width)],
         axis=1,
     )
-    x_blocks, weights, masked_cot = lax.optimization_barrier((x_blocks, weights, masked_cot))
-    cot_all = lax.all_gather(
-        masked_cot.reshape(own_rows, model_width), everyone, axis=0, tiled=True
-    )
-    x_micro = (
-        x_blocks.reshape(row_count, col_count, tok_row, width_part)
-        .transpose(0, 2, 1, 3)
-        .reshape(group_tokens, model_width)
-        .astype(jnp.float32)
-    )
+    doc_id, position = documents(lengths[:, 0][micro_at], group_tokens)
+    sin_table, cos_table = (
+        table[:, 0] for table in angles(position.astype(jnp.float32), HEAD_DIM)
+    )
+    cos_lanes = jnp.tile(cos_table, (1, 4))
+    sin_lanes = jnp.tile(jnp.concatenate([-sin_table, sin_table], axis=1), (1, 2))
+    (
+        x_micro,
+        w_mine,
+        w_out_all,
+        routes_all,
+        cot_all,
+        normed_all,
+        weights,
+        qkv,
+        attended,
+        mixed,
+    ) = front(
+        0,
+        hidden_in,
+        w_qkv.reshape(kv_here, dp_count, width_part // dp_count, qkv_width),
+        w_out.reshape(dp_count, w_out.shape[0] // dp_count, w_out.shape[1]),
+        picks,
+        masked_cot.reshape(own_rows, model_width),
+        weights,
+        (norm_gain[None], mix_gain[None]),
+        (cos_lanes, sin_lanes),
+        (
+            jnp.broadcast_to(doc_id[:, None], (group_tokens, 128)),
+            jnp.broadcast_to(doc_id[None, :], (8, group_tokens)),
+        ),
+        q_width,
+    )
+    x_micro = x_micro.astype(jnp.float32)
     w_mine = w_mine.reshape(model_width, qkv_width)
-    w_out_all = (
-        w_out_all.reshape(row_count, col_count, w_out.shape[0], w_out.shape[1])
-        .transpose(0, 2, 1, 3)
-        .reshape(row_count * w_out.shape[0], model_width)
-    )
     scale_m = lax.rsqrt(jnp.mean(x_micro * x_micro, axis=1, keepdims=True) + eps_norm)
     normed_m = (x_micro * scale_m * norm_gain).astype(jnp.bfloat16)
-    qkv = project(normed_m, w_mine)
-    doc_id, position = documents(lengths[:, 0][micro_at], group_tokens)
-    sin_table, cos_table = angles(position.astype(jnp.float32), HEAD_DIM)
-    query = rotate(
-        qkv[:, :q_width].reshape(group_tokens, group_size, HEAD_DIM), sin_table, cos_table
-    ).astype(jnp.bfloat16)
-    key = rotate(
-        qkv[:, q_width : q_width + HEAD_DIM].reshape(group_tokens, 1, HEAD_DIM),
-        sin_table,
-        cos_table,
-    )[:, 0].astype(jnp.bfloat16)
-    value = qkv[:, q_width + HEAD_DIM :].astype(jnp.bfloat16)
+    sin_table, cos_table = sin_table[:, None], cos_table[:, None]
+    query = qkv[:, :q_width].reshape(group_tokens, group_size, HEAD_DIM)
+    key = qkv[:, q_width : q_width + HEAD_DIM]
+    value = qkv[:, q_width + HEAD_DIM :]
     order = jnp.arange(group_tokens, dtype=jnp.int32)
     allowed = (doc_id[:, None] == doc_id[None, :]) & (order[None, :] <= order[:, None])
     raw_scores = jnp.einsum("qgd,kd->gqk", query, key, preferred_element_type=jnp.float32)
     scores = jnp.where(allowed[None], raw_scores * attn_scale, -1e30)
     probs = jax.nn.softmax(scores, axis=-1)
     probs_low = probs.astype(jnp.bfloat16)
-    attended = (
-        jnp.einsum("gqk,kd->qgd", probs_low, value, preferred_element_type=jnp.float32)
-        .reshape(group_tokens, q_width)
-        .astype(jnp.bfloat16)
-    )
-
-    picks = jnp.pad(routes.reshape(own_rows, TOP).T, ((0, 0), (0, 128 - own_rows)))
-    attended_own, x_own, routes_all = trade(
-        1,
-        (attended.reshape(plane_count, quarter, q_width), plane),
-        (
-            hidden_in.reshape(micro_count, col_count, quarter, width_part).transpose(1, 0, 2, 3),
-            ("col",),
-        ),
-        (picks[None], everyone),
-    )
-    attended_own, weights = lax.optimization_barrier((attended_own, weights))
-    weights = spread_plane(weights)
-    x_own = (
-        x_own.transpose(1, 2, 0, 3).reshape(own_rows, model_width).astype(jnp.float32)
-    )
+    attended = attended.reshape(group_tokens, q_width)
     routes_all = (
         routes_all[:, :, :own_rows].transpose(0, 2, 1).reshape(device_count * own_rows, TOP)
     )
-    attended_own = (
-        attended_own
-        .reshape(row_count, micro_count, kv_here, quarter, q_width)
-        .transpose(1, 3, 0, 2, 4)
-        .reshape(own_rows, row_count * kv_here * q_width)
-    )
-    mixed = x_own + resid_scale * project(attended_own, w_out_all)
     scale_two = lax.rsqrt(jnp.mean(mixed * mixed, axis=1, keepdims=True) + eps_norm)
     unit_two = mixed * scale_two
     normed_two = (unit_two * mix_gain).astype(jnp.bfloat16)
@@ -1140,16 +1595,8 @@
         logits = jnp.where(chosen, project(normed_rows, w_router), -jnp.inf)
         return jax.nn.softmax(logits, axis=-1)
 
-    normed_all = gather_all(2, normed_two).reshape(device_count * own_rows, model_width)
-    normed_all, w_mine = lax.optimization_barrier((normed_all, w_mine))
-    neighbours = [(at, at + 1 - 2 * (at % 2)) for at in range(col_count)]
-    w_pair = jnp.stack([w_mine, lax.ppermute(w_mine, "col", neighbours)])
-    w_pair = jnp.where(half_at == 0, w_pair, w_pair[::-1])
-    w_qkv_all = (
-        lax.all_gather(w_pair, "row", axis=0, tiled=False)
-        .transpose(2, 0, 1, 3)
-        .reshape(model_width, row_count * kv_here * qkv_width)
-    )
+    normed_all = normed_all.reshape(device_count * own_rows, model_width)
+    cot_all = cot_all.reshape(device_count * own_rows, model_width)
     gates_own = gating(normed_two, routes.reshape(own_rows, TOP))
 
     tile = col_count * own_rows
@@ -1158,7 +1605,7 @@
     here = jnp.any(routes_all == expert_at, axis=1).astype(jnp.int32).reshape(-1, tile)
     rank = jnp.where(here > 0, jnp.cumsum(here, axis=1, dtype=jnp.int32) - 1, -1)
     pad_experts = 128 - experts_all
-    mix_part, grad_rows_part, grad_gate_mine, grads = expert_pass(
+    mix_part, grad_rows_part, grad_gate_mine, grads, grads_down = expert_pass(
         normed_all,
         cot_all,
         jnp.pad(table.astype(jnp.float32), ((0, 0), (0, pad_experts))),
@@ -1176,8 +1623,11 @@
         ),
         (device_count, 8, 128),
     )
-    grad_normed, grad_gates = sum_all(
-        3, grad_rows_part.reshape(device_count, own_rows, model_width), scores_send
+    grad_gates, grads, grad_normed = sum_trade(
+        3,
+        grad_rows_part.reshape(device_count, own_rows, model_width),
+        (scores_send, everyone),
+        (grads, plane),
     )
     grad_gates = grad_gates[:, 0, :own_rows].T
     chosen_own = jnp.any(
@@ -1187,8 +1637,6 @@
     grad_logits = gates_own * (
         grad_gates - jnp.sum(gates_own * grad_gates, axis=1, keepdims=True)
     )
-    expert_mix = lax.psum_scatter(mix_part, everyone, scatter_dimension=0, tiled=True)
-    layer_out = (mixed + resid_scale * expert_mix.astype(jnp.float32)).astype(jnp.bfloat16)
     grad_normed = grad_normed + jnp.dot(
         grad_logits, w_router.astype(jnp.float32).T, precision=highest
     )
@@ -1206,14 +1654,14 @@
         (jnp.pad(grad_logits.T, ((0, 0), (0, 128 - own_rows)))[None], "all", True),
         (lines(mix_part_grad), "all", True),
     )
-    branch_m, grads = lax.optimization_barrier((branch_m, grads))
-    grads = spread_plane(grads)
+    branch_m, grads_down = lax.optimization_barrier((branch_m, grads_down))
+    grads_down = spread_plane(grads_down)
     out_gate = grads[:, :slice_width].astype(jnp.float32)
     out_up = grads[:, slice_width : 2 * slice_width].astype(jnp.float32)
     out_down = jnp.concatenate(
         [
-            grads[:, at : at + down_slice]
-            for at in range(2 * slice_width, grads.shape[1], down_slice)
+            grads_down[:, at : at + down_slice]
+            for at in range(0, grads_down.shape[1], down_slice)
         ],
         axis=2,
     ).astype(jnp.float32)
@@ -1258,9 +1706,10 @@
         axis=1,
     ).astype(jnp.bfloat16)
     qkv_part = jnp.dot(grad_qkv.T, normed_m, preferred_element_type=jnp.float32)
-    grad_qkv_own, qkv_part, out_part = trade(
+    heads_part = nt(grad_qkv, w_mine).astype(low)
+    qkv_part, out_part, router_grad, mix_grad, expert_mix, grad_normed_one = sum_trade(
         5,
-        (grad_qkv.reshape(plane_count, quarter, qkv_width), plane),
+        mix_part.reshape(device_count, own_rows, model_width),
         (
             qkv_part.astype(low).reshape(qkv_width, col_count, width_part).transpose(1, 0, 2),
             ("col",),
@@ -1269,18 +1718,22 @@
             out_part.astype(low).reshape(q_width, col_count, width_part).transpose(1, 0, 2),
             ("col",),
         ),
-    )
-    grad_qkv_own = (
-        grad_qkv_own.reshape(row_count, micro_count, kv_here, quarter, qkv_width)
-        .transpose(1, 3, 0, 2, 4)
-        .reshape(own_rows, row_count * kv_here * qkv_width)
-    )
-    grad_normed_one = jnp.dot(grad_qkv_own, w_qkv_all.T, preferred_element_type=jnp.float32)
-    scale_one = lax.rsqrt(jnp.mean(x_own * x_own, axis=1, keepdims=True) + eps_norm)
-    unit_one = x_own * scale_one
+        (router_part[None], ("dp",)),
+        (mix_part_grad[None], ("dp",)),
+        heads=heads_part.reshape(2 * row_count, -1, model_width),
+    )
+    layer_out = (mixed + resid_scale * expert_mix).astype(jnp.bfloat16)
+    rows_each = grad_normed_one.shape[0]
+    first = (row_at * kv_here + half_at) * rows_each
+
+    def part_of(array):
+        return lax.dynamic_slice_in_dim(array, first, rows_each)
+
+    scale_one = part_of(scale_m)
+    unit_one = part_of(x_micro) * scale_one
     norm_part = jnp.sum(grad_normed_one * unit_one, axis=0)
     grad_scaled_one = grad_normed_one * norm_gain
-    grad_x = grad_mixed + scale_one * (
+    grad_x = part_of(branch_m).astype(jnp.float32) * (1.0 / resid_scale) + scale_one * (
         grad_scaled_one
         - unit_one * jnp.mean(grad_scaled_one * unit_one, axis=1, keepdims=True)
     )
@@ -1289,25 +1742,17 @@
         part = part.astype(jnp.float32)
         return jnp.sum(part.reshape((micro_count, kv_here) + part.shape[1:]), axis=0).astype(low)
 
-    grad_input, qkv_sum, out_sum, router_grad, mix_grad, norm_grad = trade(
+    grad_input, qkv_sum, out_sum, norm_grad = trade(
         6,
         (
-            grad_x.astype(low)
-            .reshape(micro_count, quarter, col_count, width_part)
-            .transpose(2, 0, 1, 3),
+            grad_x.astype(low).reshape(rows_each, col_count, width_part).transpose(1, 0, 2),
             ("col",),
         ),
         (halves(qkv_part)[None], ("dp",)),
         (halves(out_part)[None], ("dp",)),
-        (router_part[None], ("dp",)),
-        (mix_part_grad[None], ("dp",)),
         (lines(norm_part), everyone),
     )
-    grad_input = (
-        grad_input.transpose(1, 0, 2, 3)
-        .reshape(micro_count, tok_row, width_part)
-        .astype(jnp.float32)
-    )
+    grad_input = grad_input.reshape(micro_count, tok_row, width_part).astype(jnp.float32)
     qkv_sum = jnp.sum(qkv_sum.astype(jnp.float32), axis=0)
     out_sum = jnp.sum(out_sum.astype(jnp.float32), axis=0)
     router_grad = jnp.sum(router_grad, axis=0).T

time: 841 us -> 694 us (0.83)
  waiting for transfers between devices: 123 us -> 0.01 us
  Pallas kernels: 526 us -> 548 us
  between operations: 15.1 us -> 1.4 us
  local copies, waits for them, and re-layouts: 55.1 us -> 41.5 us
  starting transfers between devices: 16 us -> 6.91 us
    pallas_call x2 -> x3, Pallas kernels: 151 us -> 422 us  [the longest x1 221 us: front(): pl.pallas_call(front_kernel, out_shape=[shape((tokens, width), low), shap...]
    pallas_call x3 -> x1, Pallas kernels: 186 us -> 38.8 us  [trade(): pl.pallas_call(functools.partial(trade_kernel, plans), out_shape=shapes,...]
    pallas_call x2 -> x1, Pallas kernels: 132 us -> 30.4 us  [gather_plane(): pl.pallas_call(functools.partial(gather_plane_kernel, kinds), out_shape=s...]
    all_to_all x2 -> x1, waiting for transfers between devices: 99.7 us -> 0.01 us  [spread_plane(): lax.all_to_all(blocks, ('row', 'col'), split_axis=0, concat_axis=0, tiled...]
    ppermute x1 -> x0, waiting for transfers between devices: 23.5 us -> none  [owned(): w_pair = jnp.stack([w_mine, lax.ppermute(w_mine, 'col', neighbours)])]
    reshape x12 -> x1, local copies, waits for them, and re-layouts: 11.9 us -> 0.74 us  [owned(): grad_x.astype(low).reshape(rows_each, col_count, width_part)]
    unnamed x122 -> x62, local copies, waits for them, and re-layouts: 22 us -> 18.3 us
  transfers between devices with their start and end apart: 6 -> 1, of which waited for: 2 -> 0; matrix products, arithmetic and copies ran while one was open for 15% -> 13% of each run, Pallas kernels for 48% -> 18%
where the time goes in v3:
time: 694 us; the launch traced here: 686 us
  Pallas kernels  548 us (79%)
  matrix products  51.7 us (7%)
  local copies, waits for them, and re-layouts  41.5 us (6%)
  other arithmetic  36.9 us (5%)
    pallas_call x1, Pallas kernels, front(): pl.pallas_call(front_kernel, out_shape=[shape((tokens, width), low), shap...  221 us
    pallas_call x2, Pallas kernels, sum_trade(): pl.pallas_call(functools.partial(sum_trade_kernel, plans, heads is not No...  201 us
    pallas_call x1, Pallas kernels, expert_pass(): pl.pallas_call(expert_kernel, grid=(tiles,), out_shape=[jax.ShapeDtypeStr...  56.5 us
    pallas_call x1, Pallas kernels, trade(): pl.pallas_call(functools.partial(trade_kernel, plans), out_shape=shapes,...  38.8 us
    pallas_call x1, Pallas kernels, gather_plane(): pl.pallas_call(functools.partial(gather_plane_kernel, kinds), out_shape=s...  30.4 us
    unnamed x62, local copies, waits for them, and re-layouts  18.3 us
  transfers between devices with their start and end apart: 1, of which 0 were waited for; matrix products, arithmetic and copies ran while one was open for 13% of the time, Pallas kernels for 18%

profile of v3, /device:TPU:0, one launch (start us, length us, event | category | flops | bytes accessed | tf_op | source)
XLA Modules:
  0.0 686.4 jit_solution(5740999228452176616)
XLA Ops:
  7.2 2.8 constant_dynamic-update-slice_fusion.1
  20.0 221.1 %front0.1 = (bf16[768,1536]{1,0:T(8,128)(2,1)}, bf16[4,2,192,320]{3,2,1,0:T(8,128)(2,1)}, bf16[1536,1536]{1,0:T(8,128)(2,1)}, s32[32,8,128]{2,1,0:T(8,128)}, bf1...) custom-call(bf16[2,192,384]{2,1,0:T(8,128)(2,1)} %x.15, ...), custom_call_target="tpu_custom_call" | custom-call | tf_op jit(solution)/shard_map/front0/pallas_call | solution.py:1036
  250.5 56.5 %expert_pass.1 = (bf16[3072,1536]{1,0:T(8,128)(2,1)}, bf16[3072,1536]{1,0:T(8,128)(2,1)}, f32[8,8,384]{2,1,0:T(8,128)}, bf16[16,192,512]{2,1,0:T(8,128)(2,1)}, bf16[16,96,512]{2,1,0:T(8,128)(2,1)}) custom-call(bf16[3072,1536]{1,0:T(8,128)(2,1)} %bitcast.232, bf16[3072,1536]{1,0:T(8,128)(2,1)} %bitcast.265, f32[3072,128]{1,0:T(8,128)} %pad_convert_fusion.table, ...), custom_call_target="tpu_custom_call" | custom-call | flops 22000001024 | bytes 50000000 | tf_op jit(solution)/shard_map/expert_pass/pallas_call | solution.py:1436
  308.1 116.6 %sum_trade3.1 = (f32[32,8,128]{2,1,0:T(8,128)S(1)}, bf16[16,192,512]{2,1,0:T(8,128)(2,1)S(1)}, f32[96,1536]{1,0:T(8,128)S(1)}) custom-call(f32[32,8,128]{2,1,0:T(8,128)S(1)} %broadcast_in_dim.76.refs_0_, bf16[16,192,512]{2,1,0:T(8,128)(2,1)} %get-tuple-element.52.refs_1_, bf16[32,96,1536]{2,1,0:T(8,128)(2,1)} %bitcast.225), custom_call_target="tpu_custom_call" | custom-call | tf_op jit(solution)/shard_map/sum_trade3/pallas_call | solution.py:1314
  424.7 1.7 copy-done
  429.6 30.4 %gather_plane4.1 = (bf16[16,48,1536]{2,1,0:T(8,128)(2,1)}, f32[16,32,128]{2,1,0:T(8,128)}, f32[16,16,128]{2,1,0:T(8,128)}) custom-call(bf16[2,48,1536]{2,1,0:T(8,128)(2,1)} %bitcast.242, f32[1,32,128]{2,1,0:T(8,128)} %pad_bitcast_fusion.refs_1_, f32[1,16,128]{2,1,0:T(8,128)} %pad_bitcast_fusion.3.refs_2_), custom_call_target="tpu_custom_call" | custom-call | tf_op jit(solution)/shard_map/gather_plane4/pallas_call | solution.py:636
  460.1 6.9 %all-to-all-start = ((bf16[16,96,512]{2,1,0:T(8,128)(2,1)}), bf16[16,96,512]{2,1,0:T(8,128)(2,1)}, u32[]{:S(2)}, u32[]{:S(2)}) async-start(bf16[16,96,512]{2,1,0:T(8,128)(2,1)} %get-tuple-element.77), calls=%async_computation | async-start | bytes 3145728 | tf_op jit(solution)/shard_map/all_to_all | solution.py:399
  469.3 2.0 convolution_convert_fusion.2
  471.3 4.9 fusion.43
  476.2 6.3 fusion.102
  482.5 4.9 fusion.29
  487.3 10.3 %fusion.25 = f32[768,1,64]{0,2,1:T(8,128)S(1)} fusion(bf16[768,3,64]{0,2,1:T(8,128)(2,1)S(1)} %bitcast.256, f32[768,768,3]{1,0,2:T(8,128)} %fusion.43, f32[3,768,768]{1,2,0:T(8,128)} %get-tuple-element.129, f32[3,768]{1,0:T(4,128)S(1)} %get-tuple-element.128), kind=kOutput, calls=%fused_computation.44 | convolution fusion | flops 238881792 | bytes 14656512 | tf_op jit(solution)/shard_map/gqk,qgd->kd/dot_general | solution.py:1698
  497.6 10.7 %fusion.24 = f32[768,3,64]{0,2,1:T(8,128)S(1)} fusion(f32[768,768,3]{1,0,2:T(8,128)} %fusion.43, bf16[768,320]{1,0:T(8,128)(2,1)} %get-tuple-element.46, f32[3,768,768]{1,2,0:T(8,128)} %get-tuple-element.129, f32[3,768]{1,0:T(4,128)S(1)} %get-tuple-element.128), kind=kOutput, calls=%fused_computation.41 | convolution fusion | flops 238881792 | bytes 29122560 | tf_op jit(solution)/shard_map/gqk,kd->qgd/dot_general | solution.py:1697
  511.3 2.5 fusion.19
  517.6 3.0 convolution_convert_fusion.1
  520.6 2.9 convolution_convert_fusion
  523.5 3.4 fusion.8
  526.9 2.8 convert_element_type.176
  531.6 84.6 %sum_trade5.1 = (bf16[4,320,384]{2,1,0:T(8,128)(2,1)S(1)}, bf16[4,192,384]{2,1,0:T(8,128)(2,1)S(1)}, f32[2,32,1536]{2,1,0:T(8,128)S(1)}, f32[2,16,128]{2,1,0:T(8...) custom-call(bf16[4,320,384]{2,1,0:T(8,128)(2,1)S(1)} %bitcast.218, bf16[4,192,384]{2,1,0:T(8,128)(2,1)S(1)} %bitcast.219, ...), custom_call_target="tpu_custom_call" | custom-call | tf_op jit(solution)/shard_map/sum_trade5/pallas_call | solution.py:1314
  616.2 1.7 multiply_reduce_fusion.1
  617.9 1.4 add_convert_fusion
  622.6 38.8 %trade6.1 = (bf16[4,96,384]{2,1,0:T(8,128)(2,1)}, bf16[2,2,320,384]{3,2,1,0:T(8,128)(2,1)}, bf16[2,2,192,384]{3,2,1,0:T(8,128)(2,1)}, f32[32,16,128]{2,1,0:T(8,128)}) custom-call(bf16[4,96,384]{2,1,0:T(8,128)(2,1)} %bitcast.241, bf16[1,2,320,384]{3,2,1,0:T(8,128)(2,1)} %bitcast.236, bf16[1,2,192,384]{3,2,1,0:T(8,128)(2,1)} %bitcast.240, ...), custom_call_target="tpu_custom_call" | custom-call | tf_op jit(solution)/shard_map/trade6/pallas_call | solution.py:519
  662.4 1.4 convert_reduce_fusion
  665.7 2.1 copy.94
  667.8 1.8 fusion.99
  669.6 1.7 copy.95
  671.3 1.7 copy.96
  673.7 2.0 convert_reduce_fusion.1
  676.4 1.8 bitcast_convert_fusion
  678.2 3.6 slice_convert_fusion
  682.5 1.5 fusion.98
  684.1 2.1 maximum_convert_fusion
  (146 shorter events, 49.3 us)
Async XLA Ops:
  0.6 9.3 %copy-start.12 = (bf16[16,96,512]{2,1,0:T(8,128)(2,1)S(1)}, bf16[16,96,512]{2,1,0:T(8,128)(2,1)}, u32[]{:S(2)}) copy-start(bf16[16,96,512]{2,1,0:T(8,128)(2,1)} %param.24) | copy-start | bytes 4718596
  5.9 5.4 copy-start.13
  7.2 6.6 copy-start.20
  7.2 7.2 %copy-start.19 = (f32[1536]{0:T(1024)S(1)}, f32[1536]{0:T(1024)}, u32[]{:S(2)}) copy-start(f32[1536]{0:T(1024)} %param.21) | copy-start | bytes 18436
  7.2 7.8 %copy-start.22 = (s32[2,1,3]{2,1,0:T(1,128)S(1)}, s32[2,1,3]{2,1,0:T(1,128)}, u32[]{:S(2)}) copy-start(s32[2,1,3]{2,1,0:T(1,128)} %param.26) | copy-start | bytes 76
  9.9 7.8 %copy-start.17 = (bf16[2,48,1536]{2,1,0:T(8,128)(2,1)S(1)}, bf16[2,48,1536]{2,1,0:T(8,128)(2,1)}, u32[]{:S(2)}) copy-start(bf16[2,48,1536]{2,1,0:T(8,128)(2,1)} %param.29) | copy-start | bytes 884740
  20.0 228.7 %copy-start.15 = (bf16[1536,32]{0,1:T(8,128)(2,1)S(1)}, bf16[1536,32]{0,1:T(8,128)(2,1)}, u32[]{:S(2)}) copy-start(bf16[1536,32]{0,1:T(8,128)(2,1)} %param.22) | copy-start | bytes 294916
  308.1 118.3 %copy-start.6 = (f32[96,1536]{1,0:T(8,128)S(1)}, f32[96,1536]{1,0:T(8,128)}, u32[]{:S(2)}) copy-start(f32[96,1536]{1,0:T(8,128)} %get-tuple-element.45) | copy-start | bytes 1769476
  308.1 120.6 %copy-start.11 = (bf16[2,48,1536]{2,1,0:T(8,128)(2,1)S(1)}, bf16[2,48,1536]{2,1,0:T(8,128)(2,1)}, u32[]{:S(2)}) copy-start(bf16[2,48,1536]{2,1,0:T(8,128)(2,1)} %broadcast_multiply_fusion) | copy-start | bytes 884740
  424.7 1.7 copy-start
  460.1 9.2 %copy-start.10 = (bf16[16,48,1536]{2,1,0:T(8,128)(2,1)S(1)}, bf16[16,48,1536]{2,1,0:T(8,128)(2,1)}, u32[]{:S(2)}) copy-start(bf16[16,48,1536]{2,1,0:T(8,128)(2,1)} %get-tuple-element.58) | copy-start | bytes 7077892
  460.1 222.5 %all-to-all-start = ((bf16[16,96,512]{2,1,0:T(8,128)(2,1)}), bf16[16,96,512]{2,1,0:T(8,128)(2,1)}, u32[]{:S(2)}, u32[]{:S(2)}) async-start(bf16[16,96,512]{2,1,0:T(8,128)(2,1)} %get-tuple-element.77), calls=%async_computation | async-start | bytes 3145728 | tf_op jit(solution)/shard_map/all_to_all | solution.py:399
  471.3 4.9 copy-start.18
  497.6 10.7 %copy-start.8 = (bf16[768,1536]{1,0:T(8,128)(2,1)S(1)}, bf16[768,1536]{1,0:T(8,128)(2,1)}, u32[]{:S(2)}) copy-start(bf16[768,1536]{1,0:T(8,128)(2,1)} %get-tuple-element.60) | copy-start | bytes 7077892
  511.3 5.3 copy-start.16
  517.6 3.0 copy-start.23
  517.6 3.0 copy-start.24
  526.9 2.8 copy-start.14
  531.6 84.6 %copy-start.21 = (f32[1536]{0:T(1024)S(1)}, f32[1536]{0:T(1024)}, u32[]{:S(2)}) copy-start(f32[1536]{0:T(1024)} %param.16) | copy-start | bytes 18436
  616.2 3.1 copy-start.2
  616.2 3.1 copy-start.4
  621.1 51.9 %copy-start.5 = (f32[2,32,1536]{2,1,0:T(8,128)S(1)}, f32[2,32,1536]{2,1,0:T(8,128)}, u32[]{:S(2)}) copy-start(f32[2,32,1536]{2,1,0:T(8,128)} %copy-done.4) | copy-start | bytes 1179652
  622.6 55.6 %copy-start.1 = (bf16[16,192,512]{2,1,0:T(8,128)(2,1)S(1)}, bf16[16,192,512]{2,1,0:T(8,128)(2,1)}, u32[]{:S(2)}) copy-start(bf16[16,192,512]{2,1,0:T(8,128)(2,1)} %copy-done) | copy-start | bytes 9437188
  663.9 0.9 copy-start.9
  678.2 3.6 copy-start.3
  678.2 3.6 copy-start.7

commit v4 on v3

--- a/solution.py
+++ b/solution.py
@@ -395,10 +395,6 @@
     )
 
 
-def spread_plane(blocks):
-    return lax.all_to_all(blocks, ("row", "col"), split_axis=0, concat_axis=0, tiled=True)
-
-
 MESH = pl.DeviceIdType.MESH
 ANYWHERE = pl.BlockSpec(memory_space=pl.ANY)
 
@@ -445,203 +441,12 @@
     return copy
 
 
-def trade_start(plans, sources, targets, sems):
-    copies, locals_, later = [], [], []
-
-    def ship(at, axes, same, step):
-        size, me = group_size_of(axes), place_in(axes)
-        to = (me + step) % size
-        copies.append(
-            send(
-                sources[at].at[0 if same else to],
-                targets[at].at[me],
-                sems[3 * at + 1].at[step],
-                sems[3 * at + 2].at[step],
-                device_at(axes, to),
-            )
-        )
-
-    for at, (axes, same, bulk) in enumerate(plans):
-        size, me = group_size_of(axes), place_in(axes)
-        own = pltpu.make_async_copy(
-            sources[at].at[0 if same else me], targets[at].at[me], sems[3 * at]
-        )
-        own.start()
-        locals_.append(own)
-        for step in range(1, size):
-            if bulk:
-                later.append((at, axes, same, step))
-            else:
-                ship(at, axes, same, step)
-
-    def more(count):
-        for item in later[:count]:
-            ship(*item)
-        del later[:count]
-
-    return locals_, copies, more
-
-
-def trade_kernel(plans, *refs):
-    count = len(plans)
-    groups = [axes for axes, _, _ in plans]
-    sources, targets, sems = refs[:count], refs[count : 2 * count], refs[2 * count :]
-    widest = max(groups, key=len)
-    peers = []
-    for axes in (widest, *(g for g in groups if not set(g) <= set(widest))):
-        size = group_size_of(axes)
-        peers += [device_at(axes, (place_in(axes) + step) % size) for step in range(1, size)]
-    meet(peers)
-    locals_, copies, _ = trade_start(plans, sources, targets, sems)
-    for own in locals_:
-        own.wait()
-    for copy in copies:
-        copy.wait()
-
-
-def trade_shapes(pairs):
-    scratch, shapes = [], []
-    for array, axes in pairs:
-        size = group_size_of(axes)
-        shapes.append(jax.ShapeDtypeStruct((size,) + array.shape[1:], array.dtype))
-        scratch += [
-            pltpu.SemaphoreType.DMA,
-            pltpu.SemaphoreType.DMA((size,)),
-            pltpu.SemaphoreType.DMA((size,)),
-        ]
-    return scratch, shapes
-
-
-def trade(number, *pairs):
-    arrays = [array for array, _ in pairs]
-    plans = [(axes, array.shape[0] == 1, False) for array, axes in pairs]
-    scratch, shapes = trade_shapes(pairs)
-    return pl.pallas_call(
-        functools.partial(trade_kernel, plans),
-        out_shape=shapes,
-        in_specs=[ANYWHERE] * len(arrays),
-        out_specs=[ANYWHERE] * len(arrays),
-        scratch_shapes=scratch,
-        compiler_params=pltpu.CompilerParams(collective_id=number, has_side_effects=True),
-        name="trade" + str(number),
-    )(*arrays)
-
-
 def row_peers():
     row = lax.axis_index("row")
     rows = lax.axis_size("row")
     across = (row + rows // 2) % rows
     beside = row + 1 - 2 * (row % 2)
     return row, across, beside
-
-
-def gather_plane_kernel(kinds, *refs):
-    count = len(kinds)
-    sources, targets, sems = refs[:count], refs[count : 2 * count], refs[2 * count :]
-    row, across, beside = row_peers()
-    col, cols = lax.axis_index("col"), lax.axis_size("col")
-    meet(
-        [{"col": (col + step) % cols} for step in range(1, cols)]
-        + [{"row": across}, {"row": beside}]
-    )
-
-    def pick(kind, at):
-        return {"micro": at // 2, "half": at % 2, "all": 0}[kind]
-
-    copies, locals_ = [], []
-    for at, (kind, rows_too) in enumerate(kinds):
-        source, target = sources[at], targets[at]
-        local_sem, send_sem, col_sem, across_sem, beside_sem = sems[5 * at : 5 * at + 5]
-        me = row * cols + col if rows_too else col
-        own = pltpu.make_async_copy(source.at[pick(kind, col)], target.at[me], local_sem)
-        own.start()
-        locals_.append(own)
-        for step in range(1, cols):
-            to = (col + step) % cols
-            copies.append(
-                send(
-                    source.at[pick(kind, to)],
-                    target.at[me],
-                    send_sem.at[step],
-                    col_sem.at[step],
-                    {"col": to},
-                )
-            )
-        if rows_too:
-            mine = source.at[pick(kind, col)]
-            copies.append(
-                send(mine, target.at[me], send_sem.at[4], across_sem.at[0], {"row": across})
-            )
-            copies.append(
-                send(mine, target.at[me], send_sem.at[5], beside_sem.at[0], {"row": beside})
-            )
-
-    def arrival(at, block, sem):
-        pltpu.make_async_copy(targets[at].at[block], targets[at].at[block], sem).wait()
-
-    for step in range(1, cols):
-        for at, (kind, rows_too) in enumerate(kinds):
-            _, send_sem, col_sem, across_sem, beside_sem = sems[5 * at : 5 * at + 5]
-            origin = (col + cols - step) % cols
-            block = row * cols + origin if rows_too else origin
-            arrival(at, block, col_sem.at[step])
-            if rows_too:
-                part = targets[at].at[block]
-                copies.append(
-                    send(part, part, send_sem.at[5 + step], across_sem.at[step], {"row": across})
-                )
-                copies.append(
-                    send(part, part, send_sem.at[8 + step], beside_sem.at[step], {"row": beside})
-                )
-    for step in range(cols):
-        for at, (kind, rows_too) in enumerate(kinds):
-            if not rows_too:
-                continue
-            _, send_sem, _, across_sem, beside_sem = sems[5 * at : 5 * at + 5]
-            block = across * cols + (col + cols - step) % cols
-            arrival(at, block, across_sem.at[step])
-            part = targets[at].at[block]
-            copies.append(
-                send(part, part, send_sem.at[12 + step], beside_sem.at[4 + step], {"row": beside})
-            )
-    for at, (kind, rows_too) in enumerate(kinds):
-        if rows_too:
-            for step in range(2 * cols):
-                side = beside if step < cols else (beside + 2) % lax.axis_size("row")
-                arrival(at, side * cols + (col + cols - step) % cols, sems[5 * at + 4].at[step])
-    for own in locals_:
-        own.wait()
-    for copy in copies:
-        copy.wait_send()
-
-
-def gather_plane(number, *items):
-    arrays = [array for array, _, _ in items]
-    kinds = [(kind, rows_too) for _, kind, rows_too in items]
-    cols, plane = lax.axis_size("col"), group_size_of(("row", "col"))
-    scratch, shapes = [], []
-    for array, kind, rows_too in items:
-        scratch += [
-            pltpu.SemaphoreType.DMA,
-            pltpu.SemaphoreType.DMA((16,)),
-            pltpu.SemaphoreType.DMA((cols,)),
-            pltpu.SemaphoreType.DMA((cols,)),
-            pltpu.SemaphoreType.DMA((2 * cols,)),
-        ]
-        shapes.append(
-            jax.ShapeDtypeStruct(
-                (plane if rows_too else cols,) + array.shape[1:], array.dtype
-            )
-        )
-    return pl.pallas_call(
-        functools.partial(gather_plane_kernel, kinds),
-        out_shape=shapes,
-        in_specs=[ANYWHERE] * len(arrays),
-        out_specs=[ANYWHERE] * len(arrays),
-        scratch_shapes=scratch,
-        compiler_params=pltpu.CompilerParams(collective_id=number, has_side_effects=True),
-        name="gather_plane" + str(number),
-    )(*arrays)
 
 
 def gather_line(source, target, sems, copies):
@@ -1073,114 +878,6 @@
     )(x, w_qkv, w_out, picks[None], cot[None], weights, *gains, *tables, *docs)
 
 
-def sum_body(
-    more,
-    between,
-    partial,
-    total_out,
-    near,
-    mine,
-    passed,
-    stage,
-    last,
-    local_sem,
-    send_sem,
-    beside_sem,
-    first_sem,
-    second_sem,
-    col_sem,
-):
-    row, across, beside = row_peers()
-    rows, cols = lax.axis_size("row"), lax.axis_size("col")
-    col, dp = lax.axis_index("col"), lax.axis_index("dp")
-    other = 1 - dp
-    copies, loads = [], []
-
-    def pass_on(src, dst, sem, peer):
-        copies.append(send(src, dst, send_sem.at[len(copies)], sem, peer))
-
-    def arrival(ref, sem):
-        pltpu.make_async_copy(ref, ref, sem).wait()
-
-    def block_of(dp_to, row_to, col_to):
-        return (dp_to * rows + row_to) * cols + col_to
-
-    far = (beside + rows // 2) % rows
-    theirs = ((other, far), (other, beside), (dp, far), (dp, beside))
-    ours = ((other, across), (other, row), (dp, across), (dp, row))
-    for turn, (dp_to, row_to) in enumerate(theirs):
-        for z in range(cols):
-            at = turn * cols + z
-            pass_on(
-                partial.at[block_of(dp_to, row_to, z)],
-                near.at[at],
-                beside_sem.at[at],
-                {"row": beside},
-            )
-            load = pltpu.make_async_copy(
-                partial.at[block_of(*ours[turn], z)], mine.at[at], local_sem.at[at]
-            )
-            load.start()
-            loads.append(load)
-
-    def chip_sum(turn, z):
-        at = turn * cols + z
-        loads[at].wait()
-        arrival(near.at[at], beside_sem.at[at])
-        return mine[at].astype(jnp.float32) + near[at].astype(jnp.float32)
-
-    low = jnp.bfloat16
-    more(5)
-    for z in range(cols):
-        passed[z] = chip_sum(0, z).astype(low)
-        peer = {"dp": other} if z < 2 else {"row": across}
-        pass_on(passed.at[z], stage.at[z], first_sem.at[z], peer)
-    more(5)
-    if between:
-        between[0]()
-    for z in range(cols):
-        value = chip_sum(1, z)
-        if z >= 2:
-            arrival(stage.at[z], first_sem.at[z])
-            value = value + stage[z].astype(jnp.float32)
-        passed[cols + z] = value.astype(low)
-        pass_on(passed.at[cols + z], stage.at[cols + z], second_sem.at[z], {"dp": other})
-        value = chip_sum(2, z)
-        if z < 2:
-            arrival(stage.at[z], first_sem.at[z])
-            value = value + stage[z].astype(jnp.float32)
-        passed[2 * cols + z] = value.astype(low)
-        pass_on(
-            passed.at[2 * cols + z],
-            stage.at[2 * cols + z],
-            second_sem.at[cols + z],
-            {"row": across},
-        )
-    more(99)
-    if between:
-        between[1]()
-    for step in range(cols - 1, -1, -1):
-        z = (col + step) % cols
-        at = 3 * cols + z
-        pltpu.make_async_copy(mine.at[at], mine.at[at], local_sem.at[at]).wait()
-        arrival(near.at[at], beside_sem.at[at])
-        value = mine[at].astype(jnp.float32) + near[at].astype(jnp.float32)
-        arrival(stage.at[cols + z], second_sem.at[z])
-        arrival(stage.at[2 * cols + z], second_sem.at[cols + z])
-        value = (
-            value + stage[cols + z].astype(jnp.float32) + stage[2 * cols + z].astype(jnp.float32)
-        )
-        if step > 0:
-            passed[at] = value.astype(low)
-            pass_on(passed.at[at], last.at[step], col_sem.at[step], {"col": z})
-    for step in range(1, cols):
-        arrival(last.at[step], col_sem.at[step])
-        value = value + last[step].astype(jnp.float32)
-    total_out[...] = value
-    for copy in copies:
-        copy.wait_send()
-
-
 def sum_scratch(block):
     cols = lax.axis_size("col")
     low = jnp.bfloat16
@@ -1199,129 +896,563 @@
     ]
 
 
-def heads_body(
-    partial, total_out, near, across_buf, pair_buf, passed, send_sem, near_sem, across_sem, pair_sem
+def sum_steps(partial, sems, copies):
+    (
+        near,
+        mine,
+        passed,
+        stage,
+        last,
+        local_sem,
+        send_sem,
+        beside_sem,
+        first_sem,
+        second_sem,
+        col_sem,
+    ) = sems
+    row, across, beside = row_peers()
+    rows, cols = lax.axis_size("row"), lax.axis_size("col")
+    col, dp = lax.axis_index("col"), lax.axis_index("dp")
+    other = 1 - dp
+    low = jnp.bfloat16
+    sent = []
+
+    def pass_on(src, dst, sem, peer):
+        copy = send(src, dst, send_sem.at[len(sent)], sem, peer)
+        sent.append(copy)
+        copies.append(copy)
+
+    def arrival(ref, sem):
+        pltpu.make_async_copy(ref, ref, sem).wait()
+
+    def block_of(dp_to, row_to, col_to):
+        return (dp_to * rows + row_to) * cols + col_to
+
+    far = (beside + rows // 2) % rows
+    theirs = ((other, far), (other, beside), (dp, far), (dp, beside))
+    ours = ((other, across), (other, row), (dp, across), (dp, row))
+
+    def start():
+        for turn in range(4):
+            for z in range(cols):
+                at = turn * cols + z
+                pass_on(
+                    partial.at[block_of(*theirs[turn], z)],
+                    near.at[at],
+                    beside_sem.at[at],
+                    {"row": beside},
+                )
+                pltpu.make_async_copy(
+                    partial.at[block_of(*ours[turn], z)], mine.at[at], local_sem.at[at]
+                ).start()
+
+    def chip_sum(at):
+        arrival(mine.at[at], local_sem.at[at])
+        arrival(near.at[at], beside_sem.at[at])
+        return mine[at].astype(jnp.float32) + near[at].astype(jnp.float32)
+
+    def diagonal():
+        for z in range(cols):
+            passed[z] = chip_sum(z).astype(low)
+            peer = {"dp": other} if z < 2 else {"row": across}
+            pass_on(passed.at[z], stage.at[z], first_sem.at[z], peer)
+
+    def middle():
+        for z in range(cols):
+            for turn, here, peer in ((1, z >= 2, {"dp": other}), (2, z < 2, {"row": across})):
+                at = turn * cols + z
+                value = chip_sum(at)
+                if here:
+                    arrival(stage.at[z], first_sem.at[z])
+                    value = value + stage[z].astype(jnp.float32)
+                passed[at] = value.astype(low)
+                pass_on(passed.at[at], stage.at[at], second_sem.at[at - cols], peer)
+
+    def chip_total(z):
+        value = chip_sum(3 * cols + z)
+        for turn in (1, 2):
+            arrival(stage.at[turn * cols + z], second_sem.at[(turn - 1) * cols + z])
+            value = value + stage[turn * cols + z].astype(jnp.float32)
+        return value
+
+    def spread():
+        for step in range(cols - 1, 0, -1):
+            z = (col + step) % cols
+            passed[3 * cols + z] = chip_total(z).astype(low)
+            pass_on(passed.at[3 * cols + z], last.at[step], col_sem.at[step], {"col": z})
+
+    def total():
+        value = chip_total(col)
+        for step in range(1, cols):
+            arrival(last.at[step], col_sem.at[step])
+            value = value + last[step].astype(jnp.float32)
+        return value
+
+    return start, diagonal, middle, spread, total
+
+
+def back_kernel(
+    partial,
+    mix_part,
+    grads,
+    scores,
+    normed_all,
+    mixed,
+    cot,
+    gates,
+    router_t,
+    gain_one,
+    gain_two,
+    x_all,
+    w_mine,
+    w_out_mine,
+    qkv,
+    attended,
+    cos_table,
+    sin_table,
+    doc_col,
+    doc_row,
+    mix_out,
+    grads_own,
+    dw_pair,
+    do_pair,
+    router_pair,
+    x_grads,
+    lines_all,
+    scores_in,
+    branch,
+    branch_all,
+    logits,
+    logits_all,
+    plane_rows,
+    rotated,
+    values_grad,
+    grad_att,
+    grad_qkv,
+    normed,
+    heads,
+    heads_near,
+    heads_across,
+    heads_pair,
+    heads_passed,
+    dw_send,
+    dw_in,
+    do_send,
+    do_in,
+    x_send,
+    lines,
+    score_local,
+    score_send,
+    score_recv,
+    ship_local,
+    ship_send,
+    ship_recv,
+    plane_sem,
+    gather_send,
+    branch_col,
+    branch_across,
+    branch_beside,
+    logits_col,
+    logits_across,
+    logits_beside,
+    heads_send,
+    near_sem,
+    across_sem,
+    pair_sem,
+    part_local,
+    part_send,
+    dw_sem,
+    do_sem,
+    x_sem,
+    swap_sem,
+    *groups,
 ):
     row, across, beside = row_peers()
-    rows = lax.axis_size("row")
-    col = lax.axis_index("col")
+    rows, cols = lax.axis_size("row"), lax.axis_size("col")
+    col, dp = lax.axis_index("col"), lax.axis_index("dp")
+    other = 1 - dp
+    far = (beside + rows // 2) % rows
     half = col % 2
     pair = col + 1 - 2 * half
-    far = (beside + rows // 2) % rows
-    copies = []
-
-    def pass_on(src, dst, sem, peer):
-        copies.append(send(src, dst, send_sem.at[len(copies)], sem, peer))
+    everyone, plane = ("dp", "row", "col"), ("row", "col")
+    size, me = group_size_of(everyone), place_in(everyone)
+    plane_size, plane_me = group_size_of(plane), place_in(plane)
+    low, wide = jnp.bfloat16, jnp.float32
+    copies, moved, parts, small, locals_ = [], [], [], [], []
+    meet([device_at(everyone, (me + step) % size) for step in range(1, size)])
 
     def arrival(ref, sem):
         pltpu.make_async_copy(ref, ref, sem).wait()
 
-    def block(row_to, part):
-        return partial.at[row_to * 2 + part]
-
-    low = jnp.bfloat16
-    parts = (1 - half, half)
-    theirs, ours = (far, beside), (across, row)
-    for turn in range(2):
-        for at, part in enumerate(parts):
-            slot = 2 * turn + at
-            pass_on(
-                block(theirs[turn], part), near.at[slot], near_sem.at[slot], {"row": beside}
+    def ship(first, last):
+        for step in range(first, last):
+            to = (plane_me + step) % plane_size
+            moved.append(
+                send(
+                    grads.at[to],
+                    grads_own.at[plane_me],
+                    ship_send.at[step],
+                    ship_recv.at[step],
+                    device_at(plane, to),
+                )
             )
 
-    def chip_sum(turn, at):
-        slot = 2 * turn + at
-        arrival(near.at[slot], near_sem.at[slot])
-        return block(ours[turn], parts[at])[...].astype(jnp.float32) + near[slot].astype(
-            jnp.float32
-        )
-
-    def first():
-        for at in range(2):
-            passed[at] = chip_sum(0, at).astype(low)
-            pass_on(passed.at[at], across_buf.at[at], across_sem.at[at], {"row": across})
-
-    def second():
-        for at in range(2):
-            value = chip_sum(1, at)
-            arrival(across_buf.at[at], across_sem.at[at])
-            value = value + across_buf[at].astype(jnp.float32)
-            if at == 0:
-                passed[2] = value.astype(low)
-                pass_on(passed.at[2], pair_buf, pair_sem, {"col": pair})
-        arrival(pair_buf, pair_sem)
-        total_out[...] = value + pair_buf[...].astype(jnp.float32)
-        for copy in copies:
-            copy.wait_send()
-
-    return first, second
-
-
-def heads_scratch(block):
-    low = jnp.bfloat16
-    return [
-        pltpu.VMEM((4,) + block, low),
-        pltpu.VMEM((2,) + block, low),
-        pltpu.VMEM(block, low),
-        pltpu.VMEM((3,) + block, low),
-        pltpu.SemaphoreType.DMA((8,)),
-        pltpu.SemaphoreType.DMA((4,)),
-        pltpu.SemaphoreType.DMA((2,)),
-        pltpu.SemaphoreType.DMA,
+    def keep(src, dst):
+        copy = pltpu.make_async_copy(src, dst, part_local.at[len(locals_)])
+        copy.start()
+        locals_.append(copy)
+
+    rows_sum = sum_steps(partial, groups[0:11], copies)
+    mix_sum = sum_steps(
+        mix_part, groups[0:3] + groups[11:12] + groups[4:5] + groups[12:18], copies
+    )
+    lines_line = gather_line(lines, lines_all, groups[18:24], copies)
+
+    score_own = pltpu.make_async_copy(scores.at[me], scores_in.at[me], score_local)
+    score_own.start()
+    for step in range(1, size):
+        to = (me + step) % size
+        small.append(
+            send(
+                scores.at[to],
+                scores_in.at[me],
+                score_send.at[step],
+                score_recv.at[step],
+                device_at(everyone, to),
+            )
+        )
+    rows_sum[0]()
+    keep(grads.at[plane_me], grads_own.at[plane_me])
+    ship(1, 5)
+    tokens, model_width = x_all.shape
+    depth = tokens // rows
+    for block in range(rows):
+        part = slice(block * depth, (block + 1) * depth)
+        normed[part, :] = norm_rows(x_all[part, :].astype(wide), gain_one[...])[1]
+    rows_sum[1]()
+    rows_sum[2]()
+    rows_sum[3]()
+    score_own.wait()
+    for copy in small:
+        copy.wait()
+    gate = gates[...]
+    scored = jnp.concatenate(
+        [scores_in[:, 0, :], jnp.zeros((128 - size, 128), wide)], axis=0
+    ).T[: gate.shape[0], :]
+    grad_logits = gate * (scored - jnp.sum(gate * scored, axis=1, keepdims=True))
+    routed = jnp.dot(
+        grad_logits, router_t[...].astype(wide), precision=highest, preferred_element_type=wide
+    )
+    logits[0] = jnp.concatenate(
+        [grad_logits, jnp.zeros((128 - gate.shape[0], 128), wide)], axis=0
+    ).T[: logits.shape[1], :]
+    value = mixed[...]
+    scale_two = lax.rsqrt(jnp.mean(value * value, axis=1, keepdims=True) + eps_norm)
+    unit_two = value * scale_two
+    grad_normed = rows_sum[4]() + routed
+    mix_row = jnp.sum(grad_normed * unit_two, axis=0, keepdims=True)
+    grad_scaled = grad_normed * gain_two[...]
+    grad_mixed = cot[...].astype(wide) + scale_two * (
+        grad_scaled - unit_two * jnp.mean(grad_scaled * unit_two, axis=1, keepdims=True)
+    )
+    quarter = branch.shape[1]
+    for m in range(2):
+        branch[m] = (resid_scale * grad_mixed[m * quarter : (m + 1) * quarter, :]).astype(low)
+
+    sent = []
+
+    def pass_on(src, dst, sem, peer):
+        sent.append(send(src, dst, gather_send.at[len(sent)], sem, peer))
+
+    def origin(step):
+        return (col + cols - step) % cols
+
+    for step in range(1, cols):
+        to = (col + step) % cols
+        pass_on(branch.at[to // 2], branch_all.at[plane_me], branch_col.at[step], {"col": to})
+        pass_on(logits.at[0], logits_all.at[plane_me], logits_col.at[step], {"col": to})
+    keep(branch.at[col // 2], branch_all.at[plane_me])
+    keep(logits.at[0], logits_all.at[plane_me])
+    plans = (
+        (branch.at[col // 2], branch_all, branch_col, branch_across, branch_beside),
+        (logits.at[0], logits_all, logits_col, logits_across, logits_beside),
+    )
+    for step in range(cols):
+        for mine, target, col_sem, side_sem, core_sem in plans:
+            part = target.at[row * cols + origin(step)]
+            if step > 0:
+                arrival(part, col_sem.at[step])
+            source = mine if step == 0 else part
+            pass_on(source, part, side_sem.at[step], {"row": across})
+            pass_on(source, part, core_sem.at[step], {"row": beside})
+    ship(5, 11)
+    for step in range(cols):
+        for mine, target, col_sem, side_sem, core_sem in plans:
+            part = target.at[across * cols + origin(step)]
+            arrival(part, side_sem.at[step])
+            pass_on(part, part, core_sem.at[cols + step], {"row": beside})
+    for at, row_from in enumerate((beside, far)):
+        for step in range(cols):
+            for mine, target, col_sem, side_sem, core_sem in plans:
+                arrival(target.at[row_from * cols + origin(step)], core_sem.at[at * cols + step])
+    for copy in locals_:
+        copy.wait()
+    for copy in copies:
+        copy.wait_send()
+    done = len(copies)
+    mix_sum[0]()
+
+    branch_rows = branch_all[...].reshape(tokens, model_width)
+    kv_at = attended.shape[2]
+    count = kv_at // HEAD_DIM
+    grad_att[...] = nt(branch_rows, w_out_mine[...]).astype(low)
+    rotated[:, kv_at : kv_at + HEAD_DIM] = jnp.zeros((tokens, HEAD_DIM), wide)
+    values_grad[...] = jnp.zeros_like(values_grad)
+    for block in range(rows):
+        part = slice(block * depth, (block + 1) * depth)
+        extent = key_extent(block, depth, tokens)
+        allowed = visible(doc_col, doc_row, block, depth, extent)
+        key = qkv[0:extent, kv_at : kv_at + HEAD_DIM]
+        value_rows = qkv[0:extent, kv_at + HEAD_DIM : kv_at + 2 * HEAD_DIM]
+        key_sum = jnp.zeros((extent, HEAD_DIM), wide)
+        value_sum = jnp.zeros((extent, HEAD_DIM), wide)
+        for head in range(count):
+            lanes = slice(head * HEAD_DIM, (head + 1) * HEAD_DIM)
+            query = qkv[part, lanes]
+            probs = attend(query, key, allowed)
+            grad_out = grad_att[part, lanes]
+            grad_probs = nt(grad_out, value_rows)
+            grad_scores = probs * (
+                grad_probs - jnp.sum(probs * grad_probs, axis=1, keepdims=True)
+            )
+            grad_raw = (grad_scores * attn_scale).astype(low)
+            rotated[part, lanes] = project(grad_raw, key)
+            key_sum = key_sum + tn(grad_raw, query)
+            value_sum = value_sum + tn(probs.astype(low), grad_out)
+        rotated[0:extent, kv_at : kv_at + HEAD_DIM] += key_sum
+        values_grad[0:extent, :] += value_sum
+        if block == 1:
+            mix_sum[1]()
+    for at in range(2):
+        piece = slice(at * 128, (at + 1) * 128)
+        grad_qkv[:, piece] = turn(rotated[:, piece], cos_table[...], -sin_table[...]).astype(low)
+    grad_qkv[:, 256:] = values_grad[...].astype(low)
+
+    rows_each = heads.shape[1]
+    projection = w_mine[...].reshape(model_width, w_mine.shape[3])
+    heads_sent = []
+
+    def heads_on(src, dst, sem, peer):
+        heads_sent.append(send(src, dst, heads_send.at[len(heads_sent)], sem, peer))
+
+    halves = (1 - half, half)
+    for at, row_to in enumerate((far, beside, across, row)):
+        for which, part in enumerate(halves):
+            slot = 2 * at + which
+            first = pl.multiple_of((row_to * 2 + part) * rows_each, rows_each)
+            heads[slot] = nt(grad_qkv[pl.ds(first, rows_each), :], projection).astype(low)
+            if at < 2:
+                heads_on(heads.at[slot], heads_near.at[slot], near_sem.at[slot], {"row": beside})
+    width = model_width // cols
+    heads_out = attended[...].reshape(tokens, kv_at)
+    for step in range(cols - 1, -1, -1):
+        to = (col + step) % cols
+        lanes = pl.ds(pl.multiple_of(to * width, width), width)
+        dw_send[to] = tn(grad_qkv[...], normed[:, lanes]).astype(low)
+        chunk = branch_all[:, :, lanes].reshape(tokens, width)
+        do_send[to] = tn(heads_out, chunk).astype(low)
+        if step > 0:
+            parts.append(
+                send(dw_send.at[to], dw_in.at[col], part_send.at[step], dw_sem.at[step], {"col": to})
+            )
+            parts.append(
+                send(
+                    do_send.at[to],
+                    do_in.at[col],
+                    part_send.at[cols + step],
+                    do_sem.at[step],
+                    {"col": to},
+                )
+            )
+    keep(dw_send.at[col], dw_in.at[col])
+    keep(do_send.at[col], do_in.at[col])
+
+    def heads_sum(slot):
+        arrival(heads_near.at[slot - 4], near_sem.at[slot - 4])
+        return heads[slot].astype(wide) + heads_near[slot - 4].astype(wide)
+
+    for which in range(2):
+        heads_passed[which] = heads_sum(4 + which).astype(low)
+        heads_on(
+            heads_passed.at[which], heads_across.at[which], across_sem.at[which], {"row": across}
+        )
+    mix_sum[2]()
+    ship(11, plane_size)
+    router_sum = jnp.zeros((logits.shape[1], model_width), wide)
+    group = plane_rows.shape[0]
+    for first in range(0, plane_size, group):
+        load = pltpu.make_async_copy(
+            normed_all.at[pl.ds(dp * plane_size + first, group)], plane_rows, score_local
+        )
+        load.start()
+        load.wait()
+        for at in range(group):
+            left = logits_all[first + at, :, 0 : 2 * quarter]
+            for _ in range(3):
+                piece = left.astype(low)
+                left = left - piece.astype(wide)
+                router_sum = router_sum + project(piece, plane_rows[at])
+    router_pair[dp] = router_sum
+    swaps = [
+        send(router_pair.at[dp], router_pair.at[dp], swap_sem.at[0], swap_sem.at[1], {"dp": other})
     ]
-
-
-def sum_trade_kernel(plans, with_heads, *refs):
-    count = len(plans)
-    refs = list(refs)
-
-    def take(number):
-        out = refs[:number]
-        del refs[:number]
-        return out
-
-    sources, (partial,) = take(count), take(1)
-    heads = take(1) if with_heads else []
-    targets, (total_out,) = take(count), take(1)
-    heads += take(1) if with_heads else []
-    sems = take(3 * count)
-    everyone = ("dp", "row", "col")
-    size, me = group_size_of(everyone), place_in(everyone)
-    meet([device_at(everyone, (me + step) % size) for step in range(1, size)])
-    locals_, copies, more = trade_start(plans, sources, targets, sems)
-    between = ()
-    if with_heads:
-        between = heads_body(*heads, *refs[11:])
-    sum_body(more, between, partial, total_out, *refs[:11])
-    for own in locals_:
-        own.wait()
-    for copy in copies:
+    for which in range(2):
+        grad_one = heads_sum(6 + which)
+        arrival(heads_across.at[which], across_sem.at[which])
+        grad_one = grad_one + heads_across[which].astype(wide)
+        if which == 0:
+            heads_passed[2] = grad_one.astype(low)
+            heads_on(heads_passed.at[2], heads_pair, pair_sem, {"col": pair})
+    arrival(heads_pair, pair_sem)
+    grad_one = grad_one + heads_pair[...].astype(wide)
+    first = (row * 2 + half) * rows_each
+    x_rows = x_all[pl.ds(pl.multiple_of(first, rows_each), rows_each), :].astype(wide)
+    scale_one = lax.rsqrt(jnp.mean(x_rows * x_rows, axis=1, keepdims=True) + eps_norm)
+    unit_one = x_rows * scale_one
+    norm_row = jnp.sum(grad_one * unit_one, axis=0, keepdims=True)
+    each = rows_each // quarter
+    grad_h = branch_all[pl.ds((row * 2 + half) * each, each)].reshape(rows_each, model_width)
+    grad_scaled = grad_one * gain_one[...]
+    grad_x = grad_h.astype(wide) * (1.0 / resid_scale) + scale_one * (
+        grad_scaled - unit_one * jnp.mean(grad_scaled * unit_one, axis=1, keepdims=True)
+    )
+    for to in range(cols):
+        x_send[to] = grad_x[:, to * width : (to + 1) * width].astype(low)
+    for step in range(1, cols):
+        to = (col + step) % cols
+        swaps.append(
+            send(
+                x_send.at[to], x_grads.at[col], x_sem.at[step], x_sem.at[cols + step], {"col": to}
+            )
+        )
+    keep(x_send.at[col], x_grads.at[col])
+    steps = model_width // 128
+    for at in range(steps):
+        piece = slice(at * 128, (at + 1) * 128)
+        lines[0, at : at + 1, :] = norm_row[:, piece]
+        lines[0, steps + at : steps + at + 1, :] = mix_row[:, piece]
+    lines_line[0]()
+    for copy in locals_[3:]:
         copy.wait()
-
-
-def sum_trade(number, partial, *pairs, heads=None):
-    arrays = [array for array, _ in pairs] + [partial]
-    plans = [(axes, array.shape[0] == 1, array.size > 2**21) for array, axes in pairs]
-    scratch, shapes = trade_shapes(pairs)
+    for step in range(1, cols):
+        arrival(dw_in.at[origin(step)], dw_sem.at[step])
+        arrival(do_in.at[origin(step)], do_sem.at[step])
+    for h in range(2):
+        dw_pair[dp, h] = (dw_in[h].astype(wide) + dw_in[2 + h].astype(wide)).astype(low)
+        do_pair[dp, h] = (do_in[h].astype(wide) + do_in[2 + h].astype(wide)).astype(low)
+    swaps.append(
+        send(dw_pair.at[dp], dw_pair.at[dp], swap_sem.at[2], swap_sem.at[3], {"dp": other})
+    )
+    swaps.append(
+        send(do_pair.at[dp], do_pair.at[dp], swap_sem.at[4], swap_sem.at[5], {"dp": other})
+    )
+    mix_sum[3]()
+    for at in range(1, 4):
+        for step in range(cols):
+            lines_line[at](step)
+    mix_out[...] = mix_sum[4]()
+    lines_line[4]()
+    for copy in swaps:
+        copy.wait()
+    for copy in moved:
+        copy.wait()
+    for copy in copies[done:] + parts + sent + heads_sent:
+        copy.wait_send()
+
+
+def back(number, partial, mix_part, grads, scores, normed_all, *rest):
+    mixed, _, _, _, _, _, x_all, w_mine, _, qkv, attended = rest[:11]
+    cols, rows = lax.axis_size("col"), lax.axis_size("row")
+    total, plane = group_size_of(("dp", "row", "col")), group_size_of(("row", "col"))
+    low, wide = jnp.bfloat16, jnp.float32
+    vmem = pl.BlockSpec(memory_space=pltpu.VMEM)
+    shape, dma = jax.ShapeDtypeStruct, pltpu.SemaphoreType.DMA
+    tokens, width = x_all.shape
+    quarter, heads_width = attended.shape[1:]
     block = partial.shape[1:]
-    vmem = pl.BlockSpec(memory_space=pltpu.VMEM)
-    in_specs, out_specs = [ANYWHERE] * len(arrays), [ANYWHERE] * len(pairs) + [vmem]
-    shapes, scratch = shapes + [jax.ShapeDtypeStruct(block, jnp.float32)], scratch + sum_scratch(block)
-    if heads is not None:
-        arrays, in_specs, out_specs = arrays + [heads], in_specs + [vmem], out_specs + [vmem]
-        shapes.append(jax.ShapeDtypeStruct(heads.shape[1:], jnp.float32))
-        scratch = scratch + heads_scratch(heads.shape[1:])
+    part = width // cols
+    qkv_width = w_mine.shape[3]
+    lines = -(-2 * (width // 128) // 8) * 8
     return pl.pallas_call(
-        functools.partial(sum_trade_kernel, plans, heads is not None),
-        out_shape=shapes,
-        in_specs=in_specs,
-        out_specs=out_specs,
-        scratch_shapes=scratch,
+        back_kernel,
+        out_shape=[
+            shape(block, wide),
+            shape(grads.shape, low),
+            shape((2, 2, qkv_width, part), low),
+            shape((2, 2, heads_width, part), low),
+            shape((2, total, width), wide),
+            shape((cols, tokens // (2 * rows), part), low),
+            shape((total, lines, 128), wide),
+        ],
+        in_specs=[ANYWHERE] * 5 + [vmem] * len(rest),
+        out_specs=[vmem, ANYWHERE, vmem, vmem, vmem, vmem, ANYWHERE],
+        scratch_shapes=[
+            pltpu.VMEM(scores.shape, wide),
+            pltpu.VMEM((2, quarter, width), low),
+            pltpu.VMEM((plane, quarter, width), low),
+            pltpu.VMEM((1, total, 128), wide),
+            pltpu.VMEM((plane, total, 128), wide),
+            pltpu.VMEM((4,) + block, low),
+            pltpu.VMEM((tokens, 256), wide),
+            pltpu.VMEM((tokens, HEAD_DIM), wide),
+            pltpu.VMEM((tokens, heads_width), low),
+            pltpu.VMEM((tokens, qkv_width), low),
+            pltpu.VMEM((tokens, width), low),
+            pltpu.VMEM((8, tokens // (2 * rows), width), low),
+            pltpu.VMEM((4, tokens // (2 * rows), width), low),
+            pltpu.VMEM((2, tokens // (2 * rows), width), low),
+            pltpu.VMEM((tokens // (2 * rows), width), low),
+            pltpu.VMEM((3, tokens // (2 * rows), width), low),
+            pltpu.VMEM((cols, qkv_width, part), low),
+            pltpu.VMEM((cols, qkv_width, part), low),
+            pltpu.VMEM((cols, heads_width, part), low),
+            pltpu.VMEM((cols, heads_width, part), low),
+            pltpu.VMEM((cols, tokens // (2 * rows), part), low),
+            pltpu.VMEM((1, lines, 128), wide),
+            dma,
+            dma((total,)),
+            dma((total,)),
+            dma,
+            dma((plane,)),
+            dma((plane,)),
+            dma,
+            dma((40,)),
+            dma((cols,)),
+            dma((cols,)),
+            dma((2 * cols,)),
+            dma((cols,)),
+            dma((cols,)),
+            dma((2 * cols,)),
+            dma((8,)),
+            dma((4,)),
+            dma((2,)),
+            dma,
+            dma((8,)),
+            dma((2 * cols,)),
+            dma((cols,)),
+            dma((cols,)),
+            dma((2 * cols,)),
+            dma((6,)),
+        ]
+        + sum_scratch(block)
+        + [pltpu.VMEM((3 * cols,) + block, low)]
+        + sum_scratch(block)[5:]
+        + gather_sems(),
         compiler_params=pltpu.CompilerParams(
-            collective_id=number, has_side_effects=True, vmem_limit_bytes=48 * 2**20
+            collective_id=number, has_side_effects=True, vmem_limit_bytes=62 * 2**20
         ),
-        name="sum_trade" + str(number),
-    )(*arrays)
+        name="back" + str(number),
+    )(partial, mix_part, grads, scores, normed_all, *rest)
 
 
 def expert_kernel(
@@ -1336,7 +1467,6 @@
     rows_out,
     score_out,
     grads_out,
-    down_out,
     kept_in,
     kept_dye,
     kept_act,
@@ -1417,8 +1547,8 @@
         for chunk in range(chunks):
             lanes = slice(chunk * ff_width, (chunk + 1) * ff_width)
             grad = tn(act_all, all_of(kept_dye.at[:, :, lanes])).astype(low)
-            at = chunk * down_depth
-            down_out[:, at : at + down_depth, :] = grad.reshape(parts, down_depth, ff_width)
+            at = 2 * depth + chunk * down_depth
+            grads_out[:, at : at + down_depth, :] = grad.reshape(parts, down_depth, ff_width)
 
 
 def expert_pass(normed, cot, table, rank, mark, router, weights, slots):
@@ -1426,9 +1556,6 @@
     tokens, width = normed.shape
     low = jnp.bfloat16
     ff_width = weights.shape[2]
-    parts, depth, _ = weights.shape
-    gate_up = jax.ShapeDtypeStruct((parts, 2 * (width // parts), ff_width), low)
-    down = jax.ShapeDtypeStruct((parts, depth - gate_up.shape[1], ff_width), low)
     rows = pl.BlockSpec((tile, width), lambda i: (i, 0))
     whole = lambda a: pl.BlockSpec(
         a.shape, lambda i: (0,) * len(a.shape), pipeline_mode=pl.Buffered(1)
@@ -1440,8 +1567,7 @@
             jax.ShapeDtypeStruct((tokens, width), low),
             jax.ShapeDtypeStruct((tokens, width), low),
             jax.ShapeDtypeStruct((tiles, 8, tile), jnp.float32),
-            gate_up,
-            down,
+            jax.ShapeDtypeStruct(weights.shape, low),
         ],
         in_specs=[
             rows,
@@ -1456,8 +1582,7 @@
             rows,
             rows,
             pl.BlockSpec((1, 8, tile), lambda i: (i, 0, 0)),
-            whole(gate_up),
-            whole(down),
+            whole(weights),
         ],
         scratch_shapes=[
             pltpu.VMEM((tiles, slots, width), low),
@@ -1538,6 +1663,8 @@
     sin_table, cos_table = (
         table[:, 0] for table in angles(position.astype(jnp.float32), HEAD_DIM)
     )
+    doc_col = jnp.broadcast_to(doc_id[:, None], (group_tokens, 128))
+    doc_row = jnp.broadcast_to(doc_id[None, :], (8, group_tokens))
     cos_lanes = jnp.tile(cos_table, (1, 4))
     sin_lanes = jnp.tile(jnp.concatenate([-sin_table, sin_table], axis=1), (1, 2))
     (
@@ -1561,33 +1688,12 @@
         weights,
         (norm_gain[None], mix_gain[None]),
         (cos_lanes, sin_lanes),
-        (
-            jnp.broadcast_to(doc_id[:, None], (group_tokens, 128)),
-            jnp.broadcast_to(doc_id[None, :], (8, group_tokens)),
-        ),
+        (doc_col, doc_row),
         q_width,
     )
-    x_micro = x_micro.astype(jnp.float32)
-    w_mine = w_mine.reshape(model_width, qkv_width)
-    scale_m = lax.rsqrt(jnp.mean(x_micro * x_micro, axis=1, keepdims=True) + eps_norm)
-    normed_m = (x_micro * scale_m * norm_gain).astype(jnp.bfloat16)
-    sin_table, cos_table = sin_table[:, None], cos_table[:, None]
-    query = qkv[:, :q_width].reshape(group_tokens, group_size, HEAD_DIM)
-    key = qkv[:, q_width : q_width + HEAD_DIM]
-    value = qkv[:, q_width + HEAD_DIM :]
-    order = jnp.arange(group_tokens, dtype=jnp.int32)
-    allowed = (doc_id[:, None] == doc_id[None, :]) & (order[None, :] <= order[:, None])
-    raw_scores = jnp.einsum("qgd,kd->gqk", query, key, preferred_element_type=jnp.float32)
-    scores = jnp.where(allowed[None], raw_scores * attn_scale, -1e30)
-    probs = jax.nn.softmax(scores, axis=-1)
-    probs_low = probs.astype(jnp.bfloat16)
-    attended = attended.reshape(group_tokens, q_width)
     routes_all = (
         routes_all[:, :, :own_rows].transpose(0, 2, 1).reshape(device_count * own_rows, TOP)
     )
-    scale_two = lax.rsqrt(jnp.mean(mixed * mixed, axis=1, keepdims=True) + eps_norm)
-    unit_two = mixed * scale_two
-    normed_two = (unit_two * mix_gain).astype(jnp.bfloat16)
     expert_ids = jnp.arange(experts_all, dtype=jnp.int32)
 
     def gating(normed_rows, picks):
@@ -1595,8 +1701,7 @@
         logits = jnp.where(chosen, project(normed_rows, w_router), -jnp.inf)
         return jax.nn.softmax(logits, axis=-1)
 
-    normed_all = normed_all.reshape(device_count * own_rows, model_width)
-    cot_all = cot_all.reshape(device_count * own_rows, model_width)
+    normed_two = lax.dynamic_index_in_dim(normed_all, expert_at, 0, keepdims=False)
     gates_own = gating(normed_two, routes.reshape(own_rows, TOP))
 
     tile = col_count * own_rows
@@ -1605,9 +1710,9 @@
     here = jnp.any(routes_all == expert_at, axis=1).astype(jnp.int32).reshape(-1, tile)
     rank = jnp.where(here > 0, jnp.cumsum(here, axis=1, dtype=jnp.int32) - 1, -1)
     pad_experts = 128 - experts_all
-    mix_part, grad_rows_part, grad_gate_mine, grads, grads_down = expert_pass(
-        normed_all,
-        cot_all,
+    mix_part, grad_rows_part, grad_gate_mine, grads = expert_pass(
+        normed_all.reshape(device_count * own_rows, model_width),
+        cot_all.reshape(device_count * own_rows, model_width),
         jnp.pad(table.astype(jnp.float32), ((0, 0), (0, pad_experts))),
         jnp.broadcast_to(rank[:, None, :], (rank.shape[0], 8, tile)),
         (jnp.arange(128, dtype=jnp.int32) == expert_at).astype(jnp.float32)[None],
@@ -1623,141 +1728,49 @@
         ),
         (device_count, 8, 128),
     )
-    grad_gates, grads, grad_normed = sum_trade(
-        3,
+    w_out_mine = lax.dynamic_slice_in_dim(
+        w_out_all, (row_at * kv_here + half_at) * q_width, q_width
+    )
+    expert_mix, grads, qkv_sum, out_sum, router_grad, grad_input, lines = back(
+        1,
         grad_rows_part.reshape(device_count, own_rows, model_width),
-        (scores_send, everyone),
-        (grads, plane),
-    )
-    grad_gates = grad_gates[:, 0, :own_rows].T
-    chosen_own = jnp.any(
-        routes.reshape(own_rows, TOP)[:, :, None] == expert_ids[None, None, :], axis=1
-    )
-    grad_gates = jnp.where(chosen_own, grad_gates, 0.0)
-    grad_logits = gates_own * (
-        grad_gates - jnp.sum(gates_own * grad_gates, axis=1, keepdims=True)
-    )
-    grad_normed = grad_normed + jnp.dot(
-        grad_logits, w_router.astype(jnp.float32).T, precision=highest
-    )
-    mix_part_grad = jnp.sum(grad_normed * unit_two, axis=0)
-    grad_scaled = grad_normed * mix_gain
-    grad_mixed = masked_cot.reshape(own_rows, model_width).astype(jnp.float32) + scale_two * (
-        grad_scaled - unit_two * jnp.mean(grad_scaled * unit_two, axis=1, keepdims=True)
-    )
-    grad_branch = (resid_scale * grad_mixed).astype(jnp.bfloat16)
-
-    lines = lambda row: jnp.pad(row.reshape(-1, 128), ((0, 4), (0, 0)))[None]
-    branch_m, logits_plane, mix_parts = gather_plane(
-        4,
-        (grad_branch.reshape(micro_count, quarter, model_width), "micro", True),
-        (jnp.pad(grad_logits.T, ((0, 0), (0, 128 - own_rows)))[None], "all", True),
-        (lines(mix_part_grad), "all", True),
-    )
-    branch_m, grads_down = lax.optimization_barrier((branch_m, grads_down))
-    grads_down = spread_plane(grads_down)
+        mix_part.reshape(device_count, own_rows, model_width),
+        grads,
+        scores_send,
+        normed_all,
+        mixed,
+        masked_cot.reshape(own_rows, model_width),
+        jnp.pad(gates_own, ((0, 0), (0, pad_experts))),
+        jnp.pad(w_router.T, ((0, pad_experts), (0, 0))),
+        norm_gain[None],
+        mix_gain[None],
+        x_micro,
+        w_mine,
+        w_out_mine,
+        qkv,
+        attended,
+        cos_lanes,
+        sin_lanes,
+        doc_col,
+        doc_row,
+    )
+    layer_out = (mixed + resid_scale * expert_mix).astype(jnp.bfloat16)
     out_gate = grads[:, :slice_width].astype(jnp.float32)
     out_up = grads[:, slice_width : 2 * slice_width].astype(jnp.float32)
     out_down = jnp.concatenate(
         [
-            grads_down[:, at : at + down_slice]
-            for at in range(0, grads_down.shape[1], down_slice)
+            grads[:, at : at + down_slice]
+            for at in range(2 * slice_width, grads.shape[1], down_slice)
         ],
         axis=2,
     ).astype(jnp.float32)
-    low = jnp.bfloat16
-    left = logits_plane[:, :, :own_rows].transpose(1, 0, 2).reshape(experts_all, -1)
-    parts = []
-    for _ in range(3):
-        parts.append(left.astype(low))
-        left = left - parts[-1].astype(jnp.float32)
-    normed_plane = lax.dynamic_slice_in_dim(
-        normed_all, dp_at * plane_count * own_rows, plane_count * own_rows
-    )
-    router_part = jnp.sum(
-        jnp.dot(
-            jnp.concatenate(parts, axis=0), normed_plane, preferred_element_type=jnp.float32
-        ).reshape(3, experts_all, model_width),
-        axis=0,
-    )
-    mix_part_grad = jnp.sum(mix_parts, axis=0)
-    branch_m = branch_m.reshape(group_tokens, model_width)
-    w_out_mine = lax.dynamic_slice_in_dim(
-        w_out_all, (row_at * kv_here + half_at) * q_width, q_width
-    )
-    grad_att = (
-        jnp.dot(branch_m, w_out_mine.T, preferred_element_type=jnp.float32)
-        .astype(jnp.bfloat16)
-        .reshape(group_tokens, group_size, HEAD_DIM)
-    )
-    out_part = jnp.dot(attended.T, branch_m, preferred_element_type=jnp.float32)
-    grad_probs = jnp.einsum("qgd,kd->gqk", grad_att, value, preferred_element_type=jnp.float32)
-    grad_scores = probs * (grad_probs - jnp.sum(probs * grad_probs, axis=-1, keepdims=True))
-    grad_raw = (grad_scores * attn_scale).astype(jnp.bfloat16)
-    grad_query = jnp.einsum("gqk,kd->qgd", grad_raw, key, preferred_element_type=jnp.float32)
-    grad_key = jnp.einsum("gqk,qgd->kd", grad_raw, query, preferred_element_type=jnp.float32)
-    grad_value = jnp.einsum("gqk,qgd->kd", probs_low, grad_att, preferred_element_type=jnp.float32)
-    grad_qkv = jnp.concatenate(
-        [
-            rotate(grad_query, -sin_table, cos_table).reshape(group_tokens, q_width),
-            rotate(grad_key[:, None], -sin_table, cos_table)[:, 0],
-            grad_value,
-        ],
-        axis=1,
-    ).astype(jnp.bfloat16)
-    qkv_part = jnp.dot(grad_qkv.T, normed_m, preferred_element_type=jnp.float32)
-    heads_part = nt(grad_qkv, w_mine).astype(low)
-    qkv_part, out_part, router_grad, mix_grad, expert_mix, grad_normed_one = sum_trade(
-        5,
-        mix_part.reshape(device_count, own_rows, model_width),
-        (
-            qkv_part.astype(low).reshape(qkv_width, col_count, width_part).transpose(1, 0, 2),
-            ("col",),
-        ),
-        (
-            out_part.astype(low).reshape(q_width, col_count, width_part).transpose(1, 0, 2),
-            ("col",),
-        ),
-        (router_part[None], ("dp",)),
-        (mix_part_grad[None], ("dp",)),
-        heads=heads_part.reshape(2 * row_count, -1, model_width),
-    )
-    layer_out = (mixed + resid_scale * expert_mix).astype(jnp.bfloat16)
-    rows_each = grad_normed_one.shape[0]
-    first = (row_at * kv_here + half_at) * rows_each
-
-    def part_of(array):
-        return lax.dynamic_slice_in_dim(array, first, rows_each)
-
-    scale_one = part_of(scale_m)
-    unit_one = part_of(x_micro) * scale_one
-    norm_part = jnp.sum(grad_normed_one * unit_one, axis=0)
-    grad_scaled_one = grad_normed_one * norm_gain
-    grad_x = part_of(branch_m).astype(jnp.float32) * (1.0 / resid_scale) + scale_one * (
-        grad_scaled_one
-        - unit_one * jnp.mean(grad_scaled_one * unit_one, axis=1, keepdims=True)
-    )
-
-    def halves(part):
-        part = part.astype(jnp.float32)
-        return jnp.sum(part.reshape((micro_count, kv_here) + part.shape[1:]), axis=0).astype(low)
-
-    grad_input, qkv_sum, out_sum, norm_grad = trade(
-        6,
-        (
-            grad_x.astype(low).reshape(rows_each, col_count, width_part).transpose(1, 0, 2),
-            ("col",),
-        ),
-        (halves(qkv_part)[None], ("dp",)),
-        (halves(out_part)[None], ("dp",)),
-        (lines(norm_part), everyone),
-    )
     grad_input = grad_input.reshape(micro_count, tok_row, width_part).astype(jnp.float32)
     qkv_sum = jnp.sum(qkv_sum.astype(jnp.float32), axis=0)
     out_sum = jnp.sum(out_sum.astype(jnp.float32), axis=0)
     router_grad = jnp.sum(router_grad, axis=0).T
-    mix_grad = jnp.sum(mix_grad, axis=0).reshape(-1)[:model_width]
-    norm_grad = jnp.sum(norm_grad, axis=0).reshape(-1)[:model_width]
+    lines = jnp.sum(lines, axis=0)
+    norm_grad = lines[: model_width // 128].reshape(-1)
+    mix_grad = lines[model_width // 128 : 2 * (model_width // 128)].reshape(-1)
     grad_wq = qkv_sum[:, :q_width].reshape(-1, width_part).T
     grad_wk = qkv_sum[:, q_width : q_width + HEAD_DIM].reshape(-1, width_part).T
     grad_wv = qkv_sum[:, q_width + HEAD_DIM :].reshape(-1, width_part).T

time: 694 us -> 603 us (0.87)
  matrix products: 51.7 us -> 1.28 us
  other arithmetic: 36.9 us -> 22.4 us
  local copies, waits for them, and re-layouts: 41.5 us -> 31.7 us
  Pallas kernels: 548 us -> 539 us
    dot_general x10 -> x0, matrix products: 45.1 us -> none  [the longest x1 10.7 us: owned(): jnp.einsum('gqk,kd->qgd', grad_raw, key, preferred_element_type=jnp.float32)]
    pallas_call x4 -> x1, Pallas kernels: 270 us -> 261 us  [back(): pl.pallas_call(back_kernel, out_shape=[shape(block, wide), shape(grads.sh...]
    unnamed x62 -> x34, local copies, waits for them, and re-layouts: 18.3 us -> 10.3 us
  transfers between devices with their start and end apart: 1 -> 0, of which waited for: 0 -> 0; matrix products, arithmetic and copies ran while one was open for 13% -> 0% of each run, Pallas kernels for 18% -> 0%
where the time goes in v4:
time: 603 us; the launch traced here: 595 us
  Pallas kernels  539 us (89%)
  local copies, waits for them, and re-layouts  31.7 us (5%)
  other arithmetic  22.4 us (4%)
    pallas_call x1, Pallas kernels, back(): pl.pallas_call(back_kernel, out_shape=[shape(block, wide), shape(grads.sh...  261 us
    pallas_call x1, Pallas kernels, front(): pl.pallas_call(front_kernel, out_shape=[shape((tokens, width), low), shap...  221 us
    pallas_call x1, Pallas kernels, expert_pass(): pl.pallas_call(expert_kernel, grid=(tiles,), out_shape=[jax.ShapeDtypeStr...  56.7 us

profile of v4, /device:TPU:0, one launch (start us, length us, event | category | flops | bytes accessed | tf_op | source)
XLA Modules:
  0.0 595.5 jit_solution(6418597260922872085)
XLA Ops:
  3.6 1.3 broadcast_in_dim.35.gain_one
  4.9 1.3 broadcast_in_dim.36.gain_two
  8.3 1.0 copy.53
  9.3 1.0 copy.54
  10.4 1.1 fusion.6
  11.5 0.9 copy.58.sin_table
  12.4 1.8 broadcast_multiply_fusion
  14.4 1.1 copy.55
  15.5 0.9 broadcast_in_dim.39.doc_col
  16.4 1.0 tile.8
  17.5 0.9 copy.57.cos_table
  18.4 1.7 pad.32.router_t
  20.0 1.1 copy.62
  22.3 1.1 copy-done.4
  23.5 2.1 copy-done
  25.7 221.3 %front0.1 = (bf16[768,1536]{1,0:T(8,128)(2,1)}, bf16[4,2,192,320]{3,2,1,0:T(8,128)(2,1)}, bf16[1536,1536]{1,0:T(8,128)(2,1)}, s32[32,8,128]{2,1,0:T(8,128)}, bf1...) custom-call(bf16[2,192,384]{2,1,0:T(8,128)(2,1)} %x.13, ...), custom_call_target="tpu_custom_call" | custom-call | tf_op jit(solution)/shard_map/front0/pallas_call | solution.py:841
  246.9 1.0 compare_reduce_fusion
  247.9 0.9 slice_bitcast_fusion
  250.9 1.3 fusion.12
  254.4 1.9 constant_dynamic-slice_fusion.w_out_mine
  256.3 1.3 pad_convert_fusion.table
  257.6 56.7 %expert_pass.1 = (bf16[3072,1536]{1,0:T(8,128)(2,1)}, bf16[3072,1536]{1,0:T(8,128)(2,1)}, f32[8,8,384]{2,1,0:T(8,128)}, bf16[16,288,512]{2,1,0:T(8,128)(2,1)}) custom-call(bf16[3072,1536]{1,0:T(8,128)(2,1)} %bitcast.64, bf16[3072,1536]{1,0:T(8,128)(2,1)} %bitcast.89, f32[3072,128]{1,0:T(8,128)} %pad_convert_fusion.table, ...), custom_call_target="tpu_custom_call" | custom-call | flops 22000001024 | bytes 50000000 | tf_op jit(solution)/shard_map/expert_pass/pallas_call | solution.py:1563
  314.3 0.9 slice_reduce_fusion.1
  316.0 260.9 %back1.1 = (f32[96,1536]{1,0:T(8,128)}, bf16[16,288,512]{2,1,0:T(8,128)(2,1)}, bf16[2,2,320,384]{3,2,1,0:T(8,128)(2,1)}, bf16[2,2,192,384]{3,2,1,0:T(8,128)(2,1)...) custom-call(bf16[32,96,1536]{2,1,0:T(8,128)(2,1)} %bitcast.66, ...), custom_call_target="tpu_custom_call" | custom-call | tf_op jit(solution)/shard_map/back1/pallas_call | solution.py:1386
  576.9 2.0 add_convert_fusion
  578.9 1.0 reduce_sum.66
  579.9 1.7 reduce_sum.69
  582.3 1.8 bitcast_convert_fusion
  585.2 1.1 copy.67
  587.9 1.7 fusion.9
  589.6 2.1 maximum_convert_fusion
  591.7 3.6 slice_convert_fusion
  (72 shorter events, 14.9 us)
Async XLA Ops:
  0.6 13.5 %copy-start.8 = (bf16[384,384]{1,0:T(8,128)(2,1)S(1)}, bf16[384,384]{1,0:T(8,128)(2,1)}, u32[]{:S(2)}) copy-start(bf16[384,384]{1,0:T(8,128)(2,1)} %param.17) | copy-start | bytes 884740
  14.2 7.8 %copy-start.2 = (bf16[16,96,512]{2,1,0:T(8,128)(2,1)S(1)}, bf16[16,96,512]{2,1,0:T(8,128)(2,1)}, u32[]{:S(2)}) copy-start(bf16[16,96,512]{2,1,0:T(8,128)(2,1)} %param.23) | copy-start | bytes 4718596
  16.4 5.7 copy-start.3
  22.0 1.4 copy-start.4
  23.5 2.2 copy-start
  25.7 225.2 %copy-start.6 = (bf16[1536,32]{0,1:T(8,128)(2,1)S(1)}, bf16[1536,32]{0,1:T(8,128)(2,1)}, u32[]{:S(2)}) copy-start(bf16[1536,32]{0,1:T(8,128)(2,1)} %param.22) | copy-start | bytes 294916
  316.0 260.9 %copy-start.1 = (f32[96,1536]{1,0:T(8,128)S(1)}, f32[96,1536]{1,0:T(8,128)}, u32[]{:S(2)}) copy-start(f32[96,1536]{1,0:T(8,128)} %get-tuple-element.33.mixed) | copy-start | bytes 1769476
  576.9 7.2 %copy-start.7 = (bf16[2,2,192,384]{3,2,1,0:T(8,128)(2,1)S(1)}, bf16[2,2,192,384]{3,2,1,0:T(8,128)(2,1)}, u32[]{:S(2)}) copy-start(bf16[2,2,192,384]{3,2,1,0:T(8,128)(2,1)} %get-tuple-element.51) | copy-start | bytes 1769476
  576.9 8.1 %copy-start.5 = (bf16[2,2,320,384]{3,2,1,0:T(8,128)(2,1)S(1)}, bf16[2,2,320,384]{3,2,1,0:T(8,128)(2,1)}, u32[]{:S(2)}) copy-start(bf16[2,2,320,384]{3,2,1,0:T(8,128)(2,1)} %get-tuple-element.50) | copy-start | bytes 2949124
  585.2 6.5 %slice-start = ((s8[4718592]{0:T(1024)(128)(4,1)}), s8[524288]{0:T(1024)(128)(4,1)S(1)}, s32[]{:S(2)}) async-start(s8[4718592]{0:T(1024)(128)(4,1)} %bitcast.67), calls=%async_computation | async-start | bytes 1048576
  587.9 3.8 slice-start.1

commit v5 on v4

--- a/solution.py
+++ b/solution.py
@@ -449,17 +449,25 @@
     return row, across, beside
 
 
+def col_peers():
+    col, cols = lax.axis_index("col"), lax.axis_size("col")
+    two_on = (col + 2) % cols
+    near = col + 1 - 2 * (col % 2)
+    return two_on, near, (col, two_on, near, (near + 2) % cols)
+
+
 def gather_line(source, target, sems, copies):
     local_sem, send_sem, col_sem, dp_sem, across_sem, beside_sem = sems
     row, across, beside = row_peers()
     rows, cols = lax.axis_size("row"), lax.axis_size("col")
-    col, dp = lax.axis_index("col"), lax.axis_index("dp")
+    dp = lax.axis_index("dp")
     other = 1 - dp
+    two_on, near, order = col_peers()
     far = (beside + rows // 2) % rows
     sent = []
 
     def block_of(dp_from, row_from, step):
-        return (dp_from * rows + row_from) * cols + (col + cols - step) % cols
+        return (dp_from * rows + row_from) * cols + order[step]
 
     def arrival(block, sem):
         pltpu.make_async_copy(target.at[block], target.at[block], sem).wait()
@@ -474,14 +482,16 @@
 
     def begin():
         own.start()
-        for step in range(1, cols):
-            pass_on(source.at[0], me, col_sem.at[step], {"col": (col + step) % cols})
+        pass_on(source.at[0], me, col_sem.at[1], {"col": two_on})
+        pass_on(source.at[0], me, col_sem.at[2], {"col": near})
 
     def line(step):
         block = block_of(dp, row, step)
         part = source.at[0] if step == 0 else target.at[block]
         if step > 0:
             arrival(block, col_sem.at[step])
+        if step == 1:
+            pass_on(part, block, col_sem.at[3], {"col": near})
         pass_on(part, block, dp_sem.at[step], {"dp": other})
         pass_on(part, block, across_sem.at[step], {"row": across})
         pass_on(part, block, beside_sem.at[step], {"row": beside})
@@ -489,18 +499,15 @@
     def side(step):
         block = block_of(other, row, step)
         arrival(block, dp_sem.at[step])
-        if step < 2:
-            pass_on(target.at[block], block, across_sem.at[cols + step], {"row": across})
         pass_on(target.at[block], block, beside_sem.at[cols + step], {"row": beside})
         block = block_of(dp, across, step)
         arrival(block, across_sem.at[step])
-        if step >= 2:
-            pass_on(target.at[block], block, dp_sem.at[cols + step], {"dp": other})
+        pass_on(target.at[block], block, dp_sem.at[cols + step], {"dp": other})
         pass_on(target.at[block], block, beside_sem.at[2 * cols + step], {"row": beside})
 
     def corner(step):
         block = block_of(other, across, step)
-        arrival(block, (across_sem if step < 2 else dp_sem).at[cols + step])
+        arrival(block, dp_sem.at[cols + step])
         pass_on(target.at[block], block, beside_sem.at[3 * cols + step], {"row": beside})
 
     def finish():
@@ -573,26 +580,57 @@
     w_out,
     picks,
     cot,
-    weights,
+    w_gate,
+    w_up,
+    w_down,
     gain_one,
     gain_two,
     cos_table,
     sin_table,
     doc_col,
     doc_row,
+    router_t,
+    table,
     x_all,
     w_mine,
-    w_out_all,
-    picks_all,
+    w_out_mine,
     cot_all,
     normed_all,
-    weights_own,
     qkv,
     attended,
     mixed,
+    gates_own,
+    rows_part,
+    mix_part,
+    scores,
+    grads_gu,
+    grads_down,
+    w_out_all,
+    picks_all,
     x_own,
     att_own,
     normed_two,
+    gate_up,
+    down,
+    down_grad,
+    pool_rows,
+    pool_cots,
+    kept_in,
+    kept_dy,
+    kept_dye,
+    kept_act,
+    kept_gate,
+    kept_up,
+    gate_proj,
+    up_proj,
+    kept_weight,
+    ranks,
+    upper,
+    load_sem,
+    store_sem,
+    grad_local,
+    grad_send,
+    grad_recv,
     local_sem,
     send_sem,
     x_sem,
@@ -633,28 +671,60 @@
         copy.start()
         locals_.append(copy)
 
-    def ship(first, last):
+    slice_rows, ff_width = w_gate.shape[1:]
+    down_rows = w_down.shape[1]
+    chunks = w_down.shape[2] // ff_width
+
+    def weight_parts(to, at):
+        parts = [
+            (w_gate.at[to], gate_up.at[at, 0:slice_rows]),
+            (w_up.at[to], gate_up.at[at, slice_rows : 2 * slice_rows]),
+        ]
+        for chunk in range(chunks):
+            parts.append(
+                (
+                    w_down.at[to, :, chunk * ff_width : (chunk + 1) * ff_width],
+                    down.at[at, chunk * down_rows : (chunk + 1) * down_rows],
+                )
+            )
+        return parts
+
+    def ship(first, last, which=range(2)):
         for step in range(first, last):
             to = (me + step) % size
-            moved.append(
-                send(
-                    weights.at[to],
-                    weights_own.at[me],
-                    ship_send.at[step],
-                    ship_recv.at[step],
-                    device_at(plane, to),
+            for part in which:
+                source, target = weight_parts(to, me)[part]
+                moved.append(
+                    send(
+                        source,
+                        target,
+                        ship_send.at[part, step],
+                        ship_recv.at[part, step],
+                        device_at(plane, to),
+                    )
                 )
-            )
+
+    def shipped(which):
+        for step in range(1, size):
+            for part in which:
+                arrival(
+                    weight_parts(me, (me + size - step) % size)[part][1], ship_recv.at[part, step]
+                )
 
     def origin(step):
         return (col + cols - step) % cols
+
+    two_on, near, order = col_peers()
 
     micro, depth, width = x.shape
     quarter = depth // cols
     half_depth = w_out.shape[1]
 
+    def lanes_of(at):
+        return pl.ds(pl.multiple_of(at * width, width), width)
+
     def lanes(step):
-        return pl.ds(pl.multiple_of(origin(step) * width, width), width)
+        return lanes_of(order[step])
 
     def x_at(row_from, step):
         return x_all.at[pl.ds(pl.multiple_of(row_from * depth, depth), depth), lanes(step)]
@@ -664,12 +734,14 @@
         return w_out_all.at[pl.ds(first, half_depth), lanes(step)]
 
     def own_at(m, step):
-        return x_own.at[pl.ds(m * quarter, quarter), lanes(step)]
+        return x_own.at[pl.ds(m * quarter, quarter), lanes_of(origin(step))]
 
     my_x = x_at(row, 0)
     for step in range(1, cols):
         to = (col + step) % cols
-        pass_on(x.at[to // 2], my_x, x_sem.at[step], {"col": to})
+        if step < 3:
+            peer = (two_on, near)[step - 1]
+            pass_on(x.at[peer // 2], my_x, x_sem.at[step], {"col": peer})
         pass_on(w_qkv.at[to % 2, dp], w_mine.at[col, dp], q_sem.at[step], {"col": to})
     local(x.at[col // 2], my_x)
     local(w_qkv.at[col % 2], w_mine.at[col])
@@ -679,7 +751,9 @@
     pass_on(x.at[col // 2], my_x, x_sem.at[2 * cols], {"row": beside})
     for step in range(1, cols):
         to = (col + step) % cols
-        pass_on(w_out.at[dp], out_at(row, 0, dp), o_sem.at[step], {"col": to})
+        if step < 3:
+            peer = (two_on, near)[step - 1]
+            pass_on(w_out.at[dp], out_at(row, 0, dp), o_sem.at[step], {"col": peer})
         first = pl.multiple_of(to * quarter, quarter)
         for m in range(micro):
             pass_on(
@@ -696,6 +770,8 @@
     for step in range(1, cols):
         part = x_at(row, step)
         arrival(part, x_sem.at[step])
+        if step == 1:
+            pass_on(part, part, x_sem.at[3], {"col": near})
         pass_on(part, part, x_sem.at[cols + step], {"row": across})
         pass_on(part, part, x_sem.at[2 * cols + step], {"row": beside})
         part = w_mine.at[origin(step), dp]
@@ -708,19 +784,21 @@
     for step in range(1, cols):
         part = out_at(row, step, dp)
         arrival(part, o_sem.at[step])
+        if step == 1:
+            pass_on(part, part, o_sem.at[3], {"col": near})
         pass_on(part, part, o_sem.at[cols + step], {"dp": other})
         pass_on(part, part, o_sem.at[2 * cols + step], {"row": across})
         pass_on(part, part, o_sem.at[4 * cols + step], {"row": beside})
     picks_line[0]()
     cot_line[0]()
-    own = pltpu.make_async_copy(weights.at[me], weights_own.at[me], ship_local)
-    own.start()
+    for source, target in weight_parts(me, me):
+        local(source, target)
     for step in range(1, cols):
         arrival(w_mine.at[origin(step), other], q_sem.at[cols + step])
     for at, row_from in enumerate((beside, far)):
         for step in range(cols):
             arrival(x_at(row_from, step), x_sem.at[(2 + at) * cols + step])
-    for copy in locals_:
+    for copy in locals_[:6]:
         copy.wait()
 
     tokens, model_width = x_all.shape
@@ -812,6 +890,13 @@
     for step in range(cols):
         line(step)
     ship(5 + 2 * cols, size)
+    ship(1, size, range(2, 2 + chunks))
+    logits = jnp.where(table[...] > 0, nt(normed_two[0], router_t[...]), -jnp.inf)
+    raised = jnp.exp(logits - jnp.max(logits, axis=1, keepdims=True))
+    gates_own[...] = raised / jnp.sum(raised, axis=1, keepdims=True)
+    w_out_mine[...] = w_out_all[
+        pl.ds(pl.multiple_of((row * 2 + col % 2) * kv_at, kv_at), kv_at), :
+    ]
     for step in range(cols):
         picks_line[3](step)
         cot_line[3](step)
@@ -821,61 +906,286 @@
     picks_line[4]()
     cot_line[4]()
     finish()
-    own.wait()
-    for copy in moved[: size - 1]:
+
+    everyone = ("dp", "row", "col")
+    expert = place_in(everyone)
+    tiles, slots = kept_in.shape[0], kept_in.shape[1]
+    padded = pool_rows.shape[2]
+    block_rows = micro * quarter
+    span = cols * padded
+    pool_rows[...] = jnp.zeros_like(pool_rows)
+    pool_cots[...] = jnp.zeros_like(pool_cots)
+    upper[...] = (
+        lax.broadcasted_iota(jnp.int32, upper.shape, 0)
+        < lax.broadcasted_iota(jnp.int32, upper.shape, 1)
+    ).astype(low)
+
+    def pool(tile, slot):
+        for at, (source, target) in enumerate(((normed_all, pool_rows), (cot_all, pool_cots))):
+            yield pltpu.make_async_copy(
+                source.at[pl.ds(tile * cols, cols)],
+                target.at[slot, :, 0:block_rows],
+                load_sem.at[at, slot],
+            )
+
+    for copy in pool(0, 0):
+        copy.start()
+    slot_of = lax.broadcasted_iota(jnp.int32, (slots, span), 0)
+
+    def picked(tile):
+        return slot_of == ranks[tile][0:1, :]
+
+    @pl.loop(0, tiles)
+    def _(tile):
+        slot = tile % 2
+        for copy in pool(tile, slot):
+            copy.wait()
+
+        @pl.when(tile + 1 < tiles)
+        def _():
+            for copy in pool(tile + 1, 1 - slot):
+                copy.start()
+
+        rows_here = pool_rows[slot].reshape(span, model_width)
+        logits = nt(router_t[...], rows_here)[0 : picks_all.shape[0], :]
+        ids = lax.broadcasted_iota(jnp.int32, logits.shape, 0)
+        names = jnp.concatenate([picks_all[tile * cols + at] for at in range(cols)], axis=1)
+        chosen = ids == names[0:1, :]
+        for choice in range(1, names.shape[0]):
+            chosen = chosen | (ids == names[choice : choice + 1, :])
+        logits = jnp.where(chosen, logits, -1e30)
+        raised = jnp.where(chosen, jnp.exp(logits - jnp.max(logits, axis=0, keepdims=True)), 0.0)
+        total = jnp.sum(raised, axis=0, keepdims=True)
+        mine = ids == expert
+        gate = jnp.sum(jnp.where(mine, raised, 0.0), axis=0, keepdims=True) / jnp.where(
+            total > 0, total, 1.0
+        )
+        here = jnp.max(jnp.where(mine & chosen, 1.0, 0.0), axis=0, keepdims=True)
+        before = project(jnp.broadcast_to(here, (16, span)).astype(low), upper[...])[0:1, :]
+        rank = jnp.where(here > 0, before.astype(jnp.int32), -1)
+        ranks[tile] = jnp.broadcast_to(rank, ranks.shape[1:])
+        select = slot_of == rank
+        kept_weight[tile] = jnp.broadcast_to(
+            jnp.sum(jnp.where(select, gate, 0.0), axis=1, keepdims=True), kept_weight.shape[1:]
+        )
+        select = select.astype(low)
+        kept_in[tile] = project(select, rows_here).astype(low)
+        kept_dy[tile] = project(select, pool_cots[slot].reshape(span, model_width)).astype(low)
+
+    shipped(range(2))
+    for copy in locals_[6:]:
+        copy.wait()
+    gate_w = gate_up[:, 0:slice_rows, :].reshape(model_width, ff_width)
+    up_w = gate_up[:, slice_rows : 2 * slice_rows, :].reshape(model_width, ff_width)
+
+    def down_w(chunk):
+        at = chunk * down_rows
+        return down[:, at : at + down_rows, :].reshape(ff_width, ff_width)
+
+    def two(ref, pair):
+        part = ref[pl.ds(2 * pair, 2)]
+        return part.reshape(2 * slots, part.shape[2])
+
+    def put(ref, pair, value):
+        ref[pl.ds(2 * pair, 2)] = value.reshape(2, slots, value.shape[1])
+
+    @pl.loop(0, tiles // 2)
+    def _(pair):
+        rows_in = two(kept_in, pair)
+        gate_value = project(rows_in, gate_w)
+        up_value = project(rows_in, up_w)
+        put(gate_proj, pair, gate_value)
+        put(up_proj, pair, up_value)
+        put(kept_act, pair, (gate_value / (1.0 + jnp.exp(-gate_value)) * up_value).astype(low))
+        weight = two(kept_weight, pair)[:, 0:1]
+        grad_mix = resid_scale * two(kept_dy, pair).astype(jnp.float32)
+        put(kept_dye, pair, (weight * grad_mix).astype(low))
+
+    def all_of(ref):
+        value = ref[...]
+        return value.reshape(tiles * slots, value.shape[2])
+
+    act_all = all_of(kept_act)
+    for chunk in range(chunks):
+        grad = tn(act_all, all_of(kept_dye.at[:, :, chunk * ff_width : (chunk + 1) * ff_width]))
+        at = chunk * down_rows
+        down_grad[:, at : at + down_rows, :] = grad.astype(low).reshape(size, down_rows, ff_width)
+    home = pltpu.make_async_copy(down_grad.at[me], grads_down.at[me], grad_local)
+    home.start()
+    given = []
+    for step in range(1, size):
+        to = (me + step) % size
+        given.append(
+            send(
+                down_grad.at[to],
+                grads_down.at[me],
+                grad_send.at[step],
+                grad_recv.at[step],
+                device_at(plane, to),
+            )
+        )
+    shipped(range(2, 2 + chunks))
+
+    def spill(tile, slot):
+        for at, (source, target) in enumerate(((pool_rows, rows_part), (pool_cots, mix_part))):
+            yield pltpu.make_async_copy(
+                source.at[slot, :, 0:block_rows],
+                target.at[pl.ds(tile * cols, cols)],
+                store_sem.at[at, slot],
+            )
+
+    @pl.loop(0, tiles // 2)
+    def _(pair):
+        act = two(kept_act, pair)
+        grad_out = two(kept_dye, pair)
+        gate_value, up_value = two(gate_proj, pair), two(up_proj, pair)
+        weight = two(kept_weight, pair)[:, 0:1]
+        score = jnp.zeros((2 * slots, 1), jnp.float32)
+        grad_act = jnp.zeros((2 * slots, ff_width), jnp.float32)
+
+        @pl.when(pair > 0)
+        def _():
+            for at in range(2):
+                for copy in spill(2 * pair - 2 + at, at):
+                    copy.wait()
+
+        selects = [picked(2 * pair + at).astype(low) for at in range(2)]
+        for chunk in range(chunks):
+            lanes = slice(chunk * ff_width, (chunk + 1) * ff_width)
+            part = down_w(chunk)
+            out = project(act, part).astype(low).astype(jnp.float32)
+            grad_mix = resid_scale * kept_dy[pl.ds(2 * pair, 2), :, lanes].reshape(
+                2 * slots, ff_width
+            ).astype(jnp.float32)
+            score = score + jnp.sum(grad_mix * out, axis=1, keepdims=True)
+            mixed_rows = (weight * out).astype(low)
+            for at in range(2):
+                pool_cots[at, :, :, lanes] = (
+                    tn(selects[at], mixed_rows[at * slots : (at + 1) * slots])
+                    .astype(low)
+                    .reshape(cols, padded, ff_width)
+                )
+            grad_act = grad_act + nt(grad_out[:, lanes], part)
+        sigmoid = 1.0 / (1.0 + jnp.exp(-gate_value))
+        grad_gate = (
+            grad_act * up_value * (sigmoid + gate_value * sigmoid * (1.0 - sigmoid))
+        ).astype(low)
+        grad_up = (grad_act * (gate_value * sigmoid)).astype(low)
+        put(kept_gate, pair, grad_gate)
+        put(kept_up, pair, grad_up)
+        grad_in = (nt(grad_gate, gate_w) + nt(grad_up, up_w)).astype(low)
+        for at in range(2):
+            tile = 2 * pair + at
+            part = slice(at * slots, (at + 1) * slots)
+            pool_rows[at] = (
+                tn(selects[at], grad_in[part]).astype(low).reshape(cols, padded, model_width)
+            )
+            line_of = jnp.sum(jnp.where(picked(tile), score[part], 0.0), axis=0, keepdims=True)
+            for block in range(cols):
+                scores[tile * cols + block] = jnp.broadcast_to(
+                    line_of[:, block * padded : (block + 1) * padded], scores.shape[1:]
+                )
+            for copy in spill(tile, at):
+                copy.start()
+
+    rows_all = all_of(kept_in)
+    for at, kept in ((0, kept_gate), (slice_rows, kept_up)):
+        grad = tn(rows_all, all_of(kept)).astype(low)
+        grads_gu[:, at : at + slice_rows, :] = grad.reshape(size, slice_rows, ff_width)
+    for at in range(2):
+        for copy in spill(tiles - 2 + at, at):
+            copy.wait()
+    home.wait()
+    for copy in given:
+        copy.wait()
+    for copy in moved + copies + sent:
         copy.wait_send()
-    for copy in moved[size - 1 :]:
-        copy.wait()
-    for copy in copies + sent:
-        copy.wait_send()
-
-
-def front(number, x, w_qkv, w_out, picks, cot, weights, gains, tables, docs, heads_width):
+
+
+def front(number, x, w_qkv, w_out, picks, cot, experts, gains, tables, docs, routing, heads_width):
     cols, rows = lax.axis_size("col"), lax.axis_size("row")
     total, plane = group_size_of(("dp", "row", "col")), group_size_of(("row", "col"))
     micro, depth, part_width = x.shape
     width, tokens, low = part_width * cols, depth * rows, jnp.bfloat16
+    wide = jnp.float32
     quarter = depth // cols
+    _, slice_rows, ff_width = experts[0].shape
+    down_depth = slice_rows * plane // ff_width * experts[2].shape[1]
+    tiles = total // cols
+    slots = cols * micro * (quarter * 3 // 8)
     vmem = pl.BlockSpec(memory_space=pltpu.VMEM)
-    shape = jax.ShapeDtypeStruct
+    shape, dma = jax.ShapeDtypeStruct, pltpu.SemaphoreType.DMA
+    pool = pltpu.VMEM((2, cols, 128, width), low)
     return pl.pallas_call(
         front_kernel,
         out_shape=[
             shape((tokens, width), low),
             shape((cols,) + w_qkv.shape[1:], low),
-            shape((rows * 2 * w_out.shape[1], width), low),
-            shape((total,) + picks.shape, picks.dtype),
+            shape((heads_width, width), low),
             shape((total,) + cot.shape, low),
             shape((total,) + cot.shape, low),
-            shape(weights.shape, low),
             shape((tokens, w_qkv.shape[3]), low),
             shape((plane, quarter, heads_width), low),
-            shape((micro * quarter, width), jnp.float32),
+            shape((micro * quarter, width), wide),
+            shape((micro * quarter, 128), wide),
+            shape((total,) + cot.shape, low),
+            shape((total,) + cot.shape, low),
+            shape((total, 8, 128), wide),
+            shape((plane, 2 * slice_rows, ff_width), low),
+            shape((plane, down_depth, ff_width), low),
         ],
-        in_specs=[ANYWHERE] * 6 + [vmem] * 6,
-        out_specs=[vmem] * 3 + [ANYWHERE] * 4 + [vmem] * 3,
+        in_specs=[ANYWHERE] * 8 + [vmem] * 8,
+        out_specs=[vmem] * 3
+        + [ANYWHERE] * 2
+        + [vmem] * 4
+        + [ANYWHERE] * 2
+        + [vmem] * 2
+        + [ANYWHERE],
         scratch_shapes=[
+            pltpu.VMEM((rows * 2 * w_out.shape[1], width), low),
+            pltpu.VMEM((total,) + picks.shape, picks.dtype),
             pltpu.VMEM((micro * quarter, width), low),
             pltpu.VMEM((plane, quarter, heads_width), low),
             pltpu.VMEM((1, micro * quarter, width), low),
-            pltpu.SemaphoreType.DMA((8,)),
-            pltpu.SemaphoreType.DMA((72,)),
-            pltpu.SemaphoreType.DMA((4 * cols,)),
-            pltpu.SemaphoreType.DMA((2 * cols,)),
-            pltpu.SemaphoreType.DMA((8 * cols,)),
-            pltpu.SemaphoreType.DMA((micro * cols,)),
-            pltpu.SemaphoreType.DMA((plane,)),
-            pltpu.SemaphoreType.DMA((plane,)),
-            pltpu.SemaphoreType.DMA,
-            pltpu.SemaphoreType.DMA((plane,)),
-            pltpu.SemaphoreType.DMA((plane,)),
+            pltpu.VMEM((plane, 2 * slice_rows, ff_width), low),
+            pltpu.VMEM((plane, down_depth, ff_width), low),
+            pltpu.VMEM((plane, down_depth, ff_width), low),
+            pool,
+            pool,
+            pltpu.VMEM((tiles, slots, width), low),
+            pltpu.VMEM((tiles, slots, width), low),
+            pltpu.VMEM((tiles, slots, width), low),
+            pltpu.VMEM((tiles, slots, ff_width), low),
+            pltpu.VMEM((tiles, slots, ff_width), low),
+            pltpu.VMEM((tiles, slots, ff_width), low),
+            pltpu.VMEM((tiles, slots, ff_width), wide),
+            pltpu.VMEM((tiles, slots, ff_width), wide),
+            pltpu.VMEM((tiles, slots, 128), wide),
+            pltpu.VMEM((tiles, 8, cols * 128), jnp.int32),
+            pltpu.VMEM((cols * 128, cols * 128), low),
+            dma((2, 2)),
+            dma((2, 2)),
+            dma,
+            dma((plane,)),
+            dma((plane,)),
+            dma((12,)),
+            dma((72,)),
+            dma((4 * cols,)),
+            dma((2 * cols,)),
+            dma((8 * cols,)),
+            dma((micro * cols,)),
+            dma((plane,)),
+            dma((plane,)),
+            dma,
+            dma((8, plane)),
+            dma((8, plane)),
         ]
         + gather_sems() * 3,
         compiler_params=pltpu.CompilerParams(
-            collective_id=number, has_side_effects=True, vmem_limit_bytes=56 * 2**20
+            collective_id=number, has_side_effects=True, vmem_limit_bytes=63 * 2**20
         ),
         name="front" + str(number),
-    )(x, w_qkv, w_out, picks[None], cot[None], weights, *gains, *tables, *docs)
+    )(x, w_qkv, w_out, picks[None], cot[None], *experts, *gains, *tables, *docs, *routing)
 
 
 def sum_scratch(block):
@@ -915,6 +1225,7 @@
     col, dp = lax.axis_index("col"), lax.axis_index("dp")
     other = 1 - dp
     low = jnp.bfloat16
+    two_on, beside_col, _ = col_peers()
     sent = []
 
     def pass_on(src, dst, sem, peer):
@@ -976,16 +1287,19 @@
         return value
 
     def spread():
-        for step in range(cols - 1, 0, -1):
-            z = (col + step) % cols
-            passed[3 * cols + z] = chip_total(z).astype(low)
-            pass_on(passed.at[3 * cols + z], last.at[step], col_sem.at[step], {"col": z})
+        for at, z in enumerate((beside_col, (beside_col + 2) % cols)):
+            passed[3 * cols + at] = chip_total(z).astype(low)
+            pass_on(passed.at[3 * cols + at], last.at[at], col_sem.at[at], {"col": beside_col})
+        value = chip_total(two_on)
+        arrival(last.at[1], col_sem.at[1])
+        passed[3 * cols + 2] = (value + last[1].astype(jnp.float32)).astype(low)
+        pass_on(passed.at[3 * cols + 2], last.at[2], col_sem.at[2], {"col": two_on})
 
     def total():
         value = chip_total(col)
-        for step in range(1, cols):
-            arrival(last.at[step], col_sem.at[step])
-            value = value + last[step].astype(jnp.float32)
+        for at, sem in ((0, 0), (2, 2)):
+            arrival(last.at[at], col_sem.at[sem])
+            value = value + last[at].astype(jnp.float32)
         return value
 
     return start, diagonal, middle, spread, total
@@ -1167,8 +1481,8 @@
     def origin(step):
         return (col + cols - step) % cols
 
-    for step in range(1, cols):
-        to = (col + step) % cols
+    two_on, near, order = col_peers()
+    for step, to in ((1, two_on), (2, near)):
         pass_on(branch.at[to // 2], branch_all.at[plane_me], branch_col.at[step], {"col": to})
         pass_on(logits.at[0], logits_all.at[plane_me], logits_col.at[step], {"col": to})
     keep(branch.at[col // 2], branch_all.at[plane_me])
@@ -1179,22 +1493,24 @@
     )
     for step in range(cols):
         for mine, target, col_sem, side_sem, core_sem in plans:
-            part = target.at[row * cols + origin(step)]
+            part = target.at[row * cols + order[step]]
             if step > 0:
                 arrival(part, col_sem.at[step])
+            if step == 1:
+                pass_on(part, part, col_sem.at[3], {"col": near})
             source = mine if step == 0 else part
             pass_on(source, part, side_sem.at[step], {"row": across})
             pass_on(source, part, core_sem.at[step], {"row": beside})
     ship(5, 11)
     for step in range(cols):
         for mine, target, col_sem, side_sem, core_sem in plans:
-            part = target.at[across * cols + origin(step)]
+            part = target.at[across * cols + order[step]]
             arrival(part, side_sem.at[step])
             pass_on(part, part, core_sem.at[cols + step], {"row": beside})
     for at, row_from in enumerate((beside, far)):
         for step in range(cols):
             for mine, target, col_sem, side_sem, core_sem in plans:
-                arrival(target.at[row_from * cols + origin(step)], core_sem.at[at * cols + step])
+                arrival(target.at[row_from * cols + order[step]], core_sem.at[at * cols + step])
     for copy in locals_:
         copy.wait()
     for copy in copies:
@@ -1455,150 +1771,6 @@
     )(partial, mix_part, grads, scores, normed_all, *rest)
 
 
-def expert_kernel(
-    normed,
-    cot,
-    table,
-    rank,
-    mark,
-    router,
-    weights,
-    mix_out,
-    rows_out,
-    score_out,
-    grads_out,
-    kept_in,
-    kept_dye,
-    kept_act,
-    kept_gate,
-    kept_up,
-):
-    low = jnp.bfloat16
-    step = pl.program_id(0)
-    slots = kept_in.shape[1]
-    parts, _, ff_width = weights.shape
-    depth = normed.shape[1] // parts
-    down_depth = ff_width // parts
-
-    gate_w = weights[:, 0:depth, :].reshape(parts * depth, ff_width)
-    up_w = weights[:, depth : 2 * depth, :].reshape(parts * depth, ff_width)
-
-    def down_w(chunk):
-        at = 2 * depth + chunk * down_depth
-        return weights[:, at : at + down_depth, :].reshape(ff_width, ff_width)
-
-    chunks = normed.shape[1] // ff_width
-    tokens = normed[...]
-    cots = cot[...]
-    logits = jnp.where(
-        table[...] > 0, project(tokens, router[...]), -jnp.inf
-    )
-    top = jnp.max(logits, axis=1, keepdims=True)
-    raised = jnp.exp(logits - top)
-    gates = raised / jnp.sum(raised, axis=1, keepdims=True)
-    slot = lax.broadcasted_iota(jnp.int32, (slots, normed.shape[0]), 0)
-    picked = slot == rank[0, 0:1, :]
-    chosen = picked.astype(jnp.float32)
-    select = chosen.astype(low)
-    gate = jnp.sum(
-        jnp.dot(chosen, gates, precision=highest, preferred_element_type=jnp.float32) * mark[...],
-        axis=1,
-        keepdims=True,
-    )
-    expert_in = project(select, tokens).astype(low)
-    grad_mix = resid_scale * project(select, cots)
-    grad_out = (gate * grad_mix).astype(low)
-    gate_proj = project(expert_in, gate_w)
-    up_proj = project(expert_in, up_w)
-    sigmoid = 1.0 / (1.0 + jnp.exp(-gate_proj))
-    silu = gate_proj * sigmoid
-    act = (silu * up_proj).astype(low)
-    score = jnp.zeros((slots, 1), jnp.float32)
-    grad_act = jnp.zeros((slots, ff_width), jnp.float32)
-    for chunk in range(chunks):
-        lanes = slice(chunk * ff_width, (chunk + 1) * ff_width)
-        part = down_w(chunk)
-        out = project(act, part).astype(low).astype(jnp.float32)
-        score = score + jnp.sum(grad_mix[:, lanes] * out, axis=1, keepdims=True)
-        mix_out[:, lanes] = tn(select, (gate * out).astype(low)).astype(low)
-        grad_act = grad_act + nt(grad_out[:, lanes], part)
-    grad_gate = (grad_act * up_proj * (sigmoid + gate_proj * sigmoid * (1.0 - sigmoid))).astype(low)
-    grad_up = (grad_act * silu).astype(low)
-    grad_in = (nt(grad_gate, gate_w) + nt(grad_up, up_w)).astype(low)
-    rows_out[...] = tn(select, grad_in).astype(low)
-    score_row = jnp.sum(chosen * score, axis=0, keepdims=True)
-    score_out[0] = jnp.broadcast_to(score_row, score_out.shape[1:])
-    kept_in[step] = expert_in
-    kept_dye[step] = grad_out
-    kept_act[step] = act
-    kept_gate[step] = grad_gate
-    kept_up[step] = grad_up
-
-    @pl.when(step == pl.num_programs(0) - 1)
-    def _():
-        def all_of(kept):
-            return kept[...].reshape(kept.shape[0] * slots, kept.shape[2])
-
-        rows = all_of(kept_in)
-        for at, kept in ((0, kept_gate), (depth, kept_up)):
-            grad = tn(rows, all_of(kept)).astype(low)
-            grads_out[:, at : at + depth, :] = grad.reshape(parts, depth, ff_width)
-        act_all = all_of(kept_act)
-        for chunk in range(chunks):
-            lanes = slice(chunk * ff_width, (chunk + 1) * ff_width)
-            grad = tn(act_all, all_of(kept_dye.at[:, :, lanes])).astype(low)
-            at = 2 * depth + chunk * down_depth
-            grads_out[:, at : at + down_depth, :] = grad.reshape(parts, down_depth, ff_width)
-
-
-def expert_pass(normed, cot, table, rank, mark, router, weights, slots):
-    tiles, tile = rank.shape[0], rank.shape[2]
-    tokens, width = normed.shape
-    low = jnp.bfloat16
-    ff_width = weights.shape[2]
-    rows = pl.BlockSpec((tile, width), lambda i: (i, 0))
-    whole = lambda a: pl.BlockSpec(
-        a.shape, lambda i: (0,) * len(a.shape), pipeline_mode=pl.Buffered(1)
-    )
-    return pl.pallas_call(
-        expert_kernel,
-        grid=(tiles,),
-        out_shape=[
-            jax.ShapeDtypeStruct((tokens, width), low),
-            jax.ShapeDtypeStruct((tokens, width), low),
-            jax.ShapeDtypeStruct((tiles, 8, tile), jnp.float32),
-            jax.ShapeDtypeStruct(weights.shape, low),
-        ],
-        in_specs=[
-            rows,
-            rows,
-            pl.BlockSpec((tile, table.shape[1]), lambda i: (i, 0)),
-            pl.BlockSpec((1,) + rank.shape[1:], lambda i: (i, 0, 0)),
-            whole(mark),
-            whole(router),
-            whole(weights),
-        ],
-        out_specs=[
-            rows,
-            rows,
-            pl.BlockSpec((1, 8, tile), lambda i: (i, 0, 0)),
-            whole(weights),
-        ],
-        scratch_shapes=[
-            pltpu.VMEM((tiles, slots, width), low),
-            pltpu.VMEM((tiles, slots, width), low),
-            pltpu.VMEM((tiles, slots, ff_width), low),
-            pltpu.VMEM((tiles, slots, ff_width), low),
-            pltpu.VMEM((tiles, slots, ff_width), low),
-        ],
-        compiler_params=pltpu.CompilerParams(vmem_limit_bytes=56 * 2**20),
-        cost_estimate=pl.CostEstimate(
-            flops=22 * 10**9, bytes_accessed=50 * 10**6, transcendentals=10**6
-        ),
-        name="expert_pass",
-    )(normed, cot, table, rank, mark, router, weights)
-
-
 def owned(
     hidden_in,
     norm_gain,
@@ -1653,12 +1825,7 @@
         axis=2,
     ).transpose(1, 0, 2)
     qkv_width = q_width + 2 * HEAD_DIM
-    picks = jnp.pad(routes.reshape(own_rows, TOP).T, ((0, 0), (0, 128 - own_rows)))
-    weights = jnp.concatenate(
-        [w_gate, w_up]
-        + [w_down[:, :, at : at + ff_width] for at in range(0, model_width, ff_width)],
-        axis=1,
-    )
+    picks = jnp.pad(routes.reshape(own_rows, TOP).T, ((0, 0), (0, 128 - own_rows)), constant_values=-1)
     doc_id, position = documents(lengths[:, 0][micro_at], group_tokens)
     sin_table, cos_table = (
         table[:, 0] for table in angles(position.astype(jnp.float32), HEAD_DIM)
@@ -1667,81 +1834,54 @@
     doc_row = jnp.broadcast_to(doc_id[None, :], (8, group_tokens))
     cos_lanes = jnp.tile(cos_table, (1, 4))
     sin_lanes = jnp.tile(jnp.concatenate([-sin_table, sin_table], axis=1), (1, 2))
+    pad_experts = 128 - experts_all
+    table = jnp.any(
+        routes.reshape(own_rows, TOP)[:, :, None]
+        == jnp.arange(experts_all, dtype=jnp.int32)[None, None, :],
+        axis=1,
+    )
+    router_t = jnp.pad(w_router.T, ((0, pad_experts), (0, 0)))
+    cot_own = masked_cot.reshape(own_rows, model_width)
     (
         x_micro,
         w_mine,
-        w_out_all,
-        routes_all,
+        w_out_mine,
         cot_all,
         normed_all,
-        weights,
         qkv,
         attended,
         mixed,
+        gates_own,
+        rows_part,
+        mix_part,
+        scores,
+        grads,
+        grads_down,
     ) = front(
         0,
         hidden_in,
         w_qkv.reshape(kv_here, dp_count, width_part // dp_count, qkv_width),
         w_out.reshape(dp_count, w_out.shape[0] // dp_count, w_out.shape[1]),
         picks,
-        masked_cot.reshape(own_rows, model_width),
-        weights,
+        cot_own,
+        (w_gate, w_up, w_down),
         (norm_gain[None], mix_gain[None]),
         (cos_lanes, sin_lanes),
         (doc_col, doc_row),
+        (router_t, jnp.pad(table.astype(jnp.float32), ((0, 0), (0, pad_experts)))),
         q_width,
-    )
-    routes_all = (
-        routes_all[:, :, :own_rows].transpose(0, 2, 1).reshape(device_count * own_rows, TOP)
-    )
-    expert_ids = jnp.arange(experts_all, dtype=jnp.int32)
-
-    def gating(normed_rows, picks):
-        chosen = jnp.any(picks[:, :, None] == expert_ids[None, None, :], axis=1)
-        logits = jnp.where(chosen, project(normed_rows, w_router), -jnp.inf)
-        return jax.nn.softmax(logits, axis=-1)
-
-    normed_two = lax.dynamic_index_in_dim(normed_all, expert_at, 0, keepdims=False)
-    gates_own = gating(normed_two, routes.reshape(own_rows, TOP))
-
-    tile = col_count * own_rows
-    slots = col_count * micro_count * (quarter * 3 // 8)
-    table = jnp.any(routes_all[:, :, None] == expert_ids[None, None, :], axis=1)
-    here = jnp.any(routes_all == expert_at, axis=1).astype(jnp.int32).reshape(-1, tile)
-    rank = jnp.where(here > 0, jnp.cumsum(here, axis=1, dtype=jnp.int32) - 1, -1)
-    pad_experts = 128 - experts_all
-    mix_part, grad_rows_part, grad_gate_mine, grads = expert_pass(
-        normed_all.reshape(device_count * own_rows, model_width),
-        cot_all.reshape(device_count * own_rows, model_width),
-        jnp.pad(table.astype(jnp.float32), ((0, 0), (0, pad_experts))),
-        jnp.broadcast_to(rank[:, None, :], (rank.shape[0], 8, tile)),
-        (jnp.arange(128, dtype=jnp.int32) == expert_at).astype(jnp.float32)[None],
-        jnp.pad(w_router, ((0, 0), (0, pad_experts))),
-        weights,
-        slots,
-    )
-    grad_gate_mine = grad_gate_mine[:, 0, :].reshape(-1)
-    scores_send = jnp.broadcast_to(
-        jnp.pad(
-            grad_gate_mine.reshape(device_count, 1, own_rows),
-            ((0, 0), (0, 0), (0, 128 - own_rows)),
-        ),
-        (device_count, 8, 128),
-    )
-    w_out_mine = lax.dynamic_slice_in_dim(
-        w_out_all, (row_at * kv_here + half_at) * q_width, q_width
     )
     expert_mix, grads, qkv_sum, out_sum, router_grad, grad_input, lines = back(
         1,
-        grad_rows_part.reshape(device_count, own_rows, model_width),
-        mix_part.reshape(device_count, own_rows, model_width),
+        rows_part,
+        mix_part,
         grads,
-        scores_send,
+        scores,
         normed_all,
         mixed,
-        masked_cot.reshape(own_rows, model_width),
-        jnp.pad(gates_own, ((0, 0), (0, pad_experts))),
-        jnp.pad(w_router.T, ((0, pad_experts), (0, 0))),
+        cot_own,
+        gates_own,
+        router_t,
         norm_gain[None],
         mix_gain[None],
         x_micro,
@@ -1759,8 +1899,8 @@
     out_up = grads[:, slice_width : 2 * slice_width].astype(jnp.float32)
     out_down = jnp.concatenate(
         [
-            grads[:, at : at + down_slice]
-            for at in range(2 * slice_width, grads.shape[1], down_slice)
+            grads_down[:, at : at + down_slice]
+            for at in range(0, grads_down.shape[1], down_slice)
         ],
         axis=2,
     ).astype(jnp.float32)

time: 603 us -> 525 us (0.87)
  the two profiles are of different devices: /device:TPU:0 before, /device:TPU:9 now
where the time goes in v5:
time: 525 us; the launch traced here: 519 us
  Pallas kernels  483 us (92%)
  other arithmetic  17.8 us (3%)
  local copies, waits for them, and re-layouts  16.7 us (3%)
    pallas_call x1, Pallas kernels, front(): pl.pallas_call(front_kernel, out_shape=[shape((tokens, width), low), shap...  257 us
    pallas_call x1, Pallas kernels, back(): pl.pallas_call(back_kernel, out_shape=[shape(block, wide), shape(grads.sh...  226 us

profile of v5, /device:TPU:9, one launch (start us, length us, event | category | flops | bytes accessed | tf_op | source)
XLA Modules:
  0.0 518.8 jit_solution(15256574005227135041)
XLA Ops:
  0.7 0.7 convert_element_type.43
  1.4 0.7 fusion.2
  2.2 0.7 bitcast_subtract_fusion
  3.1 1.3 broadcast_in_dim.23.gain_one
  4.4 1.3 broadcast_in_dim.24.gain_two
  5.7 0.7 copy.49
  6.5 0.6 pad_bitcast_fusion.picks
  7.2 0.6 broadcast_in_dim.28.doc_row
  7.8 0.6 pad_convert_fusion.table
  8.5 1.0 copy.46
  9.5 1.0 copy.47
  10.5 0.4 fusion.1
  11.0 0.9 copy.52.sin_table
  11.9 1.8 broadcast_multiply_fusion
  13.9 1.1 copy.48
  15.0 0.9 broadcast_in_dim.27.doc_col
  15.9 0.8 pad.15.router_t
  16.7 0.9 copy.51.cos_table
  17.6 256.5 %front0.1 = (bf16[768,1536]{1,0:T(8,128)(2,1)}, bf16[4,2,192,320]{3,2,1,0:T(8,128)(2,1)}, bf16[192,1536]{1,0:T(8,128)(2,1)}, bf16[32,96,1536]{2,1,0:T(8,128)(2,1...) custom-call(bf16[2,192,384]{2,1,0:T(8,128)(2,1)} %x.7, ...), custom_call_target="tpu_custom_call" | custom-call | tf_op jit(solution)/shard_map/front0/pallas_call | solution.py:1119
  274.2 226.4 %back1.1 = (f32[96,1536]{1,0:T(8,128)}, bf16[16,192,512]{2,1,0:T(8,128)(2,1)}, bf16[2,2,320,384]{3,2,1,0:T(8,128)(2,1)}, bf16[2,2,192,384]{3,2,1,0:T(8,128)(2,1)...) custom-call(bf16[32,96,1536]{2,1,0:T(8,128)(2,1)} %get-tuple-element.33.partial, ...), custom_call_target="tpu_custom_call" | custom-call | tf_op jit(solution)/shard_map/back1/pallas_call | solution.py:1702
  500.6 2.0 add_convert_fusion
  502.6 1.0 reduce_sum.56
  503.6 1.7 reduce_sum.59
  505.3 0.6 slice_bitcast_fusion
  505.9 1.8 bitcast_convert_fusion
  507.8 0.9 convert_reduce_fusion.1
  508.9 1.1 copy.55
  509.9 0.8 copy.57
  510.7 0.8 copy.56
  511.7 2.1 maximum_convert_fusion
  513.8 0.9 copy-done
  514.8 3.6 slice_convert_fusion
  (30 shorter events, 1.3 us)
Async XLA Ops:
  0.6 13.0 %copy-start.5 = (bf16[384,384]{1,0:T(8,128)(2,1)S(1)}, bf16[384,384]{1,0:T(8,128)(2,1)}, u32[]{:S(2)}) copy-start(bf16[384,384]{1,0:T(8,128)(2,1)} %param.17) | copy-start | bytes 884740
  4.4 11.5 %copy-start.6 = (bf16[1536,32]{0,1:T(8,128)(2,1)S(1)}, bf16[1536,32]{0,1:T(8,128)(2,1)}, u32[]{:S(2)}) copy-start(bf16[1536,32]{0,1:T(8,128)(2,1)} %param.22) | copy-start | bytes 294916
  274.2 226.4 %copy-start.1 = (f32[96,1536]{1,0:T(8,128)S(1)}, f32[96,1536]{1,0:T(8,128)}, u32[]{:S(2)}) copy-start(f32[96,1536]{1,0:T(8,128)} %get-tuple-element.32.mixed) | copy-start | bytes 1769476
  500.6 7.2 %copy-start.4 = (bf16[2,2,192,384]{3,2,1,0:T(8,128)(2,1)S(1)}, bf16[2,2,192,384]{3,2,1,0:T(8,128)(2,1)}, u32[]{:S(2)}) copy-start(bf16[2,2,192,384]{3,2,1,0:T(8,128)(2,1)} %get-tuple-element.48) | copy-start | bytes 1769476
  500.6 8.1 %copy-start.3 = (bf16[2,2,320,384]{3,2,1,0:T(8,128)(2,1)S(1)}, bf16[2,2,320,384]{3,2,1,0:T(8,128)(2,1)}, u32[]{:S(2)}) copy-start(bf16[2,2,320,384]{3,2,1,0:T(8,128)(2,1)} %get-tuple-element.47) | copy-start | bytes 2949124
  508.7 2.9 copy-start.2
  511.7 3.0 copy-start

commit v6 on v5

--- a/solution.py
+++ b/solution.py
@@ -841,14 +841,14 @@
     stay = pltpu.make_async_copy(attended.at[me], att_own.at[me], att_send.at[0])
     stay.start()
     ship(1, 5)
-    for step in range(cols):
-        picks_line[1](step)
-        cot_line[1](step)
     for step in range(1, cols):
         part = out_at(row, step, other)
         arrival(part, o_sem.at[cols + step])
         pass_on(part, part, o_sem.at[3 * cols + step], {"row": across})
         pass_on(part, part, o_sem.at[5 * cols + step], {"row": beside})
+    for step in range(cols):
+        picks_line[1](step)
+        cot_line[1](step)
     for at in range(2):
         for step in range(cols):
             half = at if step == 0 else (dp if at == 0 else other)
@@ -1226,6 +1226,7 @@
     other = 1 - dp
     low = jnp.bfloat16
     two_on, beside_col, _ = col_peers()
+    order = (beside_col, (beside_col + 2) % cols, two_on, col)
     sent = []
 
     def pass_on(src, dst, sem, peer):
@@ -1245,62 +1246,74 @@
 
     def start():
         for turn in range(4):
-            for z in range(cols):
-                at = turn * cols + z
+            for at in range(cols):
+                slot = turn * cols + at
                 pass_on(
-                    partial.at[block_of(*theirs[turn], z)],
-                    near.at[at],
-                    beside_sem.at[at],
+                    partial.at[block_of(*theirs[turn], order[at])],
+                    near.at[slot],
+                    beside_sem.at[slot],
                     {"row": beside},
                 )
                 pltpu.make_async_copy(
-                    partial.at[block_of(*ours[turn], z)], mine.at[at], local_sem.at[at]
+                    partial.at[block_of(*ours[turn], order[at])], mine.at[slot], local_sem.at[slot]
                 ).start()
 
-    def chip_sum(at):
-        arrival(mine.at[at], local_sem.at[at])
-        arrival(near.at[at], beside_sem.at[at])
-        return mine[at].astype(jnp.float32) + near[at].astype(jnp.float32)
+    def combine(target, *parts):
+        rows_each = 16
+
+        @pl.loop(0, target.shape[0] // rows_each)
+        def _(at):
+            lines = pl.ds(pl.multiple_of(at * rows_each, rows_each), rows_each)
+            value = parts[0][lines, :].astype(jnp.float32)
+            for part in parts[1:]:
+                value = value + part[lines, :].astype(jnp.float32)
+            target[lines, :] = value.astype(target.dtype)
+
+    def chip(slot):
+        arrival(mine.at[slot], local_sem.at[slot])
+        arrival(near.at[slot], beside_sem.at[slot])
+        return mine.at[slot], near.at[slot]
 
     def diagonal():
-        for z in range(cols):
-            passed[z] = chip_sum(z).astype(low)
-            peer = {"dp": other} if z < 2 else {"row": across}
-            pass_on(passed.at[z], stage.at[z], first_sem.at[z], peer)
+        for at in range(cols):
+            combine(passed.at[at], *chip(at))
+            peer = {"dp": other} if at < 2 else {"row": across}
+            pass_on(passed.at[at], stage.at[at], first_sem.at[at], peer)
 
     def middle():
-        for z in range(cols):
-            for turn, here, peer in ((1, z >= 2, {"dp": other}), (2, z < 2, {"row": across})):
-                at = turn * cols + z
-                value = chip_sum(at)
+        for at in range(cols):
+            for turn, here, peer in ((1, at >= 2, {"dp": other}), (2, at < 2, {"row": across})):
+                slot = turn * cols + at
+                parts = chip(slot)
                 if here:
-                    arrival(stage.at[z], first_sem.at[z])
-                    value = value + stage[z].astype(jnp.float32)
-                passed[at] = value.astype(low)
-                pass_on(passed.at[at], stage.at[at], second_sem.at[at - cols], peer)
-
-    def chip_total(z):
-        value = chip_sum(3 * cols + z)
+                    arrival(stage.at[at], first_sem.at[at])
+                    parts = parts + (stage.at[at],)
+                combine(passed.at[slot], *parts)
+                pass_on(passed.at[slot], stage.at[slot], second_sem.at[slot - cols], peer)
+
+    def chip_total(at):
+        parts = chip(3 * cols + at)
         for turn in (1, 2):
-            arrival(stage.at[turn * cols + z], second_sem.at[(turn - 1) * cols + z])
-            value = value + stage[turn * cols + z].astype(jnp.float32)
-        return value
+            slot = turn * cols + at
+            arrival(stage.at[slot], second_sem.at[slot - cols])
+            parts = parts + (stage.at[slot],)
+        return parts
 
     def spread():
-        for at, z in enumerate((beside_col, (beside_col + 2) % cols)):
-            passed[3 * cols + at] = chip_total(z).astype(low)
+        for at in range(2):
+            combine(passed.at[3 * cols + at], *chip_total(at))
             pass_on(passed.at[3 * cols + at], last.at[at], col_sem.at[at], {"col": beside_col})
-        value = chip_total(two_on)
+        parts = chip_total(2)
         arrival(last.at[1], col_sem.at[1])
-        passed[3 * cols + 2] = (value + last[1].astype(jnp.float32)).astype(low)
+        combine(passed.at[3 * cols + 2], *parts, last.at[1])
         pass_on(passed.at[3 * cols + 2], last.at[2], col_sem.at[2], {"col": two_on})
 
-    def total():
-        value = chip_total(col)
-        for at, sem in ((0, 0), (2, 2)):
-            arrival(last.at[at], col_sem.at[sem])
-            value = value + last[at].astype(jnp.float32)
-        return value
+    def total(target):
+        parts = chip_total(3)
+        for at in (0, 2):
+            arrival(last.at[at], col_sem.at[at])
+            parts = parts + (last.at[at],)
+        combine(target, *parts)
 
     return start, diagonal, middle, spread, total
 
@@ -1355,6 +1368,7 @@
     do_in,
     x_send,
     lines,
+    rows_total,
     score_local,
     score_send,
     score_recv,
@@ -1420,7 +1434,7 @@
     mix_sum = sum_steps(
         mix_part, groups[0:3] + groups[11:12] + groups[4:5] + groups[12:18], copies
     )
-    lines_line = gather_line(lines, lines_all, groups[18:24], copies)
+    line_local, line_send, line_recv = groups[18:]
 
     score_own = pltpu.make_async_copy(scores.at[me], scores_in.at[me], score_local)
     score_own.start()
@@ -1463,7 +1477,8 @@
     value = mixed[...]
     scale_two = lax.rsqrt(jnp.mean(value * value, axis=1, keepdims=True) + eps_norm)
     unit_two = value * scale_two
-    grad_normed = rows_sum[4]() + routed
+    rows_sum[4](rows_total)
+    grad_normed = rows_total[...] + routed
     mix_row = jnp.sum(grad_normed * unit_two, axis=0, keepdims=True)
     grad_scaled = grad_normed * gain_two[...]
     grad_mixed = cot[...].astype(wide) + scale_two * (
@@ -1657,7 +1672,18 @@
         piece = slice(at * 128, (at + 1) * 128)
         lines[0, at : at + 1, :] = norm_row[:, piece]
         lines[0, steps + at : steps + at + 1, :] = mix_row[:, piece]
-    lines_line[0]()
+    home = pltpu.make_async_copy(lines.at[0], lines_all.at[me], line_local)
+    home.start()
+    for step in range(1, size):
+        swaps.append(
+            send(
+                lines.at[0],
+                lines_all.at[me],
+                line_send.at[step],
+                line_recv.at[step],
+                device_at(everyone, (me + step) % size),
+            )
+        )
     for copy in locals_[3:]:
         copy.wait()
     for step in range(1, cols):
@@ -1673,11 +1699,8 @@
         send(do_pair.at[dp], do_pair.at[dp], swap_sem.at[4], swap_sem.at[5], {"dp": other})
     )
     mix_sum[3]()
-    for at in range(1, 4):
-        for step in range(cols):
-            lines_line[at](step)
-    mix_out[...] = mix_sum[4]()
-    lines_line[4]()
+    mix_sum[4](mix_out)
+    home.wait()
     for copy in swaps:
         copy.wait()
     for copy in moved:
@@ -1735,6 +1758,7 @@
             pltpu.VMEM((cols, heads_width, part), low),
             pltpu.VMEM((cols, tokens // (2 * rows), part), low),
             pltpu.VMEM((1, lines, 128), wide),
+            pltpu.VMEM(block, wide),
             dma,
             dma((total,)),
             dma((total,)),
@@ -1763,7 +1787,7 @@
         + sum_scratch(block)
         + [pltpu.VMEM((3 * cols,) + block, low)]
         + sum_scratch(block)[5:]
-        + gather_sems(),
+        + [dma, dma((total,)), dma((total,))],
         compiler_params=pltpu.CompilerParams(
             collective_id=number, has_side_effects=True, vmem_limit_bytes=62 * 2**20
         ),

time: 525 us -> 496 us (0.945)
  the two profiles are of different devices: /device:TPU:9 before, /device:TPU:0 now
where the time goes in v6:
time: 496 us; the launch traced here: 488 us
  Pallas kernels  452 us (91%)
  other arithmetic  17.8 us (4%)
  local copies, waits for them, and re-layouts  16.7 us (3%)
    pallas_call x1, Pallas kernels, front(): pl.pallas_call(front_kernel, out_shape=[shape((tokens, width), low), shap...  237 us
    pallas_call x1, Pallas kernels, back(): pl.pallas_call(back_kernel, out_shape=[shape(block, wide), shape(grads.sh...  215 us

profile of v6, /device:TPU:0, one launch (start us, length us, event | category | flops | bytes accessed | tf_op | source)
XLA Modules:
  0.0 487.9 jit_solution(1336550077652328447)
XLA Ops:
  0.7 0.7 convert_element_type.43
  1.4 0.7 fusion.2
  2.2 0.7 bitcast_subtract_fusion
  3.1 1.3 broadcast_in_dim.23.gain_one
  4.4 1.3 broadcast_in_dim.24.gain_two
  5.7 0.7 copy.49
  6.5 0.6 pad_bitcast_fusion.picks
  7.2 0.6 broadcast_in_dim.28.doc_row
  7.8 0.6 pad_convert_fusion.table
  8.5 1.0 copy.46
  9.5 1.0 copy.47
  10.5 0.4 fusion.1
  11.0 0.9 copy.52.sin_table
  11.9 1.8 broadcast_multiply_fusion
  13.9 1.1 copy.48
  15.0 0.9 broadcast_in_dim.27.doc_col
  15.9 0.8 pad.15.router_t
  16.7 0.9 copy.51.cos_table
  17.6 237.3 %front0.1 = (bf16[768,1536]{1,0:T(8,128)(2,1)}, bf16[4,2,192,320]{3,2,1,0:T(8,128)(2,1)}, bf16[192,1536]{1,0:T(8,128)(2,1)}, bf16[32,96,1536]{2,1,0:T(8,128)(2,1...) custom-call(bf16[2,192,384]{2,1,0:T(8,128)(2,1)} %x.7, ...), custom_call_target="tpu_custom_call" | custom-call | tf_op jit(solution)/shard_map/front0/pallas_call | solution.py:1119
  254.9 215.0 %back1.1 = (f32[96,1536]{1,0:T(8,128)}, bf16[16,192,512]{2,1,0:T(8,128)(2,1)}, bf16[2,2,320,384]{3,2,1,0:T(8,128)(2,1)}, bf16[2,2,192,384]{3,2,1,0:T(8,128)(2,1)...) custom-call(bf16[32,96,1536]{2,1,0:T(8,128)(2,1)} %get-tuple-element.33.partial, ...), custom_call_target="tpu_custom_call" | custom-call | tf_op jit(solution)/shard_map/back1/pallas_call | solution.py:1725
  470.0 2.0 add_convert_fusion
  471.9 1.0 reduce_sum.56
  473.0 1.7 reduce_sum.59
  474.7 0.6 slice_bitcast_fusion
  475.3 1.8 bitcast_convert_fusion
  477.1 0.9 convert_reduce_fusion.1
  478.3 1.1 copy.55
  479.3 0.8 copy.57
  480.1 0.8 copy.56
  481.1 2.1 maximum_convert_fusion
  483.2 0.9 copy-done
  484.1 3.6 slice_convert_fusion
  (30 shorter events, 1.3 us)
Async XLA Ops:
  0.6 13.0 %copy-start.5 = (bf16[384,384]{1,0:T(8,128)(2,1)S(1)}, bf16[384,384]{1,0:T(8,128)(2,1)}, u32[]{:S(2)}) copy-start(bf16[384,384]{1,0:T(8,128)(2,1)} %param.17) | copy-start | bytes 884740
  4.4 11.5 %copy-start.6 = (bf16[1536,32]{0,1:T(8,128)(2,1)S(1)}, bf16[1536,32]{0,1:T(8,128)(2,1)}, u32[]{:S(2)}) copy-start(bf16[1536,32]{0,1:T(8,128)(2,1)} %param.22) | copy-start | bytes 294916
  254.9 215.1 %copy-start.1 = (f32[96,1536]{1,0:T(8,128)S(1)}, f32[96,1536]{1,0:T(8,128)}, u32[]{:S(2)}) copy-start(f32[96,1536]{1,0:T(8,128)} %get-tuple-element.32.mixed) | copy-start | bytes 1769476
  469.9 7.2 %copy-start.4 = (bf16[2,2,192,384]{3,2,1,0:T(8,128)(2,1)S(1)}, bf16[2,2,192,384]{3,2,1,0:T(8,128)(2,1)}, u32[]{:S(2)}) copy-start(bf16[2,2,192,384]{3,2,1,0:T(8,128)(2,1)} %get-tuple-element.48) | copy-start | bytes 1769476
  470.0 8.1 %copy-start.3 = (bf16[2,2,320,384]{3,2,1,0:T(8,128)(2,1)S(1)}, bf16[2,2,320,384]{3,2,1,0:T(8,128)(2,1)}, u32[]{:S(2)}) copy-start(bf16[2,2,320,384]{3,2,1,0:T(8,128)(2,1)} %get-tuple-element.47) | copy-start | bytes 2949124
  478.0 2.9 copy-start.2
  481.1 3.0 copy-start

commit v7 on v6

--- a/solution.py
+++ b/solution.py
@@ -1569,21 +1569,6 @@
         grad_qkv[:, piece] = turn(rotated[:, piece], cos_table[...], -sin_table[...]).astype(low)
     grad_qkv[:, 256:] = values_grad[...].astype(low)
 
-    rows_each = heads.shape[1]
-    projection = w_mine[...].reshape(model_width, w_mine.shape[3])
-    heads_sent = []
-
-    def heads_on(src, dst, sem, peer):
-        heads_sent.append(send(src, dst, heads_send.at[len(heads_sent)], sem, peer))
-
-    halves = (1 - half, half)
-    for at, row_to in enumerate((far, beside, across, row)):
-        for which, part in enumerate(halves):
-            slot = 2 * at + which
-            first = pl.multiple_of((row_to * 2 + part) * rows_each, rows_each)
-            heads[slot] = nt(grad_qkv[pl.ds(first, rows_each), :], projection).astype(low)
-            if at < 2:
-                heads_on(heads.at[slot], heads_near.at[slot], near_sem.at[slot], {"row": beside})
     width = model_width // cols
     heads_out = attended[...].reshape(tokens, kv_at)
     for step in range(cols - 1, -1, -1):
@@ -1608,6 +1593,21 @@
     keep(dw_send.at[col], dw_in.at[col])
     keep(do_send.at[col], do_in.at[col])
 
+    rows_each = heads.shape[1]
+    projection = w_mine[...].reshape(model_width, w_mine.shape[3])
+    heads_sent = []
+
+    def heads_on(src, dst, sem, peer):
+        heads_sent.append(send(src, dst, heads_send.at[len(heads_sent)], sem, peer))
+
+    halves = (1 - half, half)
+    for at, row_to in enumerate((far, beside, across, row)):
+        for which, part in enumerate(halves):
+            slot = 2 * at + which
+            first = pl.multiple_of((row_to * 2 + part) * rows_each, rows_each)
+            heads[slot] = nt(grad_qkv[pl.ds(first, rows_each), :], projection).astype(low)
+            if at < 2:
+                heads_on(heads.at[slot], heads_near.at[slot], near_sem.at[slot], {"row": beside})
     def heads_sum(slot):
         arrival(heads_near.at[slot - 4], near_sem.at[slot - 4])
         return heads[slot].astype(wide) + heads_near[slot - 4].astype(wide)

time: 496 us -> 492 us (level)
  no operation moved by 1% of the time
where the time goes in v7:
time: 492 us; the launch traced here: 485 us
  Pallas kernels  449 us (91%)
  other arithmetic  17.8 us (4%)
  local copies, waits for them, and re-layouts  16.7 us (3%)
    pallas_call x1, Pallas kernels, front(): pl.pallas_call(front_kernel, out_shape=[shape((tokens, width), low), shap...  237 us
    pallas_call x1, Pallas kernels, back(): pl.pallas_call(back_kernel, out_shape=[shape(block, wide), shape(grads.sh...  212 us

profile of v7, /device:TPU:0, one launch (start us, length us, event | category | flops | bytes accessed | tf_op | source)
XLA Modules:
  0.0 484.8 jit_solution(1260606453975412908)
XLA Ops:
  0.7 0.7 convert_element_type.43
  1.4 0.7 fusion.2
  2.2 0.7 bitcast_subtract_fusion
  3.1 1.3 broadcast_in_dim.23.gain_one
  4.4 1.3 broadcast_in_dim.24.gain_two
  5.7 0.7 copy.49
  6.5 0.6 pad_bitcast_fusion.picks
  7.2 0.6 broadcast_in_dim.28.doc_row
  7.8 0.6 pad_convert_fusion.table
  8.5 1.0 copy.46
  9.5 1.0 copy.47
  10.5 0.4 fusion.1
  11.0 0.9 copy.52.sin_table
  11.9 1.8 broadcast_multiply_fusion
  13.9 1.1 copy.48
  15.0 0.9 broadcast_in_dim.27.doc_col
  15.9 0.8 pad.15.router_t
  16.7 0.9 copy.51.cos_table
  17.6 237.0 %front0.1 = (bf16[768,1536]{1,0:T(8,128)(2,1)}, bf16[4,2,192,320]{3,2,1,0:T(8,128)(2,1)}, bf16[192,1536]{1,0:T(8,128)(2,1)}, bf16[32,96,1536]{2,1,0:T(8,128)(2,1...) custom-call(bf16[2,192,384]{2,1,0:T(8,128)(2,1)} %x.7, ...), custom_call_target="tpu_custom_call" | custom-call | tf_op jit(solution)/shard_map/front0/pallas_call | solution.py:1119
  254.7 212.0 %back1.1 = (f32[96,1536]{1,0:T(8,128)}, bf16[16,192,512]{2,1,0:T(8,128)(2,1)}, bf16[2,2,320,384]{3,2,1,0:T(8,128)(2,1)}, bf16[2,2,192,384]{3,2,1,0:T(8,128)(2,1)...) custom-call(bf16[32,96,1536]{2,1,0:T(8,128)(2,1)} %get-tuple-element.33.partial, ...), custom_call_target="tpu_custom_call" | custom-call | tf_op jit(solution)/shard_map/back1/pallas_call | solution.py:1725
  466.7 2.0 add_convert_fusion
  468.7 1.0 reduce_sum.56
  469.7 1.7 reduce_sum.59
  471.4 0.6 slice_bitcast_fusion
  472.0 1.8 bitcast_convert_fusion
  473.8 0.9 convert_reduce_fusion.1
  475.0 1.1 copy.55
  476.0 0.8 copy.57
  476.8 0.8 copy.56
  477.8 2.1 maximum_convert_fusion
  479.9 0.9 copy-done
  480.9 3.6 slice_convert_fusion
  (30 shorter events, 1.3 us)
Async XLA Ops:
  0.6 13.0 %copy-start.5 = (bf16[384,384]{1,0:T(8,128)(2,1)S(1)}, bf16[384,384]{1,0:T(8,128)(2,1)}, u32[]{:S(2)}) copy-start(bf16[384,384]{1,0:T(8,128)(2,1)} %param.17) | copy-start | bytes 884740
  4.4 11.5 %copy-start.6 = (bf16[1536,32]{0,1:T(8,128)(2,1)S(1)}, bf16[1536,32]{0,1:T(8,128)(2,1)}, u32[]{:S(2)}) copy-start(bf16[1536,32]{0,1:T(8,128)(2,1)} %param.22) | copy-start | bytes 294916
  254.7 212.0 %copy-start.1 = (f32[96,1536]{1,0:T(8,128)S(1)}, f32[96,1536]{1,0:T(8,128)}, u32[]{:S(2)}) copy-start(f32[96,1536]{1,0:T(8,128)} %get-tuple-element.32.mixed) | copy-start | bytes 1769476
  466.7 7.2 %copy-start.4 = (bf16[2,2,192,384]{3,2,1,0:T(8,128)(2,1)S(1)}, bf16[2,2,192,384]{3,2,1,0:T(8,128)(2,1)}, u32[]{:S(2)}) copy-start(bf16[2,2,192,384]{3,2,1,0:T(8,128)(2,1)} %get-tuple-element.48) | copy-start | bytes 1769476
  466.7 8.1 %copy-start.3 = (bf16[2,2,320,384]{3,2,1,0:T(8,128)(2,1)S(1)}, bf16[2,2,320,384]{3,2,1,0:T(8,128)(2,1)}, u32[]{:S(2)}) copy-start(bf16[2,2,320,384]{3,2,1,0:T(8,128)(2,1)} %get-tuple-element.47) | copy-start | bytes 2949124
  474.7 2.9 copy-start.2
  477.8 3.0 copy-start

commit v8 on v7

--- a/solution.py
+++ b/solution.py
@@ -840,7 +840,6 @@
         )
     stay = pltpu.make_async_copy(attended.at[me], att_own.at[me], att_send.at[0])
     stay.start()
-    ship(1, 5)
     for step in range(1, cols):
         part = out_at(row, step, other)
         arrival(part, o_sem.at[cols + step])
@@ -849,6 +848,7 @@
     for step in range(cols):
         picks_line[1](step)
         cot_line[1](step)
+    ship(1, 5)
     for at in range(2):
         for step in range(cols):
             half = at if step == 0 else (dp if at == 0 else other)

time: 492 us -> 488 us (level)
  no operation moved by 1% of the time
where the time goes in v8:
time: 488 us; the launch traced here: 480 us
  Pallas kernels  445 us (91%)
  other arithmetic  17.8 us (4%)
  local copies, waits for them, and re-layouts  16.7 us (3%)
    pallas_call x1, Pallas kernels, front(): pl.pallas_call(front_kernel, out_shape=[shape((tokens, width), low), shap...  236 us
    pallas_call x1, Pallas kernels, back(): pl.pallas_call(back_kernel, out_shape=[shape(block, wide), shape(grads.sh...  208 us

profile of v8, /device:TPU:0, one launch (start us, length us, event | category | flops | bytes accessed | tf_op | source)
XLA Modules:
  0.0 480.4 jit_solution(3622367900603833428)
XLA Ops:
  0.7 0.7 convert_element_type.43
  1.4 0.7 fusion.2
  2.2 0.7 bitcast_subtract_fusion
  3.1 1.3 broadcast_in_dim.23.gain_one
  4.4 1.3 broadcast_in_dim.24.gain_two
  5.7 0.7 copy.49
  6.5 0.6 pad_bitcast_fusion.picks
  7.2 0.6 broadcast_in_dim.28.doc_row
  7.8 0.6 pad_convert_fusion.table
  8.5 1.0 copy.46
  9.5 1.0 copy.47
  10.5 0.4 fusion.1
  11.0 0.9 copy.52.sin_table
  11.9 1.8 broadcast_multiply_fusion
  13.9 1.1 copy.48
  15.0 0.9 broadcast_in_dim.27.doc_col
  15.9 0.8 pad.15.router_t
  16.7 0.9 copy.51.cos_table
  17.6 236.3 %front0.1 = (bf16[768,1536]{1,0:T(8,128)(2,1)}, bf16[4,2,192,320]{3,2,1,0:T(8,128)(2,1)}, bf16[192,1536]{1,0:T(8,128)(2,1)}, bf16[32,96,1536]{2,1,0:T(8,128)(2,1...) custom-call(bf16[2,192,384]{2,1,0:T(8,128)(2,1)} %x.7, ...), custom_call_target="tpu_custom_call" | custom-call | tf_op jit(solution)/shard_map/front0/pallas_call | solution.py:1119
  254.0 208.3 %back1.1 = (f32[96,1536]{1,0:T(8,128)}, bf16[16,192,512]{2,1,0:T(8,128)(2,1)}, bf16[2,2,320,384]{3,2,1,0:T(8,128)(2,1)}, bf16[2,2,192,384]{3,2,1,0:T(8,128)(2,1)...) custom-call(bf16[32,96,1536]{2,1,0:T(8,128)(2,1)} %get-tuple-element.33.partial, ...), custom_call_target="tpu_custom_call" | custom-call | tf_op jit(solution)/shard_map/back1/pallas_call | solution.py:1725
  462.3 2.0 add_convert_fusion
  464.2 1.0 reduce_sum.56
  465.3 1.7 reduce_sum.59
  467.0 0.6 slice_bitcast_fusion
  467.6 1.8 bitcast_convert_fusion
  469.4 0.9 convert_reduce_fusion.1
  470.6 1.1 copy.55
  471.6 0.8 copy.57
  472.4 0.8 copy.56
  473.4 2.1 maximum_convert_fusion
  475.5 0.9 copy-done
  476.4 3.6 slice_convert_fusion
  (30 shorter events, 1.3 us)
Async XLA Ops:
  0.6 13.0 %copy-start.5 = (bf16[384,384]{1,0:T(8,128)(2,1)S(1)}, bf16[384,384]{1,0:T(8,128)(2,1)}, u32[]{:S(2)}) copy-start(bf16[384,384]{1,0:T(8,128)(2,1)} %param.17) | copy-start | bytes 884740
  4.4 11.5 %copy-start.6 = (bf16[1536,32]{0,1:T(8,128)(2,1)S(1)}, bf16[1536,32]{0,1:T(8,128)(2,1)}, u32[]{:S(2)}) copy-start(bf16[1536,32]{0,1:T(8,128)(2,1)} %param.22) | copy-start | bytes 294916
  253.9 208.3 %copy-start.1 = (f32[96,1536]{1,0:T(8,128)S(1)}, f32[96,1536]{1,0:T(8,128)}, u32[]{:S(2)}) copy-start(f32[96,1536]{1,0:T(8,128)} %get-tuple-element.32.mixed) | copy-start | bytes 1769476
  462.3 7.2 %copy-start.4 = (bf16[2,2,192,384]{3,2,1,0:T(8,128)(2,1)S(1)}, bf16[2,2,192,384]{3,2,1,0:T(8,128)(2,1)}, u32[]{:S(2)}) copy-start(bf16[2,2,192,384]{3,2,1,0:T(8,128)(2,1)} %get-tuple-element.48) | copy-start | bytes 1769476
  462.3 8.1 %copy-start.3 = (bf16[2,2,320,384]{3,2,1,0:T(8,128)(2,1)S(1)}, bf16[2,2,320,384]{3,2,1,0:T(8,128)(2,1)}, u32[]{:S(2)}) copy-start(bf16[2,2,320,384]{3,2,1,0:T(8,128)(2,1)} %get-tuple-element.47) | copy-start | bytes 2949124
  470.3 2.9 copy-start.2
  473.4 3.0 copy-start
